TPU v7x, 512 devices: a whole 4x8x8 slice. The times are simulated.
512 devices in a mesh: row: 32 (over y, x_hi, core), col: 16 (over z, x_lo).
Axes of the slice: x: 4 (x_hi: 2, x_lo: 2; x = x_hi * 2 + x_lo), y: 8, z: 8, core: 2. Of those that a mesh axis runs over, the one named last changes fastest.
Arguments:
- features: bfloat16 [65536, 512], P(('col', 'row')), may hold values from -6 to 6
- block_values: bfloat16 [32, 16, 12, 128, 128], P('row', 'col'), may hold values from -0.21875 to 0.21875
- block_rows: int32 [32, 16, 12], P('row', 'col'), may hold values from 0 to 15
- block_cols: int32 [32, 16, 12], P('row', 'col'), may hold values from 0 to 31
- block_count: int32 [32, 16], P('row', 'col'), may hold values from 3 to 12, as said below
- weight: bfloat16 [512, 512], replicated, may hold values from -0.25 to 0.25
- bias: float32 [512], replicated, may hold values from -3 to 3
- cotangent: bfloat16 [65536, 512], P(('row', 'col')), may hold values from -6 to 6
Outputs:
- hidden: bfloat16 [65536, 512], P(('row', 'col'))
- weight_grad: float32 [512, 512], replicated
- bias_grad: float32 [512], replicated
- feature_grad: bfloat16 [65536, 512], P(('col', 'row'))
Inputs may be any that keep to these rules, and one draw needn't show every extreme that they name: `block_count`: no grid tile has more than 12 live slots, and some tile has exactly 12.
All inputs are finite; a program needn't handle non-finite values.
Results may differ from a plain program's by a relative error of at most 0.017.
Values may be sent and summed in bfloat16 or wider, within the bound.
A program may use at most 64 MiB of HBM per device.

v0:
```python
import jax
import jax.numpy as jnp
from jax import lax
from jax.sharding import PartitionSpec as P


def slot_product(tile_values, tile_rows, tile_cols, live_count, source, out_len, backward):
    capacity = tile_values.shape[0]
    block_size = tile_values.shape[1]
    width = source.shape[1]
    group = max([d for d in range(1, min(capacity, 16) + 1) if capacity % d == 0])
    groups = capacity // group
    panels = source.reshape(source.shape[0] // block_size, block_size, width)
    out_blocks = out_len // block_size
    if backward:
        source_ids = tile_rows
        target_ids = tile_cols
        form = "sba,sbf->saf"
    else:
        source_ids = tile_cols
        target_ids = tile_rows
        form = "sab,sbf->saf"
    alive = jnp.arange(capacity, dtype=jnp.int32) < live_count
    places = jnp.arange(out_blocks, dtype=jnp.int32)

    def one_group(total, items):
        values_part, source_part, target_part, alive_part = items
        segments = jnp.take(panels, source_part, axis=0)
        products = jnp.einsum(form, values_part, segments, preferred_element_type=jnp.float32)
        selector = ((target_part[None, :] == places[:, None]) & alive_part[None, :]).astype(
            jnp.float32
        )
        added = jnp.einsum("rs,saf->raf", selector, products, precision=lax.Precision.HIGHEST)
        return (total + added, None)

    items = (
        tile_values.reshape(groups, group, block_size, block_size),
        source_ids.reshape(groups, group),
        target_ids.reshape(groups, group),
        alive.reshape(groups, group),
    )
    start = jnp.zeros((out_blocks, block_size, width), jnp.float32)
    total, _ = lax.scan(one_group, start, items)
    return total.reshape(out_len, width)


def global_grads(local_weight, local_bias):
    return lax.psum((local_weight, local_bias), ("row", "col"))


def transposed_product(left, weight):
    return lax.dot_general(
        left, weight, (((1,), (1,)), ((), ())), preferred_element_type=jnp.float32
    ).astype(jnp.bfloat16)


def source_total(received):
    return jnp.sum(received.astype(jnp.float32), axis=0).astype(jnp.bfloat16)


def per_device(
    features, block_values, block_rows, block_cols, block_count, weight, bias, cotangent
):
    tile_values = block_values[0, 0]
    tile_rows = block_rows[0, 0]
    tile_cols = block_cols[0, 0]
    live_count = block_count[0, 0]
    own_nodes = features.shape[0]
    width = features.shape[1]
    row_len = lax.axis_size("col") * own_nodes
    gathered = lax.all_gather(features, "row", axis=0, tiled=True)
    col_len = gathered.shape[0]
    partial_value = slot_product(
        tile_values, tile_rows, tile_cols, live_count, gathered, row_len, False
    )
    aggregate = lax.psum_scatter(
        partial_value.astype(jnp.bfloat16), "col", scatter_dimension=0, tiled=True
    )
    preact = jnp.dot(aggregate, weight, preferred_element_type=jnp.float32) + bias
    hidden = jax.nn.silu(preact).astype(jnp.bfloat16)
    sigma = jax.nn.sigmoid(preact)
    grad_pre = cotangent.astype(jnp.float32) * sigma * (1.0 + preact * (1.0 - sigma))
    grad_low = grad_pre.astype(jnp.bfloat16)
    local_weight = lax.dot_general(
        aggregate, grad_low, (((0,), (0,)), ((), ())), preferred_element_type=jnp.float32
    )
    local_bias = jnp.sum(grad_pre, axis=0)
    grad_agg = transposed_product(grad_low, weight)
    grad_panel = lax.all_gather(grad_agg, "col", axis=0, tiled=True)
    back = slot_product(tile_values, tile_rows, tile_cols, live_count, grad_panel, col_len, True)
    back_low = back.astype(jnp.bfloat16).reshape(col_len // own_nodes, own_nodes, width)
    received = lax.all_to_all(back_low, "row", split_axis=0, concat_axis=0, tiled=True)
    feature_grad = source_total(received)
    weight_grad, bias_grad = global_grads(local_weight, local_bias)
    return (hidden, weight_grad, bias_grad, feature_grad)


def solution(mesh):
    in_specs = (
        P(("col", "row"), None),
        P("row", "col", None, None, None),
        P("row", "col", None),
        P("row", "col", None),
        P("row", "col"),
        P(),
        P(),
        P(("row", "col"), None),
    )
    out_specs = (P(("row", "col"), None), P(), P(), P(("col", "row"), None))
    return jax.shard_map(
        per_device, mesh=mesh, in_specs=in_specs, out_specs=out_specs, check_vma=False
    )
```

profile of v0, /device:TPU:7, one launch (start us, length us, event | category | flops | bytes accessed | tf_op | source)
XLA Modules:
  0.0 615.2 jit_solution(6726816917784381716)
XLA Ops:
  7.2 0.0 copy-start
  7.2 0.0 copy-start.1
  7.2 0.0 all-gather.3.cloned.1.call-start
  7.2 0.7 all-gather.3.cloned.1.call-update
  7.9 0.0 reduce-scatter.2.cloned.1.call-start
  8.6 0.7 fusion.21
  9.3 0.7 compare_and_fusion.1
  10.0 96.8 %all-gather.3.cloned.1.call-done = bf16[4096,512]{1,0:T(8,128)(2,1)} async-done(((bf16[128,512]{1,0:T(8,128)(2,1)}), bf16[4096,512]{1,0:T(8,128)(2,1)}) %all-gather.3.cloned.1.call-update) | async-done | bytes 4194320 | tf_op jit(solution)/shard_map/all_gather | solution.py:71
  106.7 2.8 gather_fusion
  109.6 0.0 copy-done.1
  109.6 2.4 convolution_bitcast_fusion.1
  112.0 0.0 copy-start.4
  112.0 5.2 copy.18
  117.2 0.0 copy-done.4
  117.2 4.3 convolution_convert_fusion.1
  121.6 2.5 copy.19
  124.1 0.0 copy-start.5
  124.1 0.0 copy-start.6
  124.1 0.0 reduce-scatter.2.cloned.1.call-update
  124.1 0.0 all-gather.5.cloned.1.call-start
  124.1 65.1 %reduce-scatter.2.cloned.1.call-done = bf16[128,512]{1,0:T(8,128)(2,1)} async-done(((bf16[2048,512]{1,0:T(8,128)(2,1)}), bf16[128,512]{1,0:T(8,128)(2,1)}) %reduce-scatter.2.cloned.1.call-update) | async-done | bytes 131088 | tf_op jit(solution)/shard_map/reduce_scatter | solution.py:76
  189.2 0.0 copy-done
  189.2 0.0 copy-done.5
  189.2 0.0 copy-done.6
  189.2 1.9 fusion.25
  191.1 1.0 convolution_convert_fusion.2
  192.1 0.0 all-gather.5.cloned.1.call-update
  192.1 76.8 %all-gather.5.cloned.1.call-done = bf16[2048,512]{1,0:T(8,128)(2,1)} async-done(((bf16[128,512]{1,0:T(8,128)(2,1)}), bf16[2048,512]{1,0:T(8,128)(2,1)}) %all-gather.5.cloned.1.call-update) | async-done | bytes 2097168 | tf_op jit(solution)/shard_map/all_gather | solution.py:89
  268.9 2.2 gather_fusion.1
  271.2 2.4 convolution_bitcast_fusion
  273.6 0.0 copy-start.3
  273.6 5.2 copy.21
  278.8 0.0 copy-done.3
  278.8 5.5 convolution_convert_fusion
  284.3 4.4 copy.22
  288.7 0.0 copy-start.2
  288.7 19.3 %all-to-all-start = ((bf16[32,128,512]{2,1,0:T(8,128)(2,1)}), bf16[32,128,512]{2,1,0:T(8,128)(2,1)}, u32[]{:S(2)}, u32[]{:S(2)}) async-start(bf16[32,128,512]{2,1,0:T(8,128)(2,1)} %copy.22), calls=%async_computation.1 | async-start | bytes 8388608 | tf_op jit(solution)/shard_map/all_to_all | solution.py:92
  308.0 0.0 all-reduce.2.cloned.1.call-start
  308.1 0.0 copy-done.2
  308.1 1.3 fusion.9
  309.4 0.0 all-reduce.2.cloned.1.call-update
  309.4 182.3 %psum.15 = f32[512]{0:T(512)} all-reduce(f32[512]{0:T(512)S(1)} %get-tuple-element.36), channel_id=1, replica_groups=mesh['row'=32,'col'=16] {'row','col'}, use_global_device_ids=true, to_apply=%region_3.4 | all-reduce | flops 512 | bytes 4096 | tf_op jit(solution)/shard_map/psum | solution.py:48
  491.7 0.0 all-to-all-done
  491.7 3.5 reduce_sum.22
  495.2 111.3 %all-reduce.2.cloned.1.call-done = f32[512,512]{1,0:T(8,128)} async-done(((f32[512,512]{1,0:T(8,128)}), f32[512,512]{1,0:T(8,128)}) %all-reduce.2.cloned.1.call-update) | async-done | bytes 1048592 | tf_op jit(solution)/shard_map/psum | solution.py:48
  606.5 2.3 copy.27
  (5 shorter events, 0.0 us)
Async XLA Ops:
  7.2 182.0 %copy-start = (bf16[512,512]{1,0:T(8,128)(2,1)S(1)}, bf16[512,512]{1,0:T(8,128)(2,1)}, u32[]{:S(2)}) copy-start(bf16[512,512]{1,0:T(8,128)(2,1)} %param.13) | copy-start | bytes 1572868
  7.2 102.4 %copy-start.1 = (bf16[1,1,12,128,128]{4,3,2,1,0:T(8,128)(2,1)S(1)}, bf16[1,1,12,128,128]{4,3,2,1,0:T(8,128)(2,1)}, u32[]{:S(2)}) copy-start(bf16[1,1,12,128,128]{4,3,2,1,0:T(8,128)(2,1)} %param.9) | copy-start | bytes 1179652
  7.2 99.5 %all-gather.3.cloned.1.call-start = ((), (), s32[]{:S(2)}) async-start(), calls=%async_computation.2 | async-start | bytes 4325376 | tf_op jit(solution)/shard_map/all_gather | solution.py:71
  7.9 181.3 %reduce-scatter.2.cloned.1.call-start = ((), (), s32[]{:S(2)}) async-start(), calls=%async_computation.3 | async-start | bytes 2228224 | tf_op jit(solution)/shard_map/reduce_scatter | solution.py:76
  112.0 5.3 copy-start.4
  124.1 65.1 %copy-start.5 = (bf16[128,512]{1,0:T(8,128)(2,1)S(1)}, bf16[128,512]{1,0:T(8,128)(2,1)}, u32[]{:S(2)}) copy-start(bf16[128,512]{1,0:T(8,128)(2,1)} %param.15) | copy-start | bytes 393220
  124.1 65.1 %copy-start.6 = (f32[512]{0:T(512)S(1)}, f32[512]{0:T(512)}, u32[]{:S(2)}) copy-start(f32[512]{0:T(512)} %param.14) | copy-start | bytes 6148
  124.1 144.9 %all-gather.5.cloned.1.call-start = ((), (), s32[]{:S(2)}) async-start(), calls=%async_computation.5 | async-start | bytes 2228224 | tf_op jit(solution)/shard_map/all_gather | solution.py:89
  273.6 5.3 copy-start.3
  288.7 19.3 %copy-start.2 = (bf16[128,512]{1,0:T(8,128)(2,1)S(1)}, bf16[128,512]{1,0:T(8,128)(2,1)}, u32[]{:S(2)}) copy-start(bf16[128,512]{1,0:T(8,128)(2,1)} %reduce-scatter.2.cloned.1.call-done) | copy-start | bytes 393220
  288.7 203.0 %all-to-all-start = ((bf16[32,128,512]{2,1,0:T(8,128)(2,1)}), bf16[32,128,512]{2,1,0:T(8,128)(2,1)}, u32[]{:S(2)}, u32[]{:S(2)}) async-start(bf16[32,128,512]{2,1,0:T(8,128)(2,1)} %copy.22), calls=%async_computation.1 | async-start | bytes 8388608 | tf_op jit(solution)/shard_map/all_to_all | solution.py:92
  308.0 298.4 %all-reduce.2.cloned.1.call-start = ((), (), s32[]{:S(2)}) async-start(), calls=%async_computation.4 | async-start | bytes 2097152 | tf_op jit(solution)/shard_map/psum | solution.py:48
Sparse Core Ops, SparseCore 0:
  11.4 95.2 all-gather.2
  124.2 64.9 reduce-scatter.1
  192.2 76.6 all-gather.4
  314.2 292.2 all-reduce.1
where the time goes:
time: 617 us; the launch traced here: 615 us
  waiting for transfers between devices  351 us (57%)
  blocking collectives  182 us (29%)
  local copies, waits for them, and re-layouts  24.8 us (4%)
  starting transfers between devices  19.4 us (3%)
  matrix products  18.8 us (3%)
  between operations  14.5 us (2%)
    psum x1, blocking collectives, global_grads(): return lax.psum((local_weight, local_bias), ('row', 'col'))  182 us
    psum x1, waiting for transfers between devices, global_grads(): return lax.psum((local_weight, local_bias), ('row', 'col'))  111 us
    all_gather x1, waiting for transfers between devices, per_device(): gathered = lax.all_gather(features, 'row', axis=0, tiled=True)  96.8 us
    all_gather x1, waiting for transfers between devices, per_device(): grad_panel = lax.all_gather(grad_agg, 'col', axis=0, tiled=True)  76.8 us
    reduce_scatter x1, waiting for transfers between devices, per_device(): lax.psum_scatter(partial_value.astype(jnp.bfloat16), 'col', scatter_dimen...  65.1 us
    all_to_all x1, starting transfers between devices, per_device(): lax.all_to_all(back_low, 'row', split_axis=0, concat_axis=0, tiled=True)  19.3 us
  transfers between devices with their start and end apart: 5, of which 4 were waited for; matrix products, arithmetic and copies ran while one was open for 1% of the time, Pallas kernels for 0%

commit v1 on v0

--- a/solution.py
+++ b/solution.py
@@ -44,8 +44,28 @@
     return total.reshape(out_len, width)
 
 
+def gather_rows(x, axis):
+    count = lax.axis_size(axis)
+    stacked = jnp.broadcast_to(x[None], (count,) + x.shape)
+    received = lax.all_to_all(stacked, axis, split_axis=0, concat_axis=0, tiled=True)
+    return received.reshape((count * x.shape[0],) + x.shape[1:])
+
+
+def scatter_sum(x, axis):
+    count = lax.axis_size(axis)
+    pieces = x.reshape((count, x.shape[0] // count) + x.shape[1:])
+    received = lax.all_to_all(pieces, axis, split_axis=0, concat_axis=0, tiled=True)
+    return jnp.sum(received.astype(jnp.float32), axis=0)
+
+
 def global_grads(local_weight, local_bias):
-    return lax.psum((local_weight, local_bias), ("row", "col"))
+    width = local_weight.shape[1]
+    pad = jnp.zeros((local_weight.shape[0], 127), jnp.float32)
+    packed = jnp.concatenate([local_weight, local_bias[:, None], pad], axis=1)
+    by_col = scatter_sum(packed, "col")
+    total = scatter_sum(by_col, "row")
+    whole = gather_rows(gather_rows(total, "row"), "col")
+    return whole[:, :width], whole[:, width]
 
 
 def transposed_product(left, weight):
@@ -68,14 +88,12 @@
     own_nodes = features.shape[0]
     width = features.shape[1]
     row_len = lax.axis_size("col") * own_nodes
-    gathered = lax.all_gather(features, "row", axis=0, tiled=True)
+    gathered = gather_rows(features, "row")
     col_len = gathered.shape[0]
     partial_value = slot_product(
         tile_values, tile_rows, tile_cols, live_count, gathered, row_len, False
     )
-    aggregate = lax.psum_scatter(
-        partial_value.astype(jnp.bfloat16), "col", scatter_dimension=0, tiled=True
-    )
+    aggregate = scatter_sum(partial_value.astype(jnp.bfloat16), "col").astype(jnp.bfloat16)
     preact = jnp.dot(aggregate, weight, preferred_element_type=jnp.float32) + bias
     hidden = jax.nn.silu(preact).astype(jnp.bfloat16)
     sigma = jax.nn.sigmoid(preact)
@@ -86,7 +104,7 @@
     )
     local_bias = jnp.sum(grad_pre, axis=0)
     grad_agg = transposed_product(grad_low, weight)
-    grad_panel = lax.all_gather(grad_agg, "col", axis=0, tiled=True)
+    grad_panel = gather_rows(grad_agg, "col")
     back = slot_product(tile_values, tile_rows, tile_cols, live_count, grad_panel, col_len, True)
     back_low = back.astype(jnp.bfloat16).reshape(col_len // own_nodes, own_nodes, width)
     received = lax.all_to_all(back_low, "row", split_axis=0, concat_axis=0, tiled=True)

time: 617 us -> 461 us (0.75)
  blocking collectives: 182 us -> 55.2 us
  waiting for transfers between devices: 351 us -> 293 us
  starting transfers between devices: 19.4 us -> 53.3 us
  between operations: 14.5 us -> 1.56 us
  local copies, waits for them, and re-layouts: 24.8 us -> 33.3 us
    all_to_all x0 -> x5, waiting for transfers between devices: none -> 203 us  [the longest x4 156 us: gather_rows(): lax.all_to_all(stacked, axis, split_axis=0, concat_axis=0, tiled=True)]
    psum x1 -> x0, blocking collectives: 182 us -> none  [global_grads(): return lax.psum((local_weight, local_bias), ('row', 'col'))]
    all_gather x2 -> x0, waiting for transfers between devices: 174 us -> none  [the longest x1 96.8 us: per_device(): gathered = lax.all_gather(features, 'row', axis=0, tiled=True)]
    psum x1 -> x0, waiting for transfers between devices: 111 us -> none  [global_grads(): return lax.psum((local_weight, local_bias), ('row', 'col'))]
    all_to_all x1, waiting for transfers between devices: 0.01 us -> 90.1 us  [per_device(): lax.all_to_all(back_low, 'row', split_axis=0, concat_axis=0, tiled=True)]
    reduce_scatter x1 -> x0, waiting for transfers between devices: 65.1 us -> none  [per_device(): lax.psum_scatter(partial_value.astype(jnp.bfloat16), 'col', scatter_dimen...]
    all_to_all x0 -> x2, blocking collectives: none -> 55.2 us  [scatter_sum(): lax.all_to_all(pieces, axis, split_axis=0, concat_axis=0, tiled=True)]
    all_to_all x0 -> x5, starting transfers between devices: none -> 39.9 us  [the longest x4 28.7 us: gather_rows(): lax.all_to_all(stacked, axis, split_axis=0, concat_axis=0, tiled=True)]
  transfers between devices with their start and end apart: 5 -> 6, of which waited for: 4 -> 6; matrix products, arithmetic and copies ran while one was open for 1% -> 5% of each run, Pallas kernels for 0% -> 0%
where the time goes in v1:
time: 461 us; the launch traced here: 458 us
  waiting for transfers between devices  293 us (64%)
  blocking collectives  55.2 us (12%)
  starting transfers between devices  53.3 us (12%)
  local copies, waits for them, and re-layouts  33.3 us (7%)
  matrix products  17.6 us (4%)
    all_to_all x4, waiting for transfers between devices, gather_rows(): lax.all_to_all(stacked, axis, split_axis=0, concat_axis=0, tiled=True)  156 us
    all_to_all x1, waiting for transfers between devices, per_device(): lax.all_to_all(back_low, 'row', split_axis=0, concat_axis=0, tiled=True)  90.1 us
    all_to_all x2, blocking collectives, scatter_sum(): lax.all_to_all(pieces, axis, split_axis=0, concat_axis=0, tiled=True)  55.2 us
    all_to_all x1, waiting for transfers between devices, scatter_sum(): lax.all_to_all(pieces, axis, split_axis=0, concat_axis=0, tiled=True)  47.4 us
    all_to_all x4, starting transfers between devices, gather_rows(): lax.all_to_all(stacked, axis, split_axis=0, concat_axis=0, tiled=True)  28.7 us
    all_to_all x1, starting transfers between devices, per_device(): lax.all_to_all(back_low, 'row', split_axis=0, concat_axis=0, tiled=True)  13.4 us
    all_to_all x1, starting transfers between devices, scatter_sum(): lax.all_to_all(pieces, axis, split_axis=0, concat_axis=0, tiled=True)  11.2 us
    dot_general x2, local copies, waits for them, and re-layouts, one_group(): jnp.einsum(form, values_part, segments, preferred_element_type=jnp.float32)  10.4 us
  transfers between devices with their start and end apart: 6, of which 6 were waited for; matrix products, arithmetic and copies ran while one was open for 5% of the time, Pallas kernels for 0%

profile of v1, /device:TPU:7, one launch (start us, length us, event | category | flops | bytes accessed | tf_op | source)
XLA Modules:
  0.0 458.3 jit_solution(4930330906509749383)
XLA Ops:
  0.6 0.0 copy-start
  0.6 3.4 broadcast_in_dim.65
  4.0 10.7 %all-to-all-start = ((bf16[32,128,512]{2,1,0:T(8,128)(2,1)}), bf16[32,128,512]{2,1,0:T(8,128)(2,1)}, u32[]{:S(2)}, u32[]{:S(2)}) async-start(bf16[32,128,512]{2,1,0:T(8,128)(2,1)} %broadcast_in_dim.65), calls=%async_computation | async-start | bytes 8388608 | tf_op jit(solution)/shard_map/all_to_all | solution.py:50
  14.8 0.0 copy-start.1
  15.5 0.0 copy-done.2
  15.5 93.2 %all-to-all-done = bf16[32,128,512]{2,1,0:T(8,128)(2,1)} async-done(((bf16[32,128,512]{2,1,0:T(8,128)(2,1)}), bf16[32,128,512]{2,1,0:T(8,128)(2,1)}, u32[]{:S(2)}, u32[]{:S(2)}) %all-to-all-start) | async-done | bytes 4194336 | tf_op jit(solution)/shard_map/all_to_all | solution.py:50
  108.7 2.8 gather_fusion
  111.6 0.0 copy-done.1
  111.6 2.4 convolution_bitcast_fusion.1
  114.0 5.2 %copy.21 = f32[12,128,512]{2,0,1:T(8,128)} copy(f32[12,128,512]{1,2,0:T(8,128)} %convolution_bitcast_fusion.1) | data formatting | bytes 6291456 | tf_op jit(solution)/shard_map/while/body/eval_jaxpr/sab,sbf->saf/dot_general | solution.py:29
  119.2 0.0 copy-done.3
  119.2 4.3 convolution_convert_fusion.1
  123.5 2.5 copy.22
  126.0 11.2 %all-to-all-start.1 = ((bf16[16,128,512]{2,1,0:T(8,128)(2,1)}), bf16[16,128,512]{2,1,0:T(8,128)(2,1)S(1)}, u32[]{:S(2)}, u32[]{:S(2)}) async-start(bf16[16,128,512]{2,1,0:T(8,128)(2,1)} %copy.22), calls=%async_computation.1 | async-start | bytes 4194304 | tf_op jit(solution)/shard_map/all_to_all | solution.py:57
  137.3 0.0 copy-start.5
  137.3 0.1 pad.2.clone
  137.4 47.4 %all-to-all-done.1 = bf16[16,128,512]{2,1,0:T(8,128)(2,1)S(1)} async-done(((bf16[16,128,512]{2,1,0:T(8,128)(2,1)}), bf16[16,128,512]{2,1,0:T(8,128)(2,1)S(1)}, u32[]{:S(2)}, u32[]{:S(2)}) %all-to-all-start.1) | async-done | bytes 2097184 | tf_op jit(solution)/shard_map/all_to_all | solution.py:57
  184.8 0.3 reduce_sum.51
  185.1 0.1 copy.24
  185.3 1.0 fusion.26
  186.3 0.2 concatenate.8
  186.5 0.3 fusion.8
  186.8 0.2 maximum_maximum_fusion
  186.9 38.4 %all_to_all.40 = f32[16,32,640]{2,1,0:T(8,128)S(1)} all-to-all(f32[16,32,640]{2,1,0:T(8,128)S(1)} %maximum_maximum_fusion), channel_id=1, replica_groups=mesh['row'=32,'col'=16] {'col'}, dimensions={0} | all-to-all | bytes 2621440 | tf_op jit(solution)/shard_map/all_to_all | solution.py:57
  225.3 0.1 reduce_sum.53
  225.4 0.1 reshape.110
  225.4 16.8 %all_to_all.41 = f32[32,1,640]{2,1,0:T(1,128)S(1)} all-to-all(f32[32,1,640]{2,1,0:T(1,128)S(1)} %reshape.110), channel_id=1, replica_groups=mesh['row'=32,'col'=16] {'row'}, dimensions={0} | all-to-all | bytes 163840 | tf_op jit(solution)/shard_map/all_to_all | solution.py:57
  242.3 0.1 reduce_sum.54
  242.3 0.7 broadcast_in_dim.68
  243.0 6.2 %all-to-all-start.4 = ((f32[32,1,640]{2,1,0:T(1,128)}), f32[32,1,640]{2,1,0:T(1,128)S(1)}, u32[]{:S(2)}, u32[]{:S(2)}) async-start(f32[32,1,640]{2,1,0:T(1,128)} %broadcast_in_dim.68), calls=%async_computation.4 | async-start | bytes 163840 | tf_op jit(solution)/shard_map/all_to_all | solution.py:50
  249.2 0.3 convolution_convert_fusion.2
  249.5 7.3 %all-to-all-done.4 = f32[32,1,640]{2,1,0:T(1,128)S(1)} async-done(((f32[32,1,640]{2,1,0:T(1,128)}), f32[32,1,640]{2,1,0:T(1,128)S(1)}, u32[]{:S(2)}, u32[]{:S(2)}) %all-to-all-start.4) | async-done | bytes 81952 | tf_op jit(solution)/shard_map/all_to_all | solution.py:50
  256.8 1.5 broadcast_in_dim.72
  258.4 4.8 %all-to-all-start.6 = ((bf16[16,128,512]{2,1,0:T(8,128)(2,1)}), bf16[16,128,512]{2,1,0:T(8,128)(2,1)S(1)}, u32[]{:S(2)}, u32[]{:S(2)}) async-start(bf16[16,128,512]{2,1,0:T(8,128)(2,1)} %broadcast_in_dim.72), calls=%async_computation.6 | async-start | bytes 4194304 | tf_op jit(solution)/shard_map/all_to_all | solution.py:50
  263.2 47.2 %all-to-all-done.6 = bf16[16,128,512]{2,1,0:T(8,128)(2,1)S(1)} async-done(((bf16[16,128,512]{2,1,0:T(8,128)(2,1)}), bf16[16,128,512]{2,1,0:T(8,128)(2,1)S(1)}, u32[]{:S(2)}, u32[]{:S(2)}) %all-to-all-start.6) | async-done | bytes 2097184 | tf_op jit(solution)/shard_map/all_to_all | solution.py:50
  310.4 1.2 broadcast_in_dim.70
  311.6 7.0 %all-to-all-start.5 = ((f32[16,32,640]{2,1,0:T(8,128)}), f32[16,32,640]{2,1,0:T(8,128)}, u32[]{:S(2)}, u32[]{:S(2)}) async-start(f32[16,32,640]{2,1,0:T(8,128)} %broadcast_in_dim.70), calls=%async_computation.5 | async-start | bytes 2621440 | tf_op jit(solution)/shard_map/all_to_all | solution.py:50
  318.6 1.9 gather_fusion.1
  320.5 3.8 convolution_bitcast_fusion
  324.3 5.2 %copy.27 = f32[12,128,512]{2,0,1:T(8,128)} copy(f32[12,128,512]{1,2,0:T(8,128)} %convolution_bitcast_fusion) | data formatting | bytes 6291456 | tf_op jit(solution)/shard_map/while/body/eval_jaxpr/sba,sbf->saf/dot_general | solution.py:29
  329.5 5.5 %convolution_convert_fusion = bf16[32,128,512]{2,0,1:T(8,128)(2,1)S(1)} fusion(f32[12,128,512]{2,0,1:T(8,128)} %copy.27, s32[12]{0:T(128)S(1)} %bitcast.48, pred[12]{0:T(512)(128)(4,1)S(1)} %iota_compare_fusion.2), kind=kOutput, calls=%fused_computation.2 | convolution fusion | flops 304087808 | bytes 7340092 | tf_op jit(solution)/shard_map/while/body/eval_jaxpr/rs,saf->raf/dot_general | solution.py:33
  335.0 4.3 copy.28
  339.3 8.1 %all-to-all-done.5 = f32[16,32,640]{2,1,0:T(8,128)} async-done(((f32[16,32,640]{2,1,0:T(8,128)}), f32[16,32,640]{2,1,0:T(8,128)}, u32[]{:S(2)}, u32[]{:S(2)}) %all-to-all-start.5) | async-done | bytes 1310752 | tf_op jit(solution)/shard_map/all_to_all | solution.py:50
  347.5 13.4 %all-to-all-start.7 = ((bf16[32,128,512]{2,1,0:T(8,128)(2,1)}), bf16[32,128,512]{2,1,0:T(8,128)(2,1)}, u32[]{:S(2)}, u32[]{:S(2)}) async-start(bf16[32,128,512]{2,1,0:T(8,128)(2,1)} %copy.28), calls=%async_computation.7 | async-start | bytes 8388608 | tf_op jit(solution)/shard_map/all_to_all | solution.py:110
  360.9 2.3 slice.12
  363.1 1.7 slice_reduce_fusion
  364.8 90.1 %all-to-all-done.7 = bf16[32,128,512]{2,1,0:T(8,128)(2,1)} async-done(((bf16[32,128,512]{2,1,0:T(8,128)(2,1)}), bf16[32,128,512]{2,1,0:T(8,128)(2,1)}, u32[]{:S(2)}, u32[]{:S(2)}) %all-to-all-start.7) | async-done | bytes 4194336 | tf_op jit(solution)/shard_map/all_to_all | solution.py:110
  454.9 3.5 reduce_sum.55
  (15 shorter events, 0.1 us)
Async XLA Ops:
  0.6 184.6 %copy-start = (bf16[512,512]{1,0:T(8,128)(2,1)S(1)}, bf16[512,512]{1,0:T(8,128)(2,1)}, u32[]{:S(2)}) copy-start(bf16[512,512]{1,0:T(8,128)(2,1)} %param.13) | copy-start | bytes 1572868
  4.0 11.5 %copy-start.2 = (s32[1,1,12]{2,1,0:T(1,128)S(1)}, s32[1,1,12]{2,1,0:T(1,128)}, u32[]{:S(2)}) copy-start(s32[1,1,12]{2,1,0:T(1,128)} %param.11) | copy-start | bytes 148
  4.0 104.7 %all-to-all-start = ((bf16[32,128,512]{2,1,0:T(8,128)(2,1)}), bf16[32,128,512]{2,1,0:T(8,128)(2,1)}, u32[]{:S(2)}, u32[]{:S(2)}) async-start(bf16[32,128,512]{2,1,0:T(8,128)(2,1)} %broadcast_in_dim.65), calls=%async_computation | async-start | bytes 8388608 | tf_op jit(solution)/shard_map/all_to_all | solution.py:50
  14.8 96.8 %copy-start.1 = (bf16[1,1,12,128,128]{4,3,2,1,0:T(8,128)(2,1)S(1)}, bf16[1,1,12,128,128]{4,3,2,1,0:T(8,128)(2,1)}, u32[]{:S(2)}) copy-start(bf16[1,1,12,128,128]{4,3,2,1,0:T(8,128)(2,1)} %param.9) | copy-start | bytes 1179652
  114.0 5.2 %copy-start.3 = (s32[1,1,12]{2,1,0:T(1,128)S(1)}, s32[1,1,12]{2,1,0:T(1,128)}, u32[]{:S(2)}) copy-start(s32[1,1,12]{2,1,0:T(1,128)} %param.10) | copy-start | bytes 148
  126.0 58.8 %all-to-all-start.1 = ((bf16[16,128,512]{2,1,0:T(8,128)(2,1)}), bf16[16,128,512]{2,1,0:T(8,128)(2,1)S(1)}, u32[]{:S(2)}, u32[]{:S(2)}) async-start(bf16[16,128,512]{2,1,0:T(8,128)(2,1)} %copy.22), calls=%async_computation.1 | async-start | bytes 4194304 | tf_op jit(solution)/shard_map/all_to_all | solution.py:57
  137.3 48.0 %copy-start.4 = (bf16[128,512]{1,0:T(8,128)(2,1)S(1)}, bf16[128,512]{1,0:T(8,128)(2,1)}, u32[]{:S(2)}) copy-start(bf16[128,512]{1,0:T(8,128)(2,1)} %param.15) | copy-start | bytes 393220
  137.3 48.0 %copy-start.5 = (f32[512]{0:T(512)S(1)}, f32[512]{0:T(512)}, u32[]{:S(2)}) copy-start(f32[512]{0:T(512)} %param.14) | copy-start | bytes 6148
  243.0 13.8 %all-to-all-start.4 = ((f32[32,1,640]{2,1,0:T(1,128)}), f32[32,1,640]{2,1,0:T(1,128)S(1)}, u32[]{:S(2)}, u32[]{:S(2)}) async-start(f32[32,1,640]{2,1,0:T(1,128)} %broadcast_in_dim.68), calls=%async_computation.4 | async-start | bytes 163840 | tf_op jit(solution)/shard_map/all_to_all | solution.py:50
  258.4 52.0 %all-to-all-start.6 = ((bf16[16,128,512]{2,1,0:T(8,128)(2,1)}), bf16[16,128,512]{2,1,0:T(8,128)(2,1)S(1)}, u32[]{:S(2)}, u32[]{:S(2)}) async-start(bf16[16,128,512]{2,1,0:T(8,128)(2,1)} %broadcast_in_dim.72), calls=%async_computation.6 | async-start | bytes 4194304 | tf_op jit(solution)/shard_map/all_to_all | solution.py:50
  311.6 35.9 %all-to-all-start.5 = ((f32[16,32,640]{2,1,0:T(8,128)}), f32[16,32,640]{2,1,0:T(8,128)}, u32[]{:S(2)}, u32[]{:S(2)}) async-start(f32[16,32,640]{2,1,0:T(8,128)} %broadcast_in_dim.70), calls=%async_computation.5 | async-start | bytes 2621440 | tf_op jit(solution)/shard_map/all_to_all | solution.py:50
  347.5 107.4 %all-to-all-start.7 = ((bf16[32,128,512]{2,1,0:T(8,128)(2,1)}), bf16[32,128,512]{2,1,0:T(8,128)(2,1)}, u32[]{:S(2)}, u32[]{:S(2)}) async-start(bf16[32,128,512]{2,1,0:T(8,128)(2,1)} %copy.28), calls=%async_computation.7 | async-start | bytes 8388608 | tf_op jit(solution)/shard_map/all_to_all | solution.py:110

commit v2 on v1

--- a/solution.py
+++ b/solution.py
@@ -1,7 +1,84 @@
+import functools
+
 import jax
 import jax.numpy as jnp
 from jax import lax
+from jax.experimental import pallas as pl
+from jax.experimental.pallas import tpu as pltpu
 from jax.sharding import PartitionSpec as P
+
+MESH_ID = pl.DeviceIdType.MESH
+
+
+def _exchange_kernel(axis, other, n, broadcast, src_ref, out_ref, send_sem, recv_sem, own_sem):
+    me = lax.axis_index(axis)
+    there = lax.axis_index(other)
+
+    def device(k):
+        return (k, there) if axis == "row" else (there, k)
+
+    def piece(k):
+        return src_ref if broadcast else src_ref.at[k]
+
+    barrier = pltpu.get_barrier_semaphore()
+
+    def greet(step, carry):
+        peer = lax.rem(me + step, n)
+        pl.semaphore_signal(barrier, inc=1, device_id=device(peer), device_id_type=MESH_ID)
+        return carry
+
+    lax.fori_loop(1, n, greet, 0)
+    pl.semaphore_wait(barrier, n - 1)
+
+    own = pltpu.make_async_copy(piece(me), out_ref.at[me], own_sem)
+    own.start()
+
+    def send(step, carry):
+        peer = lax.rem(me + step, n)
+        pltpu.make_async_remote_copy(
+            src_ref=piece(peer), dst_ref=out_ref.at[me], send_sem=send_sem.at[step],
+            recv_sem=recv_sem.at[step], device_id=device(peer), device_id_type=MESH_ID,
+        ).start()
+        return carry
+
+    lax.fori_loop(1, n, send, 0)
+
+    def finish(step, carry):
+        peer = lax.rem(me + step, n)
+        source = lax.rem(me + n - step, n)
+        pltpu.make_async_remote_copy(
+            src_ref=piece(peer), dst_ref=out_ref.at[me], send_sem=send_sem.at[step],
+            recv_sem=recv_sem.at[step], device_id=device(peer), device_id_type=MESH_ID,
+        ).wait_send()
+        pltpu.make_async_remote_copy(
+            src_ref=piece(source), dst_ref=out_ref.at[source], send_sem=send_sem.at[step],
+            recv_sem=recv_sem.at[step], device_id=device(source), device_id_type=MESH_ID,
+        ).wait_recv()
+        return carry
+
+    lax.fori_loop(1, n, finish, 0)
+    own.wait()
+
+
+def exchange(x, axis, broadcast, ident):
+    n = lax.axis_size(axis)
+    other = "col" if axis == "row" else "row"
+    shape = (n,) + (x.shape if broadcast else x.shape[1:])
+    return pl.pallas_call(
+        functools.partial(_exchange_kernel, axis, other, n, broadcast),
+        out_shape=jax.ShapeDtypeStruct(shape, x.dtype),
+        in_specs=[pl.BlockSpec(memory_space=pl.ANY)],
+        out_specs=pl.BlockSpec(memory_space=pl.ANY),
+        scratch_shapes=[
+            pltpu.SemaphoreType.DMA((n,)),
+            pltpu.SemaphoreType.DMA((n,)),
+            pltpu.SemaphoreType.DMA(()),
+        ],
+        compiler_params=pltpu.CompilerParams(collective_id=ident, has_side_effects=True),
+        cost_estimate=pl.CostEstimate(
+            flops=0, transcendentals=0, bytes_accessed=2 * n * x.size * x.dtype.itemsize
+        ),
+    )(x)
 
 
 def slot_product(tile_values, tile_rows, tile_cols, live_count, source, out_len, backward):
@@ -58,13 +135,14 @@
     return jnp.sum(received.astype(jnp.float32), axis=0)
 
 
-def global_grads(local_weight, local_bias):
-    width = local_weight.shape[1]
+def pack_grads(local_weight, local_bias):
     pad = jnp.zeros((local_weight.shape[0], 127), jnp.float32)
-    packed = jnp.concatenate([local_weight, local_bias[:, None], pad], axis=1)
-    by_col = scatter_sum(packed, "col")
-    total = scatter_sum(by_col, "row")
-    whole = gather_rows(gather_rows(total, "row"), "col")
+    return jnp.concatenate([local_weight, local_bias[:, None], pad], axis=1)
+
+
+def unpack_grads(by_col_then_row, width):
+    cols, rows = by_col_then_row.shape[0], by_col_then_row.shape[1]
+    whole = by_col_then_row.transpose(1, 0, 2).reshape(cols * rows, -1)
     return whole[:, :width], whole[:, width]
 
 
@@ -104,12 +182,20 @@
     )
     local_bias = jnp.sum(grad_pre, axis=0)
     grad_agg = transposed_product(grad_low, weight)
-    grad_panel = gather_rows(grad_agg, "col")
+    packed = pack_grads(local_weight, local_bias)
+    by_row = scatter_sum(packed, "row")
+    grad_panel = exchange(grad_agg, "col", True, 0).reshape(-1, width)
+    grad_panel, by_row = lax.optimization_barrier((grad_panel, by_row))
+    reduced = scatter_sum(by_row, "col")
     back = slot_product(tile_values, tile_rows, tile_cols, live_count, grad_panel, col_len, True)
     back_low = back.astype(jnp.bfloat16).reshape(col_len // own_nodes, own_nodes, width)
-    received = lax.all_to_all(back_low, "row", split_axis=0, concat_axis=0, tiled=True)
+    back_low, reduced = lax.optimization_barrier((back_low, reduced))
+    row_part = gather_rows(reduced, "row")
+    back_low, row_part = lax.optimization_barrier((back_low, row_part))
+    received = exchange(back_low, "row", False, 1)
+    every = gather_rows(row_part[None], "col")
     feature_grad = source_total(received)
-    weight_grad, bias_grad = global_grads(local_weight, local_bias)
+    weight_grad, bias_grad = unpack_grads(every, width)
     return (hidden, weight_grad, bias_grad, feature_grad)
 
 

time: 461 us -> 433 us (0.939)
  the two profiles are of different devices: /device:TPU:7 before, /device:TPU:87 now
where the time goes in v2:
time: 433 us; the launch traced here: 432 us
  Pallas kernels  176 us (41%)
  waiting for transfers between devices  140 us (32%)
  starting transfers between devices  47.5 us (11%)
  local copies, waits for them, and re-layouts  30.8 us (7%)
  matrix products  16.9 us (4%)
  blocking collectives  15.1 us (3%)
  other arithmetic  5.15 us (1%)
    pallas_call x2, Pallas kernels, exchange(): pl.pallas_call(functools.partial(_exchange_kernel, axis, other, n, broadc...  176 us
    all_to_all x2, waiting for transfers between devices, gather_rows(): lax.all_to_all(stacked, axis, split_axis=0, concat_axis=0, tiled=True)  93.5 us
    all_to_all x3, waiting for transfers between devices, scatter_sum(): lax.all_to_all(pieces, axis, split_axis=0, concat_axis=0, tiled=True)  46.1 us
    all_to_all x3, starting transfers between devices, scatter_sum(): lax.all_to_all(pieces, axis, split_axis=0, concat_axis=0, tiled=True)  29.4 us
    all_to_all x2, starting transfers between devices, gather_rows(): lax.all_to_all(stacked, axis, split_axis=0, concat_axis=0, tiled=True)  18.1 us
    all_to_all x1, blocking collectives, gather_rows(): lax.all_to_all(stacked, axis, split_axis=0, concat_axis=0, tiled=True)  15.1 us
    dot_general x2, local copies, waits for them, and re-layouts, one_group(): jnp.einsum(form, values_part, segments, preferred_element_type=jnp.float32)  10.4 us
    dot_general x2, matrix products, one_group(): jnp.einsum('rs,saf->raf', selector, products, precision=lax.Precision.HIG...  9.83 us
  transfers between devices with their start and end apart: 5, of which 2 were waited for; matrix products, arithmetic and copies ran while one was open for 6% of the time, Pallas kernels for 41%

profile of v2, /device:TPU:87, one launch (start us, length us, event | category | flops | bytes accessed | tf_op | source)
XLA Modules:
  0.0 432.1 jit_solution(10347086245425832048)
XLA Ops:
  0.6 0.0 copy-start
  0.6 3.4 broadcast_in_dim.59
  4.1 10.5 %all-to-all-start = ((bf16[32,128,512]{2,1,0:T(8,128)(2,1)}), bf16[32,128,512]{2,1,0:T(8,128)(2,1)}, u32[]{:S(2)}, u32[]{:S(2)}) async-start(bf16[32,128,512]{2,1,0:T(8,128)(2,1)} %broadcast_in_dim.59), calls=%async_computation | async-start | bytes 8388608 | tf_op jit(solution)/shard_map/all_to_all | solution.py:127
  15.2 0.0 copy-done.2
  15.3 0.0 copy-start.1
  15.3 93.5 %all-to-all-done = bf16[32,128,512]{2,1,0:T(8,128)(2,1)} async-done(((bf16[32,128,512]{2,1,0:T(8,128)(2,1)}), bf16[32,128,512]{2,1,0:T(8,128)(2,1)}, u32[]{:S(2)}, u32[]{:S(2)}) %all-to-all-start) | async-done | bytes 4194336 | tf_op jit(solution)/shard_map/all_to_all | solution.py:127
  108.7 2.8 gather_fusion
  111.6 0.0 copy-done.1
  111.6 2.4 convolution_bitcast_fusion.1
  114.0 5.2 %copy.23 = f32[12,128,512]{2,0,1:T(8,128)} copy(f32[12,128,512]{1,2,0:T(8,128)} %convolution_bitcast_fusion.1) | data formatting | bytes 6291456 | tf_op jit(solution)/shard_map/while/body/eval_jaxpr/sab,sbf->saf/dot_general | solution.py:106
  119.2 0.0 copy-done.3
  119.2 4.3 %convolution_convert_fusion = bf16[16,128,512]{2,0,1:T(8,128)(2,1)S(1)} fusion(f32[12,128,512]{2,0,1:T(8,128)} %copy.23, s32[12]{0:T(128)S(1)} %bitcast.57, pred[12]{0:T(512)(128)(4,1)S(1)} %iota_compare_fusion.2), kind=kOutput, calls=%fused_computation.5 | convolution fusion | flops 152043904 | bytes 5242940 | tf_op jit(solution)/shard_map/while/body/eval_jaxpr/rs,saf->raf/dot_general | solution.py:110
  123.6 2.5 copy.24
  126.1 10.3 %all-to-all-start.1 = ((bf16[16,128,512]{2,1,0:T(8,128)(2,1)}), bf16[16,128,512]{2,1,0:T(8,128)(2,1)S(1)}, u32[]{:S(2)}, u32[]{:S(2)}) async-start(bf16[16,128,512]{2,1,0:T(8,128)(2,1)} %copy.24), calls=%async_computation.1 | async-start | bytes 4194304 | tf_op jit(solution)/shard_map/all_to_all | solution.py:134
  136.4 0.0 copy-start.5
  136.4 0.1 pad.2.clone
  136.5 46.1 %all-to-all-done.1 = bf16[16,128,512]{2,1,0:T(8,128)(2,1)S(1)} async-done(((bf16[16,128,512]{2,1,0:T(8,128)(2,1)}), bf16[16,128,512]{2,1,0:T(8,128)(2,1)S(1)}, u32[]{:S(2)}, u32[]{:S(2)}) %all-to-all-start.1) | async-done | bytes 2097184 | tf_op jit(solution)/shard_map/all_to_all | solution.py:134
  182.6 0.3 reduce_sum.53
  182.9 0.1 copy.26
  183.1 0.0 copy-done
  183.1 0.0 copy-done.4
  183.1 0.0 copy-done.5
  183.1 1.0 fusion.27
  184.1 0.2 concatenate.8
  184.3 0.3 fusion.8
  184.6 1.2 maximum_maximum_fusion
  185.8 8.7 %all-to-all-start.2 = ((f32[32,16,640]{2,1,0:T(8,128)}), f32[32,16,640]{2,1,0:T(8,128)S(1)}, u32[]{:S(2)}, u32[]{:S(2)}) async-start(f32[32,16,640]{2,1,0:T(8,128)} %maximum_maximum_fusion), calls=%async_computation.2 | async-start | bytes 2621440 | tf_op jit(solution)/shard_map/all_to_all | solution.py:134
  194.5 1.0 convolution_convert_fusion.1.src_ref
  195.5 55.8 %shard_map.111 = bf16[16,128,512]{2,1,0:T(8,128)(2,1)} custom-call(bf16[128,512]{1,0:T(8,128)(2,1)} %convolution_convert_fusion.1.src_ref), custom_call_target="tpu_custom_call" | custom-call | bytes 4194304 | tf_op jit(solution)/shard_map/pallas_call | solution.py:67
  251.3 0.0 all-to-all-done.2
  251.3 0.1 reduce_sum.55
  251.4 0.6 reshape.124
  252.0 10.4 %all-to-all-start.3 = ((f32[16,1,640]{2,1,0:T(1,128)}), f32[16,1,640]{2,1,0:T(1,128)S(1)}, u32[]{:S(2)}, u32[]{:S(2)}) async-start(f32[16,1,640]{2,1,0:T(1,128)} %reshape.124), calls=%async_computation.3 | async-start | bytes 81920 | tf_op jit(solution)/shard_map/all_to_all | solution.py:134
  262.5 2.2 gather_fusion.1
  264.7 2.4 convolution_bitcast_fusion
  267.1 5.2 %copy.29 = f32[12,128,512]{2,0,1:T(8,128)} copy(f32[12,128,512]{1,2,0:T(8,128)} %convolution_bitcast_fusion) | data formatting | bytes 6291456 | tf_op jit(solution)/shard_map/while/body/eval_jaxpr/sba,sbf->saf/dot_general | solution.py:106
  272.3 5.5 %fusion.17 = bf16[32,128,512]{2,0,1:T(8,128)(2,1)S(1)} fusion(f32[12,128,512]{2,0,1:T(8,128)} %copy.29, s32[12]{0:T(128)S(1)} %bitcast.56, pred[12]{0:T(512)(128)(4,1)S(1)} %iota_compare_fusion.2), kind=kOutput, calls=%fused_computation.32 | convolution fusion | flops 301990656 | bytes 7340092 | tf_op jit(solution)/shard_map/while/body/eval_jaxpr/rs,saf->raf/dot_general | solution.py:110
  277.8 4.3 %copy.38.src_ref = bf16[32,128,512]{2,1,0:T(8,128)(2,1)} copy(bf16[32,128,512]{2,0,1:T(8,128)(2,1)S(1)} %fusion.17) | data formatting | bytes 8388608 | tf_op jit(solution)/shard_map/while/body/eval_jaxpr/rs,saf->raf/dot_general | solution.py:110
  282.2 0.0 all-to-all-done.3
  282.3 15.1 %all_to_all.30 = f32[32,1,640]{2,1,0:T(1,128)S(1)} all-to-all(f32[32,1,640]{2,1,0:T(1,128)S(1)} %broadcast_in_dim.64), channel_id=1, replica_groups=mesh['row'=32,'col'=16] {'row'}, dimensions={0} | all-to-all | bytes 163840 | tf_op jit(solution)/shard_map/all_to_all | solution.py:127
  297.4 1.3 broadcast_in_dim.65
  298.7 7.6 %all-to-all-start.5 = ((f32[16,1,32,640]{3,2,1,0:T(8,128)}), f32[16,1,32,640]{3,2,1,0:T(8,128)S(1)}, u32[]{:S(2)}, u32[]{:S(2)}) async-start(f32[16,1,32,640]{3,2,1,0:T(8,128)} %broadcast_in_dim.65), calls=%async_computation.5 | async-start | bytes 2621440 | tf_op jit(solution)/shard_map/all_to_all | solution.py:127
  306.3 119.8 %shard_map.112 = bf16[32,128,512]{2,1,0:T(8,128)(2,1)} custom-call(bf16[32,128,512]{2,1,0:T(8,128)(2,1)} %copy.38.src_ref), custom_call_target="tpu_custom_call" | custom-call | bytes 268435456 | tf_op jit(solution)/shard_map/pallas_call | solution.py:67
  426.1 3.5 reduce_sum.58
  429.5 0.0 all-to-all-done.5
  429.5 0.8 copy.31
  430.3 0.7 slice_reduce_fusion
  431.0 1.1 slice.12
  (16 shorter events, 0.2 us)
Async XLA Ops:
  0.6 182.4 %copy-start = (bf16[512,512]{1,0:T(8,128)(2,1)S(1)}, bf16[512,512]{1,0:T(8,128)(2,1)}, u32[]{:S(2)}) copy-start(bf16[512,512]{1,0:T(8,128)(2,1)} %param.13) | copy-start | bytes 1572868
  4.0 11.2 %copy-start.2 = (s32[1,1,12]{2,1,0:T(1,128)S(1)}, s32[1,1,12]{2,1,0:T(1,128)}, u32[]{:S(2)}) copy-start(s32[1,1,12]{2,1,0:T(1,128)} %param.11) | copy-start | bytes 148
  4.1 104.7 %all-to-all-start = ((bf16[32,128,512]{2,1,0:T(8,128)(2,1)}), bf16[32,128,512]{2,1,0:T(8,128)(2,1)}, u32[]{:S(2)}, u32[]{:S(2)}) async-start(bf16[32,128,512]{2,1,0:T(8,128)(2,1)} %broadcast_in_dim.59), calls=%async_computation | async-start | bytes 8388608 | tf_op jit(solution)/shard_map/all_to_all | solution.py:127
  15.3 96.3 %copy-start.1 = (bf16[1,1,12,128,128]{4,3,2,1,0:T(8,128)(2,1)S(1)}, bf16[1,1,12,128,128]{4,3,2,1,0:T(8,128)(2,1)}, u32[]{:S(2)}) copy-start(bf16[1,1,12,128,128]{4,3,2,1,0:T(8,128)(2,1)} %param.9) | copy-start | bytes 1179652
  114.0 5.2 %copy-start.3 = (s32[1,1,12]{2,1,0:T(1,128)S(1)}, s32[1,1,12]{2,1,0:T(1,128)}, u32[]{:S(2)}) copy-start(s32[1,1,12]{2,1,0:T(1,128)} %param.10) | copy-start | bytes 148
  126.1 56.6 %all-to-all-start.1 = ((bf16[16,128,512]{2,1,0:T(8,128)(2,1)}), bf16[16,128,512]{2,1,0:T(8,128)(2,1)S(1)}, u32[]{:S(2)}, u32[]{:S(2)}) async-start(bf16[16,128,512]{2,1,0:T(8,128)(2,1)} %copy.24), calls=%async_computation.1 | async-start | bytes 4194304 | tf_op jit(solution)/shard_map/all_to_all | solution.py:134
  136.4 46.7 %copy-start.4 = (bf16[128,512]{1,0:T(8,128)(2,1)S(1)}, bf16[128,512]{1,0:T(8,128)(2,1)}, u32[]{:S(2)}) copy-start(bf16[128,512]{1,0:T(8,128)(2,1)} %param.15) | copy-start | bytes 393220
  136.4 46.7 %copy-start.5 = (f32[512]{0:T(512)S(1)}, f32[512]{0:T(512)}, u32[]{:S(2)}) copy-start(f32[512]{0:T(512)} %param.14) | copy-start | bytes 6148
  185.8 65.5 %all-to-all-start.2 = ((f32[32,16,640]{2,1,0:T(8,128)}), f32[32,16,640]{2,1,0:T(8,128)S(1)}, u32[]{:S(2)}, u32[]{:S(2)}) async-start(f32[32,16,640]{2,1,0:T(8,128)} %maximum_maximum_fusion), calls=%async_computation.2 | async-start | bytes 2621440 | tf_op jit(solution)/shard_map/all_to_all | solution.py:134
  252.0 30.1 %all-to-all-start.3 = ((f32[16,1,640]{2,1,0:T(1,128)}), f32[16,1,640]{2,1,0:T(1,128)S(1)}, u32[]{:S(2)}, u32[]{:S(2)}) async-start(f32[16,1,640]{2,1,0:T(1,128)} %reshape.124), calls=%async_computation.3 | async-start | bytes 81920 | tf_op jit(solution)/shard_map/all_to_all | solution.py:134
  298.7 130.8 %all-to-all-start.5 = ((f32[16,1,32,640]{3,2,1,0:T(8,128)}), f32[16,1,32,640]{3,2,1,0:T(8,128)S(1)}, u32[]{:S(2)}, u32[]{:S(2)}) async-start(f32[16,1,32,640]{3,2,1,0:T(8,128)} %broadcast_in_dim.65), calls=%async_computation.5 | async-start | bytes 2621440 | tf_op jit(solution)/shard_map/all_to_all | solution.py:127

commit v3 on v2

--- a/solution.py
+++ b/solution.py
@@ -81,44 +81,67 @@
     )(x)
 
 
+def _slot_kernel(backward, slots, src_ids, tgt_ids, count_ref, vals_ref, src_ref, out_ref, acc_ref):
+    s = pl.program_id(0)
+
+    @pl.when(s == 0)
+    def _():
+        acc_ref[...] = jnp.zeros_like(acc_ref)
+
+    @pl.when(s < count_ref[0])
+    def _():
+        block = vals_ref[0]
+        segment = src_ref[0]
+        if backward:
+            dims = (((0,), (0,)), ((), ()))
+        else:
+            dims = (((1,), (0,)), ((), ()))
+        product = lax.dot_general(block, segment, dims, preferred_element_type=jnp.float32)
+        target = tgt_ids[s]
+        acc_ref[target] = acc_ref[target] + product
+
+    @pl.when(s == slots - 1)
+    def _():
+        out_ref[...] = acc_ref[...].astype(out_ref.dtype)
+
+
 def slot_product(tile_values, tile_rows, tile_cols, live_count, source, out_len, backward):
-    capacity = tile_values.shape[0]
-    block_size = tile_values.shape[1]
+    slots, block_size = tile_values.shape[0], tile_values.shape[1]
     width = source.shape[1]
-    group = max([d for d in range(1, min(capacity, 16) + 1) if capacity % d == 0])
-    groups = capacity // group
-    panels = source.reshape(source.shape[0] // block_size, block_size, width)
-    out_blocks = out_len // block_size
+    n_src = source.shape[0] // block_size
+    n_out = out_len // block_size
+    panels = source.reshape(n_src, block_size, width)
     if backward:
-        source_ids = tile_rows
-        target_ids = tile_cols
-        form = "sba,sbf->saf"
+        src_ids, tgt_ids = tile_rows, tile_cols
     else:
-        source_ids = tile_cols
-        target_ids = tile_rows
-        form = "sab,sbf->saf"
-    alive = jnp.arange(capacity, dtype=jnp.int32) < live_count
-    places = jnp.arange(out_blocks, dtype=jnp.int32)
-
-    def one_group(total, items):
-        values_part, source_part, target_part, alive_part = items
-        segments = jnp.take(panels, source_part, axis=0)
-        products = jnp.einsum(form, values_part, segments, preferred_element_type=jnp.float32)
-        selector = ((target_part[None, :] == places[:, None]) & alive_part[None, :]).astype(
-            jnp.float32
-        )
-        added = jnp.einsum("rs,saf->raf", selector, products, precision=lax.Precision.HIGHEST)
-        return (total + added, None)
-
-    items = (
-        tile_values.reshape(groups, group, block_size, block_size),
-        source_ids.reshape(groups, group),
-        target_ids.reshape(groups, group),
-        alive.reshape(groups, group),
-    )
-    start = jnp.zeros((out_blocks, block_size, width), jnp.float32)
-    total, _ = lax.scan(one_group, start, items)
-    return total.reshape(out_len, width)
+        src_ids, tgt_ids = tile_cols, tile_rows
+    src_ids = jnp.clip(src_ids, 0, n_src - 1).astype(jnp.int32)
+    tgt_ids = jnp.clip(tgt_ids, 0, n_out - 1).astype(jnp.int32)
+    count = jnp.reshape(live_count, (1,)).astype(jnp.int32)
+    grid_spec = pltpu.PrefetchScalarGridSpec(
+        num_scalar_prefetch=3,
+        grid=(slots,),
+        in_specs=[
+            pl.BlockSpec((1, block_size, block_size), lambda s, src, tgt, cnt: (s, 0, 0)),
+            pl.BlockSpec((1, block_size, width), lambda s, src, tgt, cnt: (src[s], 0, 0)),
+        ],
+        out_specs=pl.BlockSpec((n_out, block_size, width), lambda s, src, tgt, cnt: (0, 0, 0)),
+        scratch_shapes=[pltpu.VMEM((n_out, block_size, width), jnp.float32)],
+    )
+    out = pl.pallas_call(
+        functools.partial(_slot_kernel, backward, slots),
+        out_shape=jax.ShapeDtypeStruct((n_out, block_size, width), jnp.bfloat16),
+        grid_spec=grid_spec,
+        compiler_params=pltpu.CompilerParams(
+            dimension_semantics=("arbitrary",), vmem_limit_bytes=48 * 1024 * 1024
+        ),
+        cost_estimate=pl.CostEstimate(
+            flops=2 * slots * block_size * block_size * width,
+            transcendentals=0,
+            bytes_accessed=2 * (slots * block_size * (block_size + width) + n_out * block_size * width),
+        ),
+    )(src_ids, tgt_ids, count, tile_values, panels)
+    return out.reshape(out_len, width)
 
 
 def gather_rows(x, axis):

time: 433 us -> 412 us (0.952)
  local copies, waits for them, and re-layouts: 30.8 us -> 10 us
  matrix products: 16.9 us -> 2.24 us
  Pallas kernels: 176 us -> 189 us
    dot_general x3 -> x0, local copies, waits for them, and re-layouts: 14.8 us -> none  [the longest x2 10.4 us: one_group(): jnp.einsum(form, values_part, segments, preferred_element_type=jnp.float32)]
    dot_general x4 -> x0, matrix products: 14.6 us -> none  [the longest x2 9.83 us: one_group(): jnp.einsum('rs,saf->raf', selector, products, precision=lax.Precision.HIG...]
    pallas_call x0 -> x2, Pallas kernels: none -> 13.8 us  [slot_product(): pl.pallas_call(functools.partial(_slot_kernel, backward, slots), out_shap...]
    gather x2 -> x0, local copies, waits for them, and re-layouts: 5.07 us -> none  [one_group(): segments = jnp.take(panels, source_part, axis=0)]
  transfers between devices with their start and end apart: 5 -> 5, of which waited for: 2 -> 2; matrix products, arithmetic and copies ran while one was open for 6% -> 1% of each run, Pallas kernels for 41% -> 44%
where the time goes in v3:
time: 412 us; the launch traced here: 411 us
  Pallas kernels  189 us (46%)
  waiting for transfers between devices  140 us (34%)
  starting transfers between devices  47.6 us (12%)
  blocking collectives  16 us (4%)
  local copies, waits for them, and re-layouts  10 us (2%)
  other arithmetic  5.11 us (1%)
    pallas_call x2, Pallas kernels, exchange(): pl.pallas_call(functools.partial(_exchange_kernel, axis, other, n, broadc...  175 us
    all_to_all x2, waiting for transfers between devices, gather_rows(): lax.all_to_all(stacked, axis, split_axis=0, concat_axis=0, tiled=True)  93.5 us
    all_to_all x3, waiting for transfers between devices, scatter_sum(): lax.all_to_all(pieces, axis, split_axis=0, concat_axis=0, tiled=True)  46.4 us
    all_to_all x3, starting transfers between devices, scatter_sum(): lax.all_to_all(pieces, axis, split_axis=0, concat_axis=0, tiled=True)  30 us
    all_to_all x2, starting transfers between devices, gather_rows(): lax.all_to_all(stacked, axis, split_axis=0, concat_axis=0, tiled=True)  17.7 us
    all_to_all x1, blocking collectives, gather_rows(): lax.all_to_all(stacked, axis, split_axis=0, concat_axis=0, tiled=True)  16 us
    pallas_call x2, Pallas kernels, slot_product(): pl.pallas_call(functools.partial(_slot_kernel, backward, slots), out_shap...  13.8 us
  transfers between devices with their start and end apart: 5, of which 2 were waited for; matrix products, arithmetic and copies ran while one was open for 1% of the time, Pallas kernels for 44%

profile of v3, /device:TPU:87, one launch (start us, length us, event | category | flops | bytes accessed | tf_op | source)
XLA Modules:
  0.0 411.5 jit_solution(2172706140501116382)
XLA Ops:
  0.6 0.0 copy-start
  0.6 3.4 broadcast_in_dim.10
  4.0 0.0 copy-start.3
  4.1 0.0 copy-start.4
  4.1 0.0 copy-start.2
  4.1 10.5 %all-to-all-start = ((bf16[32,128,512]{2,1,0:T(8,128)(2,1)}), bf16[32,128,512]{2,1,0:T(8,128)(2,1)}, u32[]{:S(2)}, u32[]{:S(2)}) async-start(bf16[32,128,512]{2,1,0:T(8,128)(2,1)} %broadcast_in_dim.10), calls=%async_computation | async-start | bytes 8388608 | tf_op jit(solution)/shard_map/all_to_all | solution.py:150
  15.2 0.0 copy-done.3
  15.2 0.0 copy-done.4
  15.2 93.5 %all-to-all-done.src_ref = bf16[32,128,512]{2,1,0:T(8,128)(2,1)} async-done(((bf16[32,128,512]{2,1,0:T(8,128)(2,1)}), bf16[32,128,512]{2,1,0:T(8,128)(2,1)}, u32[]{:S(2)}, u32[]{:S(2)}) %all-to-all-start) | async-done | bytes 4194336 | tf_op jit(solution)/shard_map/all_to_all | solution.py:150
  108.7 0.0 copy-done.2
  108.8 8.6 %shard_map.111 = bf16[16,128,512]{2,1,0:T(8,128)(2,1)} custom-call(s32[12]{0:T(128)S(1)} %get-tuple-element.20.src_ids.tgt_ids, s32[12]{0:T(128)S(1)} %get-tuple-element.19.tgt_ids.src_ids, s32[1]{0:T(128)} %bitcast.26.count_ref, bf16[12,128,128]{2,1,0:T(8,128)(2,1)S(1)} %bitcast.28, bf16[32,128,512]{2,1,0:T(8,128)(2,1)} %all-to-all-done.src_ref), custom_call_target="tpu_custom_call" | custom-call | flops 201326592 | bytes 4063232 | tf_op jit(solution)/shard_map/pallas_call | solution.py:131
  117.4 10.7 %all-to-all-start.1 = ((bf16[16,128,512]{2,1,0:T(8,128)(2,1)}), bf16[16,128,512]{2,1,0:T(8,128)(2,1)S(1)}, u32[]{:S(2)}, u32[]{:S(2)}) async-start(bf16[16,128,512]{2,1,0:T(8,128)(2,1)} %shard_map.111), calls=%async_computation.1 | async-start | bytes 4194304 | tf_op jit(solution)/shard_map/all_to_all | solution.py:157
  128.1 0.0 copy-start.5
  128.1 0.0 copy-start.6
  128.1 0.1 pad.2.clone
  128.2 46.4 %all-to-all-done.1 = bf16[16,128,512]{2,1,0:T(8,128)(2,1)S(1)} async-done(((bf16[16,128,512]{2,1,0:T(8,128)(2,1)}), bf16[16,128,512]{2,1,0:T(8,128)(2,1)S(1)}, u32[]{:S(2)}, u32[]{:S(2)}) %all-to-all-start.1) | async-done | bytes 2097184 | tf_op jit(solution)/shard_map/all_to_all | solution.py:157
  174.5 0.3 reduce_sum.53
  174.8 0.1 copy.15
  175.0 0.0 copy-done
  175.0 0.0 copy-done.5
  175.0 0.0 copy-done.6
  175.0 1.0 fusion.4
  176.0 0.2 concatenate.8
  176.2 0.3 fusion
  176.5 1.2 maximum_maximum_fusion
  177.7 8.6 %all-to-all-start.2 = ((f32[32,16,640]{2,1,0:T(8,128)}), f32[32,16,640]{2,1,0:T(8,128)S(1)}, u32[]{:S(2)}, u32[]{:S(2)}) async-start(f32[32,16,640]{2,1,0:T(8,128)} %maximum_maximum_fusion), calls=%async_computation.2 | async-start | bytes 2621440 | tf_op jit(solution)/shard_map/all_to_all | solution.py:157
  186.2 1.0 convolution_convert_fusion.src_ref
  187.2 55.5 %shard_map.112 = bf16[16,128,512]{2,1,0:T(8,128)(2,1)} custom-call(bf16[128,512]{1,0:T(8,128)(2,1)} %convolution_convert_fusion.src_ref), custom_call_target="tpu_custom_call" | custom-call | bytes 4194304 | tf_op jit(solution)/shard_map/pallas_call | solution.py:67
  242.8 0.0 all-to-all-done.2
  242.8 0.1 reduce_sum.55
  242.8 0.6 reshape.49
  243.5 10.7 %all-to-all-start.3 = ((f32[16,1,640]{2,1,0:T(1,128)}), f32[16,1,640]{2,1,0:T(1,128)S(1)}, u32[]{:S(2)}, u32[]{:S(2)}) async-start(f32[16,1,640]{2,1,0:T(1,128)} %reshape.49), calls=%async_computation.3 | async-start | bytes 81920 | tf_op jit(solution)/shard_map/all_to_all | solution.py:157
  254.2 0.0 copy-start.1
  254.2 1.6 copy-done.1
  255.8 5.2 %shard_map.113.src_ref = bf16[32,128,512]{2,1,0:T(8,128)(2,1)} custom-call(s32[12]{0:T(128)S(1)} %get-tuple-element.19.tgt_ids.src_ids, s32[12]{0:T(128)S(1)} %get-tuple-element.20.src_ids.tgt_ids, s32[1]{0:T(128)} %bitcast.27.count_ref, bf16[12,128,128]{2,1,0:T(8,128)(2,1)S(1)} %bitcast.29, bf16[16,128,512]{2,1,0:T(8,128)(2,1)S(1)} %copy-done.1), custom_call_target="tpu_custom_call" | custom-call | flops 201326592 | bytes 6160384 | tf_op jit(solution)/shard_map/pallas_call | solution.py:131
  261.0 0.0 all-to-all-done.3
  261.1 16.0 %all_to_all.30 = f32[32,1,640]{2,1,0:T(1,128)S(1)} all-to-all(f32[32,1,640]{2,1,0:T(1,128)S(1)} %broadcast_in_dim.13), channel_id=1, replica_groups=mesh['row'=32,'col'=16] {'row'}, dimensions={0} | all-to-all | bytes 163840 | tf_op jit(solution)/shard_map/all_to_all | solution.py:150
  277.1 1.3 broadcast_in_dim.28
  278.4 7.2 %all-to-all-start.5 = ((f32[16,1,32,640]{3,2,1,0:T(8,128)}), f32[16,1,32,640]{3,2,1,0:T(8,128)S(1)}, u32[]{:S(2)}, u32[]{:S(2)}) async-start(f32[16,1,32,640]{3,2,1,0:T(8,128)} %broadcast_in_dim.28), calls=%async_computation.5 | async-start | bytes 2621440 | tf_op jit(solution)/shard_map/all_to_all | solution.py:150
  285.6 119.8 %shard_map.114 = bf16[32,128,512]{2,1,0:T(8,128)(2,1)} custom-call(bf16[32,128,512]{2,1,0:T(8,128)(2,1)} %shard_map.113.src_ref), custom_call_target="tpu_custom_call" | custom-call | bytes 268435456 | tf_op jit(solution)/shard_map/pallas_call | solution.py:67
  405.4 3.5 reduce_sum.58
  408.9 0.0 all-to-all-done.5
  408.9 0.8 copy.17
  409.6 1.1 slice.8
  410.7 0.7 slice_reduce_fusion
  (7 shorter events, 0.1 us)
Async XLA Ops:
  0.6 174.3 %copy-start = (bf16[512,512]{1,0:T(8,128)(2,1)S(1)}, bf16[512,512]{1,0:T(8,128)(2,1)}, u32[]{:S(2)}) copy-start(bf16[512,512]{1,0:T(8,128)(2,1)} %param.13) | copy-start | bytes 1572868
  4.0 11.2 %copy-start.3 = (s32[1,1,12]{2,1,0:T(1,128)S(1)}, s32[1,1,12]{2,1,0:T(1,128)}, u32[]{:S(2)}) copy-start(s32[1,1,12]{2,1,0:T(1,128)} %param.10) | copy-start | bytes 148
  4.1 11.2 %copy-start.4 = (s32[1,1,12]{2,1,0:T(1,128)S(1)}, s32[1,1,12]{2,1,0:T(1,128)}, u32[]{:S(2)}) copy-start(s32[1,1,12]{2,1,0:T(1,128)} %param.11) | copy-start | bytes 148
  4.1 104.7 %copy-start.2 = (bf16[1,1,12,128,128]{4,3,2,1,0:T(8,128)(2,1)S(1)}, bf16[1,1,12,128,128]{4,3,2,1,0:T(8,128)(2,1)}, u32[]{:S(2)}) copy-start(bf16[1,1,12,128,128]{4,3,2,1,0:T(8,128)(2,1)} %param.9) | copy-start | bytes 1179652
  4.1 104.7 %all-to-all-start = ((bf16[32,128,512]{2,1,0:T(8,128)(2,1)}), bf16[32,128,512]{2,1,0:T(8,128)(2,1)}, u32[]{:S(2)}, u32[]{:S(2)}) async-start(bf16[32,128,512]{2,1,0:T(8,128)(2,1)} %broadcast_in_dim.10), calls=%async_computation | async-start | bytes 8388608 | tf_op jit(solution)/shard_map/all_to_all | solution.py:150
  117.4 57.1 %all-to-all-start.1 = ((bf16[16,128,512]{2,1,0:T(8,128)(2,1)}), bf16[16,128,512]{2,1,0:T(8,128)(2,1)S(1)}, u32[]{:S(2)}, u32[]{:S(2)}) async-start(bf16[16,128,512]{2,1,0:T(8,128)(2,1)} %shard_map.111), calls=%async_computation.1 | async-start | bytes 4194304 | tf_op jit(solution)/shard_map/all_to_all | solution.py:157
  128.1 46.9 %copy-start.5 = (bf16[128,512]{1,0:T(8,128)(2,1)S(1)}, bf16[128,512]{1,0:T(8,128)(2,1)}, u32[]{:S(2)}) copy-start(bf16[128,512]{1,0:T(8,128)(2,1)} %param.15) | copy-start | bytes 393220
  128.1 46.9 %copy-start.6 = (f32[512]{0:T(512)S(1)}, f32[512]{0:T(512)}, u32[]{:S(2)}) copy-start(f32[512]{0:T(512)} %param.14) | copy-start | bytes 6148
  177.7 65.1 %all-to-all-start.2 = ((f32[32,16,640]{2,1,0:T(8,128)}), f32[32,16,640]{2,1,0:T(8,128)S(1)}, u32[]{:S(2)}, u32[]{:S(2)}) async-start(f32[32,16,640]{2,1,0:T(8,128)} %maximum_maximum_fusion), calls=%async_computation.2 | async-start | bytes 2621440 | tf_op jit(solution)/shard_map/all_to_all | solution.py:157
  243.5 17.5 %all-to-all-start.3 = ((f32[16,1,640]{2,1,0:T(1,128)}), f32[16,1,640]{2,1,0:T(1,128)S(1)}, u32[]{:S(2)}, u32[]{:S(2)}) async-start(f32[16,1,640]{2,1,0:T(1,128)} %reshape.49), calls=%async_computation.3 | async-start | bytes 81920 | tf_op jit(solution)/shard_map/all_to_all | solution.py:157
  254.2 1.6 copy-start.1
  278.4 130.4 %all-to-all-start.5 = ((f32[16,1,32,640]{3,2,1,0:T(8,128)}), f32[16,1,32,640]{3,2,1,0:T(8,128)S(1)}, u32[]{:S(2)}, u32[]{:S(2)}) async-start(f32[16,1,32,640]{3,2,1,0:T(8,128)} %broadcast_in_dim.28), calls=%async_computation.5 | async-start | bytes 2621440 | tf_op jit(solution)/shard_map/all_to_all | solution.py:150

commit v4 on v3

--- a/solution.py
+++ b/solution.py
@@ -58,6 +58,73 @@
 
     lax.fori_loop(1, n, finish, 0)
     own.wait()
+
+
+def _steps_kernel(axis, other, n, lo, hi, src_ref, out_ref, send_sem, recv_sem, own_sem):
+    me = lax.axis_index(axis)
+    there = lax.axis_index(other)
+    first = max(lo, 1)
+
+    def device(k):
+        return (k, there) if axis == "row" else (there, k)
+
+    def copy(step, peer, piece):
+        return pltpu.make_async_remote_copy(
+            src_ref=src_ref.at[piece], dst_ref=out_ref.at[step - lo], send_sem=send_sem.at[step - lo],
+            recv_sem=recv_sem.at[step - lo], device_id=device(peer), device_id_type=MESH_ID,
+        )
+
+    barrier = pltpu.get_barrier_semaphore()
+
+    def greet(step, carry):
+        for peer in (lax.rem(me + step, n), lax.rem(me + n - step, n)):
+            pl.semaphore_signal(barrier, inc=1, device_id=device(peer), device_id_type=MESH_ID)
+        return carry
+
+    lax.fori_loop(first, hi, greet, 0)
+    pl.semaphore_wait(barrier, 2 * (hi - first))
+    if lo == 0:
+        own = pltpu.make_async_copy(src_ref.at[me], out_ref.at[0], own_sem)
+        own.start()
+
+    def send(step, carry):
+        peer = lax.rem(me + step, n)
+        copy(step, peer, peer).start()
+        return carry
+
+    lax.fori_loop(first, hi, send, 0)
+
+    def finish(step, carry):
+        peer = lax.rem(me + step, n)
+        copy(step, peer, peer).wait_send()
+        source = lax.rem(me + n - step, n)
+        copy(step, source, me).wait_recv()
+        return carry
+
+    lax.fori_loop(first, hi, finish, 0)
+    if lo == 0:
+        own.wait()
+
+
+def exchange_steps(pieces, axis, lo, hi, ident):
+    n = lax.axis_size(axis)
+    other = "col" if axis == "row" else "row"
+    shape = (hi - lo,) + pieces.shape[1:]
+    return pl.pallas_call(
+        functools.partial(_steps_kernel, axis, other, n, lo, hi),
+        out_shape=jax.ShapeDtypeStruct(shape, pieces.dtype),
+        in_specs=[pl.BlockSpec(memory_space=pl.ANY)],
+        out_specs=pl.BlockSpec(memory_space=pl.ANY),
+        scratch_shapes=[
+            pltpu.SemaphoreType.DMA((hi - lo,)),
+            pltpu.SemaphoreType.DMA((hi - lo,)),
+            pltpu.SemaphoreType.DMA(()),
+        ],
+        compiler_params=pltpu.CompilerParams(collective_id=ident, has_side_effects=True),
+        cost_estimate=pl.CostEstimate(
+            flops=0, transcendentals=0, bytes_accessed=2 * (hi - lo) * pieces[0].size * pieces.dtype.itemsize
+        ),
+    )(pieces)
 
 
 def exchange(x, axis, broadcast, ident):
@@ -194,7 +261,9 @@
     partial_value = slot_product(
         tile_values, tile_rows, tile_cols, live_count, gathered, row_len, False
     )
-    aggregate = scatter_sum(partial_value.astype(jnp.bfloat16), "col").astype(jnp.bfloat16)
+    pieces = partial_value.reshape(lax.axis_size("col"), own_nodes, width)
+    received = exchange_steps(pieces, "col", 0, lax.axis_size("col"), 2)
+    aggregate = jnp.sum(received.astype(jnp.float32), axis=0).astype(jnp.bfloat16)
     preact = jnp.dot(aggregate, weight, preferred_element_type=jnp.float32) + bias
     hidden = jax.nn.silu(preact).astype(jnp.bfloat16)
     sigma = jax.nn.sigmoid(preact)
@@ -214,10 +283,13 @@
     back_low = back.astype(jnp.bfloat16).reshape(col_len // own_nodes, own_nodes, width)
     back_low, reduced = lax.optimization_barrier((back_low, reduced))
     row_part = gather_rows(reduced, "row")
-    back_low, row_part = lax.optimization_barrier((back_low, row_part))
-    received = exchange(back_low, "row", False, 1)
+    half = lax.axis_size("row") // 2
+    first_half = exchange_steps(back_low, "row", 0, half, 1)
+    first_half, row_part, back_low = lax.optimization_barrier((first_half, row_part, back_low))
     every = gather_rows(row_part[None], "col")
-    feature_grad = source_total(received)
+    second_half = exchange_steps(back_low, "row", half, lax.axis_size("row"), 3)
+    every_piece = jnp.concatenate([first_half, second_half], axis=0)
+    feature_grad = jnp.sum(every_piece.astype(jnp.float32), axis=0).astype(jnp.bfloat16)
     weight_grad, bias_grad = unpack_grads(every, width)
     return (hidden, weight_grad, bias_grad, feature_grad)
 

time: 412 us -> 483 us (1.17)
  the two profiles are of different devices: /device:TPU:87 before, /device:TPU:7 now
where the time goes in v4:
time: 483 us; the launch traced here: 482 us
  Pallas kernels  317 us (66%)
  waiting for transfers between devices  93.2 us (19%)
  starting transfers between devices  48.3 us (10%)
  local copies, waits for them, and re-layouts  13.3 us (3%)
  other arithmetic  6.16 us (1%)
    pallas_call x3, Pallas kernels, exchange_steps(): pl.pallas_call(functools.partial(_steps_kernel, axis, other, n, lo, hi),...  249 us
    all_to_all x3, waiting for transfers between devices, gather_rows(): lax.all_to_all(stacked, axis, split_axis=0, concat_axis=0, tiled=True)  93.2 us
    pallas_call x1, Pallas kernels, exchange(): pl.pallas_call(functools.partial(_exchange_kernel, axis, other, n, broadc...  54.6 us
    all_to_all x3, starting transfers between devices, gather_rows(): lax.all_to_all(stacked, axis, split_axis=0, concat_axis=0, tiled=True)  27.2 us
    all_to_all x2, starting transfers between devices, scatter_sum(): lax.all_to_all(pieces, axis, split_axis=0, concat_axis=0, tiled=True)  21.2 us
    pallas_call x2, Pallas kernels, slot_product(): pl.pallas_call(functools.partial(_slot_kernel, backward, slots), out_shap...  13.1 us
  transfers between devices with their start and end apart: 5, of which 1 were waited for; matrix products, arithmetic and copies ran while one was open for 1% of the time, Pallas kernels for 52%

profile of v4, /device:TPU:7, one launch (start us, length us, event | category | flops | bytes accessed | tf_op | source)
XLA Modules:
  0.0 481.8 jit_solution(16189015348794110858)
XLA Ops:
  0.6 0.0 copy-start
  0.6 3.4 broadcast_in_dim.10
  4.1 10.7 %all-to-all-start = ((bf16[32,128,512]{2,1,0:T(8,128)(2,1)}), bf16[32,128,512]{2,1,0:T(8,128)(2,1)}, u32[]{:S(2)}, u32[]{:S(2)}) async-start(bf16[32,128,512]{2,1,0:T(8,128)(2,1)} %broadcast_in_dim.10), calls=%async_computation | async-start | bytes 8388608 | tf_op jit(solution)/shard_map/all_to_all | solution.py:217
  15.4 0.1 pad.2.clone
  15.5 0.0 copy-done.5
  15.5 0.0 copy-done.6
  15.5 93.2 %all-to-all-done.src_ref = bf16[32,128,512]{2,1,0:T(8,128)(2,1)} async-done(((bf16[32,128,512]{2,1,0:T(8,128)(2,1)}), bf16[32,128,512]{2,1,0:T(8,128)(2,1)}, u32[]{:S(2)}, u32[]{:S(2)}) %all-to-all-start) | async-done | bytes 4194336 | tf_op jit(solution)/shard_map/all_to_all | solution.py:217
  108.7 0.0 copy-done.3
  108.7 7.5 %shard_map.111.src_ref = bf16[16,128,512]{2,1,0:T(8,128)(2,1)S(1)} custom-call(s32[12]{0:T(128)S(1)} %get-tuple-element.22.src_ids.tgt_ids, s32[12]{0:T(128)S(1)} %get-tuple-element.21.tgt_ids.src_ids, s32[1]{0:T(128)} %bitcast.26.count_ref, bf16[12,128,128]{2,1,0:T(8,128)(2,1)S(1)} %bitcast.28, bf16[32,128,512]{2,1,0:T(8,128)(2,1)} %all-to-all-done.src_ref), custom_call_target="tpu_custom_call" | custom-call | flops 201326592 | bytes 4063232 | tf_op jit(solution)/shard_map/pallas_call | solution.py:198
  116.2 0.0 copy-start.2
  116.2 1.3 copy-done.2
  117.6 58.5 %shard_map.112 = bf16[16,128,512]{2,1,0:T(8,128)(2,1)} custom-call(bf16[16,128,512]{2,1,0:T(8,128)(2,1)} %copy-done.2), custom_call_target="tpu_custom_call" | custom-call | bytes 4194304 | tf_op jit(solution)/shard_map/pallas_call | solution.py:113
  176.1 0.0 copy-start.7
  176.1 0.0 copy-start.8
  176.1 1.9 reduce_sum.61
  178.0 0.1 copy.15
  178.1 0.0 copy-done
  178.1 0.0 copy-done.7
  178.2 0.0 copy-done.8
  178.2 1.0 fusion.4
  179.2 0.2 concatenate.9
  179.4 0.3 fusion
  179.7 1.2 maximum_maximum_fusion
  180.9 8.3 %all-to-all-start.1 = ((f32[32,16,640]{2,1,0:T(8,128)}), f32[32,16,640]{2,1,0:T(8,128)S(1)}, u32[]{:S(2)}, u32[]{:S(2)}) async-start(f32[32,16,640]{2,1,0:T(8,128)} %maximum_maximum_fusion), calls=%async_computation.1 | async-start | bytes 2621440 | tf_op jit(solution)/shard_map/all_to_all | solution.py:224
  189.2 1.0 convolution_convert_fusion.src_ref
  190.2 54.6 %shard_map.113 = bf16[16,128,512]{2,1,0:T(8,128)(2,1)} custom-call(bf16[128,512]{1,0:T(8,128)(2,1)} %convolution_convert_fusion.src_ref), custom_call_target="tpu_custom_call" | custom-call | bytes 4194304 | tf_op jit(solution)/shard_map/pallas_call | solution.py:134
  244.8 0.0 all-to-all-done.1
  244.8 0.1 reduce_sum.63
  244.9 0.6 reshape.49
  245.5 12.8 %all-to-all-start.2 = ((f32[16,1,640]{2,1,0:T(1,128)}), f32[16,1,640]{2,1,0:T(1,128)S(1)}, u32[]{:S(2)}, u32[]{:S(2)}) async-start(f32[16,1,640]{2,1,0:T(1,128)} %reshape.49), calls=%async_computation.2 | async-start | bytes 81920 | tf_op jit(solution)/shard_map/all_to_all | solution.py:224
  258.4 1.6 copy-done.1
  260.0 5.6 %shard_map.114.src_ref = bf16[32,128,512]{2,1,0:T(8,128)(2,1)} custom-call(s32[12]{0:T(128)S(1)} %get-tuple-element.21.tgt_ids.src_ids, s32[12]{0:T(128)S(1)} %get-tuple-element.22.src_ids.tgt_ids, s32[1]{0:T(128)} %bitcast.27.count_ref, bf16[12,128,128]{2,1,0:T(8,128)(2,1)S(1)} %bitcast.29, bf16[16,128,512]{2,1,0:T(8,128)(2,1)S(1)} %copy-done.1), custom_call_target="tpu_custom_call" | custom-call | flops 201326592 | bytes 6160384 | tf_op jit(solution)/shard_map/pallas_call | solution.py:198
  265.6 0.0 all-to-all-done.2
  265.7 0.7 broadcast_in_dim.13
  266.3 9.8 %all-to-all-start.3 = ((f32[32,1,640]{2,1,0:T(1,128)}), f32[32,1,640]{2,1,0:T(1,128)S(1)}, u32[]{:S(2)}, u32[]{:S(2)}) async-start(f32[32,1,640]{2,1,0:T(1,128)} %broadcast_in_dim.13), calls=%async_computation.3 | async-start | bytes 163840 | tf_op jit(solution)/shard_map/all_to_all | solution.py:217
  276.2 91.8 %shard_map.115 = bf16[16,128,512]{2,1,0:T(8,128)(2,1)} custom-call(bf16[32,128,512]{2,1,0:T(8,128)(2,1)} %shard_map.114.src_ref), custom_call_target="tpu_custom_call" | custom-call | bytes 4194304 | tf_op jit(solution)/shard_map/pallas_call | solution.py:113
  367.9 0.0 all-to-all-done.3
  368.0 1.3 broadcast_in_dim.28
  369.3 6.6 %all-to-all-start.4 = ((f32[16,1,32,640]{3,2,1,0:T(8,128)}), f32[16,1,32,640]{3,2,1,0:T(8,128)}, u32[]{:S(2)}, u32[]{:S(2)}) async-start(f32[16,1,32,640]{3,2,1,0:T(8,128)} %broadcast_in_dim.28), calls=%async_computation.4 | async-start | bytes 2621440 | tf_op jit(solution)/shard_map/all_to_all | solution.py:217
  375.9 0.0 copy-done.4
  375.9 0.3 reduce_sum.66
  376.2 99.1 %shard_map.116 = bf16[16,128,512]{2,1,0:T(8,128)(2,1)} custom-call(bf16[32,128,512]{2,1,0:T(8,128)(2,1)} %shard_map.114.src_ref), custom_call_target="tpu_custom_call" | custom-call | bytes 4194304 | tf_op jit(solution)/shard_map/pallas_call | solution.py:113
  475.3 1.9 reduce_sum.67
  477.2 0.7 reduce_sum.68
  477.9 0.0 all-to-all-done.4
  477.9 2.1 copy.17
  479.9 0.7 slice_reduce_fusion
  480.7 1.1 slice.8
  (11 shorter events, 0.1 us)
Async XLA Ops:
  0.6 177.5 %copy-start = (bf16[512,512]{1,0:T(8,128)(2,1)S(1)}, bf16[512,512]{1,0:T(8,128)(2,1)}, u32[]{:S(2)}) copy-start(bf16[512,512]{1,0:T(8,128)(2,1)} %param.13) | copy-start | bytes 1572868
  4.0 11.5 %copy-start.5 = (s32[1,1,12]{2,1,0:T(1,128)S(1)}, s32[1,1,12]{2,1,0:T(1,128)}, u32[]{:S(2)}) copy-start(s32[1,1,12]{2,1,0:T(1,128)} %param.10) | copy-start | bytes 148
  4.1 11.5 %copy-start.6 = (s32[1,1,12]{2,1,0:T(1,128)S(1)}, s32[1,1,12]{2,1,0:T(1,128)}, u32[]{:S(2)}) copy-start(s32[1,1,12]{2,1,0:T(1,128)} %param.11) | copy-start | bytes 148
  4.1 104.7 %copy-start.3 = (bf16[1,1,12,128,128]{4,3,2,1,0:T(8,128)(2,1)S(1)}, bf16[1,1,12,128,128]{4,3,2,1,0:T(8,128)(2,1)}, u32[]{:S(2)}) copy-start(bf16[1,1,12,128,128]{4,3,2,1,0:T(8,128)(2,1)} %param.9) | copy-start | bytes 1179652
  4.1 104.7 %all-to-all-start = ((bf16[32,128,512]{2,1,0:T(8,128)(2,1)}), bf16[32,128,512]{2,1,0:T(8,128)(2,1)}, u32[]{:S(2)}, u32[]{:S(2)}) async-start(bf16[32,128,512]{2,1,0:T(8,128)(2,1)} %broadcast_in_dim.10), calls=%async_computation | async-start | bytes 8388608 | tf_op jit(solution)/shard_map/all_to_all | solution.py:217
  116.2 1.4 copy-start.2
  176.1 2.1 copy-start.7
  176.1 2.1 copy-start.8
  180.9 63.9 %all-to-all-start.1 = ((f32[32,16,640]{2,1,0:T(8,128)}), f32[32,16,640]{2,1,0:T(8,128)S(1)}, u32[]{:S(2)}, u32[]{:S(2)}) async-start(f32[32,16,640]{2,1,0:T(8,128)} %maximum_maximum_fusion), calls=%async_computation.1 | async-start | bytes 2621440 | tf_op jit(solution)/shard_map/all_to_all | solution.py:224
  245.5 20.0 %all-to-all-start.2 = ((f32[16,1,640]{2,1,0:T(1,128)}), f32[16,1,640]{2,1,0:T(1,128)S(1)}, u32[]{:S(2)}, u32[]{:S(2)}) async-start(f32[16,1,640]{2,1,0:T(1,128)} %reshape.49), calls=%async_computation.2 | async-start | bytes 81920 | tf_op jit(solution)/shard_map/all_to_all | solution.py:224
  258.4 1.6 copy-start.1
  266.3 101.6 %all-to-all-start.3 = ((f32[32,1,640]{2,1,0:T(1,128)}), f32[32,1,640]{2,1,0:T(1,128)S(1)}, u32[]{:S(2)}, u32[]{:S(2)}) async-start(f32[32,1,640]{2,1,0:T(1,128)} %broadcast_in_dim.13), calls=%async_computation.3 | async-start | bytes 163840 | tf_op jit(solution)/shard_map/all_to_all | solution.py:217
  369.3 6.6 %copy-start.4 = (bf16[16,128,512]{2,1,0:T(8,128)(2,1)S(1)}, bf16[16,128,512]{2,1,0:T(8,128)(2,1)}, u32[]{:S(2)}) copy-start(bf16[16,128,512]{2,1,0:T(8,128)(2,1)} %shard_map.115) | copy-start | bytes 6291460
  369.3 108.6 %all-to-all-start.4 = ((f32[16,1,32,640]{3,2,1,0:T(8,128)}), f32[16,1,32,640]{3,2,1,0:T(8,128)}, u32[]{:S(2)}, u32[]{:S(2)}) async-start(f32[16,1,32,640]{3,2,1,0:T(8,128)} %broadcast_in_dim.28), calls=%async_computation.4 | async-start | bytes 2621440 | tf_op jit(solution)/shard_map/all_to_all | solution.py:217

commit v5 on v4

--- a/solution.py
+++ b/solution.py
@@ -60,69 +60,72 @@
     own.wait()
 
 
-def _steps_kernel(axis, other, n, lo, hi, src_ref, out_ref, send_sem, recv_sem, own_sem):
+def _steps_kernel(axis, other, n, first, stride, count, src_ref, out_ref, send_sem, recv_sem, own_sem):
     me = lax.axis_index(axis)
     there = lax.axis_index(other)
-    first = max(lo, 1)
+    begin = 1 if first == 0 else 0
 
     def device(k):
         return (k, there) if axis == "row" else (there, k)
 
-    def copy(step, peer, piece):
+    def copy(slot, peer, piece):
         return pltpu.make_async_remote_copy(
-            src_ref=src_ref.at[piece], dst_ref=out_ref.at[step - lo], send_sem=send_sem.at[step - lo],
-            recv_sem=recv_sem.at[step - lo], device_id=device(peer), device_id_type=MESH_ID,
+            src_ref=src_ref.at[piece], dst_ref=out_ref.at[slot], send_sem=send_sem.at[slot],
+            recv_sem=recv_sem.at[slot], device_id=device(peer), device_id_type=MESH_ID,
         )
 
     barrier = pltpu.get_barrier_semaphore()
 
-    def greet(step, carry):
+    def greet(slot, carry):
+        step = first + stride * slot
         for peer in (lax.rem(me + step, n), lax.rem(me + n - step, n)):
             pl.semaphore_signal(barrier, inc=1, device_id=device(peer), device_id_type=MESH_ID)
         return carry
 
-    lax.fori_loop(first, hi, greet, 0)
-    pl.semaphore_wait(barrier, 2 * (hi - first))
-    if lo == 0:
+    lax.fori_loop(begin, count, greet, 0)
+    pl.semaphore_wait(barrier, 2 * (count - begin))
+    if first == 0:
         own = pltpu.make_async_copy(src_ref.at[me], out_ref.at[0], own_sem)
         own.start()
 
-    def send(step, carry):
+    def send(slot, carry):
+        peer = lax.rem(me + first + stride * slot, n)
+        copy(slot, peer, peer).start()
+        return carry
+
+    lax.fori_loop(begin, count, send, 0)
+
+    def finish(slot, carry):
+        step = first + stride * slot
         peer = lax.rem(me + step, n)
-        copy(step, peer, peer).start()
-        return carry
-
-    lax.fori_loop(first, hi, send, 0)
-
-    def finish(step, carry):
-        peer = lax.rem(me + step, n)
-        copy(step, peer, peer).wait_send()
+        copy(slot, peer, peer).wait_send()
         source = lax.rem(me + n - step, n)
-        copy(step, source, me).wait_recv()
-        return carry
-
-    lax.fori_loop(first, hi, finish, 0)
-    if lo == 0:
+        copy(slot, source, me).wait_recv()
+        return carry
+
+    lax.fori_loop(begin, count, finish, 0)
+    if first == 0:
         own.wait()
 
 
-def exchange_steps(pieces, axis, lo, hi, ident):
+def exchange_steps(pieces, axis, first, stride, ident):
     n = lax.axis_size(axis)
+    count = (n - first + stride - 1) // stride
     other = "col" if axis == "row" else "row"
-    shape = (hi - lo,) + pieces.shape[1:]
+    shape = (count,) + pieces.shape[1:]
     return pl.pallas_call(
-        functools.partial(_steps_kernel, axis, other, n, lo, hi),
+        functools.partial(_steps_kernel, axis, other, n, first, stride, count),
         out_shape=jax.ShapeDtypeStruct(shape, pieces.dtype),
         in_specs=[pl.BlockSpec(memory_space=pl.ANY)],
         out_specs=pl.BlockSpec(memory_space=pl.ANY),
         scratch_shapes=[
-            pltpu.SemaphoreType.DMA((hi - lo,)),
-            pltpu.SemaphoreType.DMA((hi - lo,)),
+            pltpu.SemaphoreType.DMA((count,)),
+            pltpu.SemaphoreType.DMA((count,)),
             pltpu.SemaphoreType.DMA(()),
         ],
         compiler_params=pltpu.CompilerParams(collective_id=ident, has_side_effects=True),
         cost_estimate=pl.CostEstimate(
-            flops=0, transcendentals=0, bytes_accessed=2 * (hi - lo) * pieces[0].size * pieces.dtype.itemsize
+            flops=0, transcendentals=0, bytes_accessed=2 * count * pieces[0].size * pieces.dtype.itemsize
         ),
     )(pieces)
 
@@ -262,7 +265,7 @@
         tile_values, tile_rows, tile_cols, live_count, gathered, row_len, False
     )
     pieces = partial_value.reshape(lax.axis_size("col"), own_nodes, width)
-    received = exchange_steps(pieces, "col", 0, lax.axis_size("col"), 2)
+    received = exchange_steps(pieces, "col", 0, 1, 2)
     aggregate = jnp.sum(received.astype(jnp.float32), axis=0).astype(jnp.bfloat16)
     preact = jnp.dot(aggregate, weight, preferred_element_type=jnp.float32) + bias
     hidden = jax.nn.silu(preact).astype(jnp.bfloat16)
@@ -283,11 +286,10 @@
     back_low = back.astype(jnp.bfloat16).reshape(col_len // own_nodes, own_nodes, width)
     back_low, reduced = lax.optimization_barrier((back_low, reduced))
     row_part = gather_rows(reduced, "row")
-    half = lax.axis_size("row") // 2
-    first_half = exchange_steps(back_low, "row", 0, half, 1)
+    first_half = exchange_steps(back_low, "row", 1, 2, 1)
     first_half, row_part, back_low = lax.optimization_barrier((first_half, row_part, back_low))
     every = gather_rows(row_part[None], "col")
-    second_half = exchange_steps(back_low, "row", half, lax.axis_size("row"), 3)
+    second_half = exchange_steps(back_low, "row", 0, 2, 3)
     every_piece = jnp.concatenate([first_half, second_half], axis=0)
     feature_grad = jnp.sum(every_piece.astype(jnp.float32), axis=0).astype(jnp.bfloat16)
     weight_grad, bias_grad = unpack_grads(every, width)

time: 483 us -> 402 us (0.83)
  Pallas kernels: 317 us -> 238 us
    pallas_call x3, Pallas kernels: 249 us -> 169 us  [exchange_steps(): pl.pallas_call(functools.partial(_steps_kernel, axis, other, n, first, st...]
    all_to_all x2, starting transfers between devices: 21.2 us -> 15.6 us  [scatter_sum(): lax.all_to_all(pieces, axis, split_axis=0, concat_axis=0, tiled=True)]
  transfers between devices with their start and end apart: 5 -> 5, of which waited for: 1 -> 1; matrix products, arithmetic and copies ran while one was open for 1% -> 1% of each run, Pallas kernels for 52% -> 43%
where the time goes in v5:
time: 402 us; the launch traced here: 399 us
  Pallas kernels  238 us (59%)
  waiting for transfers between devices  93.2 us (23%)
  starting transfers between devices  45.2 us (11%)
  local copies, waits for them, and re-layouts  13.3 us (3%)
  other arithmetic  6.16 us (2%)
    pallas_call x3, Pallas kernels, exchange_steps(): pl.pallas_call(functools.partial(_steps_kernel, axis, other, n, first, st...  169 us
    all_to_all x3, waiting for transfers between devices, gather_rows(): lax.all_to_all(stacked, axis, split_axis=0, concat_axis=0, tiled=True)  93.2 us
    pallas_call x1, Pallas kernels, exchange(): pl.pallas_call(functools.partial(_exchange_kernel, axis, other, n, broadc...  54.7 us
    all_to_all x3, starting transfers between devices, gather_rows(): lax.all_to_all(stacked, axis, split_axis=0, concat_axis=0, tiled=True)  29.6 us
    all_to_all x2, starting transfers between devices, scatter_sum(): lax.all_to_all(pieces, axis, split_axis=0, concat_axis=0, tiled=True)  15.6 us
    pallas_call x2, Pallas kernels, slot_product(): pl.pallas_call(functools.partial(_slot_kernel, backward, slots), out_shap...  13.7 us
  transfers between devices with their start and end apart: 5, of which 1 were waited for; matrix products, arithmetic and copies ran while one was open for 1% of the time, Pallas kernels for 43%

profile of v5, /device:TPU:7, one launch (start us, length us, event | category | flops | bytes accessed | tf_op | source)
XLA Modules:
  0.0 399.2 jit_solution(13716199575091883164)
XLA Ops:
  0.6 0.0 copy-start
  0.6 3.4 broadcast_in_dim.10
  4.1 10.7 %all-to-all-start = ((bf16[32,128,512]{2,1,0:T(8,128)(2,1)}), bf16[32,128,512]{2,1,0:T(8,128)(2,1)}, u32[]{:S(2)}, u32[]{:S(2)}) async-start(bf16[32,128,512]{2,1,0:T(8,128)(2,1)} %broadcast_in_dim.10), calls=%async_computation | async-start | bytes 8388608 | tf_op jit(solution)/shard_map/all_to_all | solution.py:220
  15.4 0.1 pad.2.clone
  15.5 0.0 copy-done.5
  15.5 0.0 copy-done.6
  15.5 93.2 %all-to-all-done.src_ref = bf16[32,128,512]{2,1,0:T(8,128)(2,1)} async-done(((bf16[32,128,512]{2,1,0:T(8,128)(2,1)}), bf16[32,128,512]{2,1,0:T(8,128)(2,1)}, u32[]{:S(2)}, u32[]{:S(2)}) %all-to-all-start) | async-done | bytes 4194336 | tf_op jit(solution)/shard_map/all_to_all | solution.py:220
  108.7 0.0 copy-done.3
  108.7 7.7 %shard_map.111.src_ref = bf16[16,128,512]{2,1,0:T(8,128)(2,1)S(1)} custom-call(s32[12]{0:T(128)S(1)} %get-tuple-element.22.src_ids.tgt_ids, s32[12]{0:T(128)S(1)} %get-tuple-element.21.tgt_ids.src_ids, s32[1]{0:T(128)} %bitcast.26.count_ref, bf16[12,128,128]{2,1,0:T(8,128)(2,1)S(1)} %bitcast.28, bf16[32,128,512]{2,1,0:T(8,128)(2,1)} %all-to-all-done.src_ref), custom_call_target="tpu_custom_call" | custom-call | flops 201326592 | bytes 4063232 | tf_op jit(solution)/shard_map/pallas_call | solution.py:201
  116.4 0.0 copy-start.2
  116.4 1.3 copy-done.2
  117.8 58.6 %shard_map.112 = bf16[16,128,512]{2,1,0:T(8,128)(2,1)} custom-call(bf16[16,128,512]{2,1,0:T(8,128)(2,1)} %copy-done.2), custom_call_target="tpu_custom_call" | custom-call | bytes 4194304 | tf_op jit(solution)/shard_map/pallas_call | solution.py:116
  176.4 0.0 copy-start.7
  176.4 0.0 copy-start.8
  176.4 1.9 reduce_sum.61
  178.4 0.1 copy.15
  178.5 0.0 copy-done
  178.5 0.0 copy-done.7
  178.5 0.0 copy-done.8
  178.5 1.0 fusion.4
  179.5 0.2 concatenate.9
  179.7 0.3 fusion
  180.0 1.2 maximum_maximum_fusion
  181.2 8.1 %all-to-all-start.1 = ((f32[32,16,640]{2,1,0:T(8,128)}), f32[32,16,640]{2,1,0:T(8,128)S(1)}, u32[]{:S(2)}, u32[]{:S(2)}) async-start(f32[32,16,640]{2,1,0:T(8,128)} %maximum_maximum_fusion), calls=%async_computation.1 | async-start | bytes 2621440 | tf_op jit(solution)/shard_map/all_to_all | solution.py:227
  189.3 1.0 convolution_convert_fusion.src_ref
  190.3 54.7 %shard_map.113 = bf16[16,128,512]{2,1,0:T(8,128)(2,1)} custom-call(bf16[128,512]{1,0:T(8,128)(2,1)} %convolution_convert_fusion.src_ref), custom_call_target="tpu_custom_call" | custom-call | bytes 4194304 | tf_op jit(solution)/shard_map/pallas_call | solution.py:137
  245.0 0.0 all-to-all-done.1
  245.0 0.1 reduce_sum.63
  245.1 0.6 reshape.49
  245.7 7.5 %all-to-all-start.2 = ((f32[16,1,640]{2,1,0:T(1,128)}), f32[16,1,640]{2,1,0:T(1,128)S(1)}, u32[]{:S(2)}, u32[]{:S(2)}) async-start(f32[16,1,640]{2,1,0:T(1,128)} %reshape.49), calls=%async_computation.2 | async-start | bytes 81920 | tf_op jit(solution)/shard_map/all_to_all | solution.py:227
  253.3 1.6 copy-done.1
  254.8 6.0 %shard_map.114.src_ref = bf16[32,128,512]{2,1,0:T(8,128)(2,1)} custom-call(s32[12]{0:T(128)S(1)} %get-tuple-element.21.tgt_ids.src_ids, s32[12]{0:T(128)S(1)} %get-tuple-element.22.src_ids.tgt_ids, s32[1]{0:T(128)} %bitcast.27.count_ref, bf16[12,128,128]{2,1,0:T(8,128)(2,1)S(1)} %bitcast.29, bf16[16,128,512]{2,1,0:T(8,128)(2,1)S(1)} %copy-done.1), custom_call_target="tpu_custom_call" | custom-call | flops 201326592 | bytes 6160384 | tf_op jit(solution)/shard_map/pallas_call | solution.py:201
  260.8 0.0 all-to-all-done.2
  260.9 0.7 broadcast_in_dim.13
  261.6 11.8 %all-to-all-start.3 = ((f32[32,1,640]{2,1,0:T(1,128)}), f32[32,1,640]{2,1,0:T(1,128)S(1)}, u32[]{:S(2)}, u32[]{:S(2)}) async-start(f32[32,1,640]{2,1,0:T(1,128)} %broadcast_in_dim.13), calls=%async_computation.3 | async-start | bytes 163840 | tf_op jit(solution)/shard_map/all_to_all | solution.py:220
  273.4 55.8 %shard_map.115 = bf16[16,128,512]{2,1,0:T(8,128)(2,1)} custom-call(bf16[32,128,512]{2,1,0:T(8,128)(2,1)} %shard_map.114.src_ref), custom_call_target="tpu_custom_call" | custom-call | bytes 4194304 | tf_op jit(solution)/shard_map/pallas_call | solution.py:116
  329.3 0.0 all-to-all-done.3
  329.3 1.3 broadcast_in_dim.28
  330.6 7.1 %all-to-all-start.4 = ((f32[16,1,32,640]{3,2,1,0:T(8,128)}), f32[16,1,32,640]{3,2,1,0:T(8,128)}, u32[]{:S(2)}, u32[]{:S(2)}) async-start(f32[16,1,32,640]{3,2,1,0:T(8,128)} %broadcast_in_dim.28), calls=%async_computation.4 | async-start | bytes 2621440 | tf_op jit(solution)/shard_map/all_to_all | solution.py:220
  337.7 0.0 copy-done.4
  337.7 0.3 reduce_sum.66
  338.0 54.7 %shard_map.116 = bf16[16,128,512]{2,1,0:T(8,128)(2,1)} custom-call(bf16[32,128,512]{2,1,0:T(8,128)(2,1)} %shard_map.114.src_ref), custom_call_target="tpu_custom_call" | custom-call | bytes 4194304 | tf_op jit(solution)/shard_map/pallas_call | solution.py:116
  392.7 1.9 reduce_sum.67
  394.6 0.7 reduce_sum.68
  395.3 0.0 all-to-all-done.4
  395.3 2.1 copy.17
  397.4 0.7 slice_reduce_fusion
  398.1 1.1 slice.8
  (11 shorter events, 0.1 us)
Async XLA Ops:
  0.6 177.9 %copy-start = (bf16[512,512]{1,0:T(8,128)(2,1)S(1)}, bf16[512,512]{1,0:T(8,128)(2,1)}, u32[]{:S(2)}) copy-start(bf16[512,512]{1,0:T(8,128)(2,1)} %param.13) | copy-start | bytes 1572868
  4.0 11.5 %copy-start.5 = (s32[1,1,12]{2,1,0:T(1,128)S(1)}, s32[1,1,12]{2,1,0:T(1,128)}, u32[]{:S(2)}) copy-start(s32[1,1,12]{2,1,0:T(1,128)} %param.10) | copy-start | bytes 148
  4.1 11.5 %copy-start.6 = (s32[1,1,12]{2,1,0:T(1,128)S(1)}, s32[1,1,12]{2,1,0:T(1,128)}, u32[]{:S(2)}) copy-start(s32[1,1,12]{2,1,0:T(1,128)} %param.11) | copy-start | bytes 148
  4.1 104.7 %copy-start.3 = (bf16[1,1,12,128,128]{4,3,2,1,0:T(8,128)(2,1)S(1)}, bf16[1,1,12,128,128]{4,3,2,1,0:T(8,128)(2,1)}, u32[]{:S(2)}) copy-start(bf16[1,1,12,128,128]{4,3,2,1,0:T(8,128)(2,1)} %param.9) | copy-start | bytes 1179652
  4.1 104.7 %all-to-all-start = ((bf16[32,128,512]{2,1,0:T(8,128)(2,1)}), bf16[32,128,512]{2,1,0:T(8,128)(2,1)}, u32[]{:S(2)}, u32[]{:S(2)}) async-start(bf16[32,128,512]{2,1,0:T(8,128)(2,1)} %broadcast_in_dim.10), calls=%async_computation | async-start | bytes 8388608 | tf_op jit(solution)/shard_map/all_to_all | solution.py:220
  116.4 1.4 copy-start.2
  176.4 2.1 copy-start.7
  176.4 2.1 copy-start.8
  181.2 63.7 %all-to-all-start.1 = ((f32[32,16,640]{2,1,0:T(8,128)}), f32[32,16,640]{2,1,0:T(8,128)S(1)}, u32[]{:S(2)}, u32[]{:S(2)}) async-start(f32[32,16,640]{2,1,0:T(8,128)} %maximum_maximum_fusion), calls=%async_computation.1 | async-start | bytes 2621440 | tf_op jit(solution)/shard_map/all_to_all | solution.py:227
  245.7 15.1 %all-to-all-start.2 = ((f32[16,1,640]{2,1,0:T(1,128)}), f32[16,1,640]{2,1,0:T(1,128)S(1)}, u32[]{:S(2)}, u32[]{:S(2)}) async-start(f32[16,1,640]{2,1,0:T(1,128)} %reshape.49), calls=%async_computation.2 | async-start | bytes 81920 | tf_op jit(solution)/shard_map/all_to_all | solution.py:227
  253.3 1.6 copy-start.1
  261.6 67.7 %all-to-all-start.3 = ((f32[32,1,640]{2,1,0:T(1,128)}), f32[32,1,640]{2,1,0:T(1,128)S(1)}, u32[]{:S(2)}, u32[]{:S(2)}) async-start(f32[32,1,640]{2,1,0:T(1,128)} %broadcast_in_dim.13), calls=%async_computation.3 | async-start | bytes 163840 | tf_op jit(solution)/shard_map/all_to_all | solution.py:220
  330.6 7.1 %copy-start.4 = (bf16[16,128,512]{2,1,0:T(8,128)(2,1)S(1)}, bf16[16,128,512]{2,1,0:T(8,128)(2,1)}, u32[]{:S(2)}) copy-start(bf16[16,128,512]{2,1,0:T(8,128)(2,1)} %shard_map.115) | copy-start | bytes 6291460
  330.6 64.7 %all-to-all-start.4 = ((f32[16,1,32,640]{3,2,1,0:T(8,128)}), f32[16,1,32,640]{3,2,1,0:T(8,128)}, u32[]{:S(2)}, u32[]{:S(2)}) async-start(f32[16,1,32,640]{3,2,1,0:T(8,128)} %broadcast_in_dim.28), calls=%async_computation.4 | async-start | bytes 2621440 | tf_op jit(solution)/shard_map/all_to_all | solution.py:220

commit v6 on v5

--- a/solution.py
+++ b/solution.py
@@ -128,6 +128,117 @@
             flops=0, transcendentals=0, bytes_accessed=2 * count * pieces[0].size * pieces.dtype.itemsize
         ),
     )(pieces)
+
+
+def _steps_gather_kernel(
+    axis, other, n, m, first, stride, count, src_ref, extra_ref, out_ref, extra_out,
+    send_sem, recv_sem, own_sem, extra_send, extra_recv, extra_own,
+):
+    me = lax.axis_index(axis)
+    there = lax.axis_index(other)
+    begin = 1 if first == 0 else 0
+
+    def device(k):
+        return (k, there) if axis == "row" else (there, k)
+
+    def across(k):
+        return (me, k) if axis == "row" else (k, me)
+
+    def copy(slot, peer, piece):
+        return pltpu.make_async_remote_copy(
+            src_ref=src_ref.at[piece], dst_ref=out_ref.at[slot], send_sem=send_sem.at[slot],
+            recv_sem=recv_sem.at[slot], device_id=device(peer), device_id_type=MESH_ID,
+        )
+
+    def extra_copy(offset, peer, slot):
+        return pltpu.make_async_remote_copy(
+            src_ref=extra_ref, dst_ref=extra_out.at[slot], send_sem=extra_send.at[offset],
+            recv_sem=extra_recv.at[offset], device_id=across(peer), device_id_type=MESH_ID,
+        )
+
+    barrier = pltpu.get_barrier_semaphore()
+
+    def greet(slot, carry):
+        step = first + stride * slot
+        for peer in (lax.rem(me + step, n), lax.rem(me + n - step, n)):
+            pl.semaphore_signal(barrier, inc=1, device_id=device(peer), device_id_type=MESH_ID)
+        return carry
+
+    def greet_across(offset, carry):
+        peer = lax.rem(there + offset, m)
+        pl.semaphore_signal(barrier, inc=1, device_id=across(peer), device_id_type=MESH_ID)
+        return carry
+
+    lax.fori_loop(begin, count, greet, 0)
+    lax.fori_loop(1, m, greet_across, 0)
+    pl.semaphore_wait(barrier, 2 * (count - begin) + m - 1)
+    own_extra = pltpu.make_async_copy(extra_ref, extra_out.at[there], extra_own)
+    own_extra.start()
+    if first == 0:
+        own = pltpu.make_async_copy(src_ref.at[me], out_ref.at[0], own_sem)
+        own.start()
+
+    def send_across(offset, carry):
+        extra_copy(offset, lax.rem(there + offset, m), there).start()
+        return carry
+
+    lax.fori_loop(1, m, send_across, 0)
+
+    def send(slot, carry):
+        peer = lax.rem(me + first + stride * slot, n)
+        copy(slot, peer, peer).start()
+        return carry
+
+    lax.fori_loop(begin, count, send, 0)
+
+    def finish(slot, carry):
+        step = first + stride * slot
+        peer = lax.rem(me + step, n)
+        copy(slot, peer, peer).wait_send()
+        source = lax.rem(me + n - step, n)
+        copy(slot, source, me).wait_recv()
+        return carry
+
+    lax.fori_loop(begin, count, finish, 0)
+
+    def finish_across(offset, carry):
+        extra_copy(offset, lax.rem(there + offset, m), there).wait_send()
+        source = lax.rem(there + m - offset, m)
+        extra_copy(offset, source, source).wait_recv()
+        return carry
+
+    lax.fori_loop(1, m, finish_across, 0)
+    own_extra.wait()
+    if first == 0:
+        own.wait()
+
+
+def exchange_steps_and_gather(pieces, extra, axis, first, stride, ident):
+    n = lax.axis_size(axis)
+    other = "col" if axis == "row" else "row"
+    m = lax.axis_size(other)
+    count = (n - first + stride - 1) // stride
+    shapes = (
+        jax.ShapeDtypeStruct((count,) + pieces.shape[1:], pieces.dtype),
+        jax.ShapeDtypeStruct((m,) + extra.shape, extra.dtype),
+    )
+    moved = 2 * count * pieces[0].size * pieces.dtype.itemsize + 2 * m * extra.size * extra.dtype.itemsize
+    return pl.pallas_call(
+        functools.partial(_steps_gather_kernel, axis, other, n, m, first, stride, count),
+        out_shape=shapes,
+        in_specs=[pl.BlockSpec(memory_space=pl.ANY), pl.BlockSpec(memory_space=pl.ANY)],
+        out_specs=(pl.BlockSpec(memory_space=pl.ANY), pl.BlockSpec(memory_space=pl.ANY)),
+        scratch_shapes=[
+            pltpu.SemaphoreType.DMA((count,)),
+            pltpu.SemaphoreType.DMA((count,)),
+            pltpu.SemaphoreType.DMA(()),
+            pltpu.SemaphoreType.DMA((m,)),
+            pltpu.SemaphoreType.DMA((m,)),
+            pltpu.SemaphoreType.DMA(()),
+        ],
+        compiler_params=pltpu.CompilerParams(collective_id=ident, has_side_effects=True),
+        cost_estimate=pl.CostEstimate(flops=0, transcendentals=0, bytes_accessed=moved),
+    )(pieces, extra)
 
 
 def exchange(x, axis, broadcast, ident):
@@ -288,8 +399,7 @@
     row_part = gather_rows(reduced, "row")
     first_half = exchange_steps(back_low, "row", 1, 2, 1)
     first_half, row_part, back_low = lax.optimization_barrier((first_half, row_part, back_low))
-    every = gather_rows(row_part[None], "col")
-    second_half = exchange_steps(back_low, "row", 0, 2, 3)
+    second_half, every = exchange_steps_and_gather(back_low, row_part, "row", 0, 2, 3)
     every_piece = jnp.concatenate([first_half, second_half], axis=0)
     feature_grad = jnp.sum(every_piece.astype(jnp.float32), axis=0).astype(jnp.bfloat16)
     weight_grad, bias_grad = unpack_grads(every, width)

time: 402 us -> 401 us (level)
  the two profiles are of different devices: /device:TPU:7 before, /device:TPU:86 now
where the time goes in v6:
time: 401 us
  Pallas kernels  248 us (62%)
  waiting for transfers between devices  94 us (23%)
  starting transfers between devices  35.5 us (9%)
  local copies, waits for them, and re-layouts  12.8 us (3%)
  other arithmetic  6.31 us (2%)
    pallas_call x2, Pallas kernels, exchange_steps(): pl.pallas_call(functools.partial(_steps_kernel, axis, other, n, first, st...  114 us
    all_to_all x2, waiting for transfers between devices, gather_rows(): lax.all_to_all(stacked, axis, split_axis=0, concat_axis=0, tiled=True)  94 us
    pallas_call x1, Pallas kernels, exchange_steps_and_gather(): pl.pallas_call(functools.partial(_steps_gather_kernel, axis, other, n, m,...  64.9 us
    pallas_call x1, Pallas kernels, exchange(): pl.pallas_call(functools.partial(_exchange_kernel, axis, other, n, broadc...  57.3 us
    all_to_all x2, starting transfers between devices, scatter_sum(): lax.all_to_all(pieces, axis, split_axis=0, concat_axis=0, tiled=True)  18.6 us
    all_to_all x2, starting transfers between devices, gather_rows(): lax.all_to_all(stacked, axis, split_axis=0, concat_axis=0, tiled=True)  16.9 us
    pallas_call x2, Pallas kernels, slot_product(): pl.pallas_call(functools.partial(_slot_kernel, backward, slots), out_shap...  12.3 us
  transfers between devices with their start and end apart: 4, of which 1 were waited for; matrix products, arithmetic and copies ran while one was open for 0% of the time, Pallas kernels for 30%

profile of v6, /device:TPU:86, one launch (start us, length us, event | category | flops | bytes accessed | tf_op | source)
XLA Modules:
  0.0 400.7 jit_solution(9236237616456719918)
XLA Ops:
  0.6 0.0 copy-start
  0.6 3.4 broadcast_in_dim.8
  4.0 0.0 copy-start.5
  4.1 0.0 copy-start.6
  4.1 10.2 %all-to-all-start = ((bf16[32,128,512]{2,1,0:T(8,128)(2,1)}), bf16[32,128,512]{2,1,0:T(8,128)(2,1)}, u32[]{:S(2)}, u32[]{:S(2)}) async-start(bf16[32,128,512]{2,1,0:T(8,128)(2,1)} %broadcast_in_dim.8), calls=%async_computation | async-start | bytes 8388608 | tf_op jit(solution)/shard_map/all_to_all | solution.py:331
  14.9 0.1 pad.2.clone
  15.0 0.0 copy-done.5
  15.0 0.0 copy-done.6
  15.0 94.0 %all-to-all-done.src_ref = bf16[32,128,512]{2,1,0:T(8,128)(2,1)} async-done(((bf16[32,128,512]{2,1,0:T(8,128)(2,1)}), bf16[32,128,512]{2,1,0:T(8,128)(2,1)}, u32[]{:S(2)}, u32[]{:S(2)}) %all-to-all-start) | async-done | bytes 4194336 | tf_op jit(solution)/shard_map/all_to_all | solution.py:331
  108.9 0.0 copy-done.3
  108.9 7.3 %shard_map.111.src_ref = bf16[16,128,512]{2,1,0:T(8,128)(2,1)S(1)} custom-call(s32[12]{0:T(128)S(1)} %get-tuple-element.26.src_ids.tgt_ids, s32[12]{0:T(128)S(1)} %get-tuple-element.25.tgt_ids.src_ids, s32[1]{0:T(128)} %bitcast.23.count_ref, bf16[12,128,128]{2,1,0:T(8,128)(2,1)S(1)} %bitcast.25, bf16[32,128,512]{2,1,0:T(8,128)(2,1)} %all-to-all-done.src_ref), custom_call_target="tpu_custom_call" | custom-call | flops 201326592 | bytes 4063232 | tf_op jit(solution)/shard_map/pallas_call | solution.py:312
  116.2 0.0 copy-start.2
  116.2 1.3 copy-done.2
  117.6 57.1 %shard_map.112 = bf16[16,128,512]{2,1,0:T(8,128)(2,1)} custom-call(bf16[16,128,512]{2,1,0:T(8,128)(2,1)} %copy-done.2), custom_call_target="tpu_custom_call" | custom-call | bytes 4194304 | tf_op jit(solution)/shard_map/pallas_call | solution.py:116
  174.7 0.0 copy-start.7
  174.7 0.0 copy-start.8
  174.7 1.9 reduce_sum.61
  176.7 0.1 copy.17
  176.8 0.0 copy-done
  176.8 0.0 copy-done.7
  176.8 0.0 copy-done.8
  176.8 1.0 fusion.4
  177.8 0.2 concatenate.9
  178.0 0.3 fusion
  178.3 1.2 maximum_maximum_fusion
  179.5 7.8 %all-to-all-start.1 = ((f32[32,16,640]{2,1,0:T(8,128)}), f32[32,16,640]{2,1,0:T(8,128)S(1)}, u32[]{:S(2)}, u32[]{:S(2)}) async-start(f32[32,16,640]{2,1,0:T(8,128)} %maximum_maximum_fusion), calls=%async_computation.1 | async-start | bytes 2621440 | tf_op jit(solution)/shard_map/all_to_all | solution.py:338
  187.3 1.0 convolution_convert_fusion.src_ref
  188.3 57.3 %shard_map.113 = bf16[16,128,512]{2,1,0:T(8,128)(2,1)} custom-call(bf16[128,512]{1,0:T(8,128)(2,1)} %convolution_convert_fusion.src_ref), custom_call_target="tpu_custom_call" | custom-call | bytes 4194304 | tf_op jit(solution)/shard_map/pallas_call | solution.py:248
  245.6 0.0 all-to-all-done.1
  245.6 0.1 reduce_sum.63
  245.7 0.6 reshape.43
  246.3 10.8 %all-to-all-start.2 = ((f32[16,1,640]{2,1,0:T(1,128)}), f32[16,1,640]{2,1,0:T(1,128)S(1)}, u32[]{:S(2)}, u32[]{:S(2)}) async-start(f32[16,1,640]{2,1,0:T(1,128)} %reshape.43), calls=%async_computation.2 | async-start | bytes 81920 | tf_op jit(solution)/shard_map/all_to_all | solution.py:338
  257.1 1.6 copy-done.1
  258.7 5.0 %shard_map.114.src_ref = bf16[32,128,512]{2,1,0:T(8,128)(2,1)} custom-call(s32[12]{0:T(128)S(1)} %get-tuple-element.25.tgt_ids.src_ids, s32[12]{0:T(128)S(1)} %get-tuple-element.26.src_ids.tgt_ids, s32[1]{0:T(128)} %bitcast.24.count_ref, bf16[12,128,128]{2,1,0:T(8,128)(2,1)S(1)} %bitcast.26, bf16[16,128,512]{2,1,0:T(8,128)(2,1)S(1)} %copy-done.1), custom_call_target="tpu_custom_call" | custom-call | flops 201326592 | bytes 6160384 | tf_op jit(solution)/shard_map/pallas_call | solution.py:312
  263.7 0.0 all-to-all-done.2
  263.8 0.7 broadcast_in_dim.22
  264.4 6.8 %all-to-all-start.3 = ((f32[32,1,640]{2,1,0:T(1,128)}), f32[32,1,640]{2,1,0:T(1,128)S(1)}, u32[]{:S(2)}, u32[]{:S(2)}) async-start(f32[32,1,640]{2,1,0:T(1,128)} %broadcast_in_dim.22), calls=%async_computation.3 | async-start | bytes 163840 | tf_op jit(solution)/shard_map/all_to_all | solution.py:331
  271.2 56.8 %shard_map.115 = bf16[16,128,512]{2,1,0:T(8,128)(2,1)} custom-call(bf16[32,128,512]{2,1,0:T(8,128)(2,1)} %shard_map.114.src_ref), custom_call_target="tpu_custom_call" | custom-call | bytes 4194304 | tf_op jit(solution)/shard_map/pallas_call | solution.py:116
  328.0 0.0 all-to-all-done.3
  328.0 0.6 copy.22
  328.6 64.9 %shard_map.116 = (bf16[16,128,512]{2,1,0:T(8,128)(2,1)}, f32[16,32,640]{2,1,0:T(8,128)}) custom-call(bf16[32,128,512]{2,1,0:T(8,128)(2,1)} %shard_map.114.src_ref, f32[32,640]{1,0:T(8,128)} %bitcast.32), custom_call_target="tpu_custom_call" | custom-call | bytes 6815744 | tf_op jit(solution)/shard_map/pallas_call | solution.py:226
  393.6 2.1 copy.19
  395.7 0.7 slice_reduce_fusion
  396.4 1.1 slice.8
  397.5 2.0 reduce_sum.67
  399.6 0.2 copy-done.4
  399.7 0.3 reduce_sum.66
  400.0 0.7 reduce_sum.68
  (8 shorter events, 0.1 us)
Async XLA Ops:
  0.6 176.2 %copy-start = (bf16[512,512]{1,0:T(8,128)(2,1)S(1)}, bf16[512,512]{1,0:T(8,128)(2,1)}, u32[]{:S(2)}) copy-start(bf16[512,512]{1,0:T(8,128)(2,1)} %param.13) | copy-start | bytes 1572868
  4.0 10.9 %copy-start.5 = (s32[1,1,12]{2,1,0:T(1,128)S(1)}, s32[1,1,12]{2,1,0:T(1,128)}, u32[]{:S(2)}) copy-start(s32[1,1,12]{2,1,0:T(1,128)} %param.10) | copy-start | bytes 148
  4.1 10.9 %copy-start.6 = (s32[1,1,12]{2,1,0:T(1,128)S(1)}, s32[1,1,12]{2,1,0:T(1,128)}, u32[]{:S(2)}) copy-start(s32[1,1,12]{2,1,0:T(1,128)} %param.11) | copy-start | bytes 148
  4.1 104.9 %copy-start.3 = (bf16[1,1,12,128,128]{4,3,2,1,0:T(8,128)(2,1)S(1)}, bf16[1,1,12,128,128]{4,3,2,1,0:T(8,128)(2,1)}, u32[]{:S(2)}) copy-start(bf16[1,1,12,128,128]{4,3,2,1,0:T(8,128)(2,1)} %param.9) | copy-start | bytes 1179652
  4.1 104.9 %all-to-all-start = ((bf16[32,128,512]{2,1,0:T(8,128)(2,1)}), bf16[32,128,512]{2,1,0:T(8,128)(2,1)}, u32[]{:S(2)}, u32[]{:S(2)}) async-start(bf16[32,128,512]{2,1,0:T(8,128)(2,1)} %broadcast_in_dim.8), calls=%async_computation | async-start | bytes 8388608 | tf_op jit(solution)/shard_map/all_to_all | solution.py:331
  116.2 1.4 copy-start.2
  174.7 2.1 copy-start.7
  174.7 2.1 copy-start.8
  179.5 66.1 %all-to-all-start.1 = ((f32[32,16,640]{2,1,0:T(8,128)}), f32[32,16,640]{2,1,0:T(8,128)S(1)}, u32[]{:S(2)}, u32[]{:S(2)}) async-start(f32[32,16,640]{2,1,0:T(8,128)} %maximum_maximum_fusion), calls=%async_computation.1 | async-start | bytes 2621440 | tf_op jit(solution)/shard_map/all_to_all | solution.py:338
  246.3 17.4 %all-to-all-start.2 = ((f32[16,1,640]{2,1,0:T(1,128)}), f32[16,1,640]{2,1,0:T(1,128)S(1)}, u32[]{:S(2)}, u32[]{:S(2)}) async-start(f32[16,1,640]{2,1,0:T(1,128)} %reshape.43), calls=%async_computation.2 | async-start | bytes 81920 | tf_op jit(solution)/shard_map/all_to_all | solution.py:338
  257.1 1.6 copy-start.1
  264.4 63.5 %all-to-all-start.3 = ((f32[32,1,640]{2,1,0:T(1,128)}), f32[32,1,640]{2,1,0:T(1,128)S(1)}, u32[]{:S(2)}, u32[]{:S(2)}) async-start(f32[32,1,640]{2,1,0:T(1,128)} %broadcast_in_dim.22), calls=%async_computation.3 | async-start | bytes 163840 | tf_op jit(solution)/shard_map/all_to_all | solution.py:331
  397.5 2.2 copy-start.4

commit v7 on v5

--- a/solution.py
+++ b/solution.py
@@ -259,7 +259,7 @@
     own_nodes = features.shape[0]
     width = features.shape[1]
     row_len = lax.axis_size("col") * own_nodes
-    gathered = gather_rows(features, "row")
+    gathered = exchange(features, "row", True, 4).reshape(-1, width)
     col_len = gathered.shape[0]
     partial_value = slot_product(
         tile_values, tile_rows, tile_cols, live_count, gathered, row_len, False

time: 402 us -> 404 us (level)
  Pallas kernels: 238 us -> 340 us
  waiting for transfers between devices: 93.2 us -> 0.01 us
    pallas_call x1 -> x2, Pallas kernels: 54.7 us -> 159 us  [exchange(): pl.pallas_call(functools.partial(_exchange_kernel, axis, other, n, broadc...]
    all_to_all x3 -> x2, waiting for transfers between devices: 93.2 us -> 0.01 us  [gather_rows(): lax.all_to_all(stacked, axis, split_axis=0, concat_axis=0, tiled=True)]
    all_to_all x3 -> x2, starting transfers between devices: 29.6 us -> 24.4 us  [gather_rows(): lax.all_to_all(stacked, axis, split_axis=0, concat_axis=0, tiled=True)]
  transfers between devices with their start and end apart: 5 -> 4, of which waited for: 1 -> 0; matrix products, arithmetic and copies ran while one was open for 1% -> 1% of each run, Pallas kernels for 43% -> 42%
where the time goes in v7:
time: 404 us; the launch traced here: 401 us
  Pallas kernels  340 us (84%)
  starting transfers between devices  41.2 us (10%)
  local copies, waits for them, and re-layouts  9.91 us (2%)
  other arithmetic  6.17 us (2%)
    pallas_call x3, Pallas kernels, exchange_steps(): pl.pallas_call(functools.partial(_steps_kernel, axis, other, n, first, st...  168 us
    pallas_call x2, Pallas kernels, exchange(): pl.pallas_call(functools.partial(_exchange_kernel, axis, other, n, broadc...  159 us
    all_to_all x2, starting transfers between devices, gather_rows(): lax.all_to_all(stacked, axis, split_axis=0, concat_axis=0, tiled=True)  24.4 us
    all_to_all x2, starting transfers between devices, scatter_sum(): lax.all_to_all(pieces, axis, split_axis=0, concat_axis=0, tiled=True)  16.8 us
    pallas_call x2, Pallas kernels, slot_product(): pl.pallas_call(functools.partial(_slot_kernel, backward, slots), out_shap...  12.5 us
  transfers between devices with their start and end apart: 4, of which 0 were waited for; matrix products, arithmetic and copies ran while one was open for 1% of the time, Pallas kernels for 42%

profile of v7, /device:TPU:7, one launch (start us, length us, event | category | flops | bytes accessed | tf_op | source)
XLA Modules:
  0.0 401.3 jit_solution(16033224109612604035)
XLA Ops:
  0.6 0.0 copy-start
  1.4 0.0 copy-start.5
  1.4 0.0 copy-start.6
  1.4 0.0 copy-start.3
  1.4 104.4 %shard_map.111.src_ref = bf16[32,128,512]{2,1,0:T(8,128)(2,1)} custom-call(bf16[128,512]{1,0:T(8,128)(2,1)} %src_ref.1), custom_call_target="tpu_custom_call" | custom-call | bytes 8388608 | tf_op jit(solution)/shard_map/pallas_call | solution.py:137
  105.8 0.0 copy-done.5
  105.8 0.0 copy-done.6
  105.8 0.0 copy-done.3
  105.8 7.3 %shard_map.112.src_ref = bf16[16,128,512]{2,1,0:T(8,128)(2,1)S(1)} custom-call(s32[12]{0:T(128)S(1)} %get-tuple-element.22.src_ids.tgt_ids, s32[12]{0:T(128)S(1)} %get-tuple-element.21.tgt_ids.src_ids, s32[1]{0:T(128)} %bitcast.26.count_ref, bf16[12,128,128]{2,1,0:T(8,128)(2,1)S(1)} %bitcast.28, bf16[32,128,512]{2,1,0:T(8,128)(2,1)} %shard_map.111.src_ref), custom_call_target="tpu_custom_call" | custom-call | flops 201326592 | bytes 4063232 | tf_op jit(solution)/shard_map/pallas_call | solution.py:201
  113.2 0.0 copy-start.2
  113.2 1.3 copy-done.2
  114.5 57.9 %shard_map.113 = bf16[16,128,512]{2,1,0:T(8,128)(2,1)} custom-call(bf16[16,128,512]{2,1,0:T(8,128)(2,1)} %copy-done.2), custom_call_target="tpu_custom_call" | custom-call | bytes 4194304 | tf_op jit(solution)/shard_map/pallas_call | solution.py:116
  172.4 0.0 copy-start.7
  172.4 0.0 copy-start.8
  172.4 1.9 reduce_sum.61
  174.4 0.1 copy.15
  174.5 0.0 copy-done
  174.5 0.0 copy-done.7
  174.5 0.0 copy-done.8
  174.5 1.0 fusion.4
  175.5 0.2 concatenate.9
  175.7 0.1 pad.2.clone
  175.8 0.3 fusion
  176.1 1.2 maximum_maximum_fusion
  177.3 10.3 %all-to-all-start = ((f32[32,16,640]{2,1,0:T(8,128)}), f32[32,16,640]{2,1,0:T(8,128)S(1)}, u32[]{:S(2)}, u32[]{:S(2)}) async-start(f32[32,16,640]{2,1,0:T(8,128)} %maximum_maximum_fusion), calls=%async_computation | async-start | bytes 2621440 | tf_op jit(solution)/shard_map/all_to_all | solution.py:227
  187.7 1.0 convolution_convert_fusion.src_ref
  188.6 54.8 %shard_map.114 = bf16[16,128,512]{2,1,0:T(8,128)(2,1)} custom-call(bf16[128,512]{1,0:T(8,128)(2,1)} %convolution_convert_fusion.src_ref), custom_call_target="tpu_custom_call" | custom-call | bytes 4194304 | tf_op jit(solution)/shard_map/pallas_call | solution.py:137
  243.4 0.0 all-to-all-done
  243.4 0.1 reduce_sum.63
  243.5 0.6 reshape.48
  244.1 6.5 %all-to-all-start.1 = ((f32[16,1,640]{2,1,0:T(1,128)}), f32[16,1,640]{2,1,0:T(1,128)S(1)}, u32[]{:S(2)}, u32[]{:S(2)}) async-start(f32[16,1,640]{2,1,0:T(1,128)} %reshape.48), calls=%async_computation.1 | async-start | bytes 81920 | tf_op jit(solution)/shard_map/all_to_all | solution.py:227
  250.6 1.6 copy-done.1
  252.2 5.2 %shard_map.115.src_ref = bf16[32,128,512]{2,1,0:T(8,128)(2,1)} custom-call(s32[12]{0:T(128)S(1)} %get-tuple-element.21.tgt_ids.src_ids, s32[12]{0:T(128)S(1)} %get-tuple-element.22.src_ids.tgt_ids, s32[1]{0:T(128)} %bitcast.27.count_ref, bf16[12,128,128]{2,1,0:T(8,128)(2,1)S(1)} %bitcast.29, bf16[16,128,512]{2,1,0:T(8,128)(2,1)S(1)} %copy-done.1), custom_call_target="tpu_custom_call" | custom-call | flops 201326592 | bytes 6160384 | tf_op jit(solution)/shard_map/pallas_call | solution.py:201
  257.4 0.0 all-to-all-done.1
  257.5 0.7 broadcast_in_dim.20
  258.2 17.2 %all-to-all-start.2 = ((f32[32,1,640]{2,1,0:T(1,128)}), f32[32,1,640]{2,1,0:T(1,128)S(1)}, u32[]{:S(2)}, u32[]{:S(2)}) async-start(f32[32,1,640]{2,1,0:T(1,128)} %broadcast_in_dim.20), calls=%async_computation.2 | async-start | bytes 163840 | tf_op jit(solution)/shard_map/all_to_all | solution.py:220
  275.4 55.8 %shard_map.116 = bf16[16,128,512]{2,1,0:T(8,128)(2,1)} custom-call(bf16[32,128,512]{2,1,0:T(8,128)(2,1)} %shard_map.115.src_ref), custom_call_target="tpu_custom_call" | custom-call | bytes 4194304 | tf_op jit(solution)/shard_map/pallas_call | solution.py:116
  331.2 0.0 all-to-all-done.2
  331.2 1.3 broadcast_in_dim.21
  332.5 7.2 %all-to-all-start.3 = ((f32[16,1,32,640]{3,2,1,0:T(8,128)}), f32[16,1,32,640]{3,2,1,0:T(8,128)}, u32[]{:S(2)}, u32[]{:S(2)}) async-start(f32[16,1,32,640]{3,2,1,0:T(8,128)} %broadcast_in_dim.21), calls=%async_computation.3 | async-start | bytes 2621440 | tf_op jit(solution)/shard_map/all_to_all | solution.py:220
  339.7 0.3 reduce_sum.66
  340.0 54.7 %shard_map.117 = bf16[16,128,512]{2,1,0:T(8,128)(2,1)} custom-call(bf16[32,128,512]{2,1,0:T(8,128)(2,1)} %shard_map.115.src_ref), custom_call_target="tpu_custom_call" | custom-call | bytes 4194304 | tf_op jit(solution)/shard_map/pallas_call | solution.py:116
  394.8 1.9 reduce_sum.67
  396.6 0.7 reduce_sum.68
  397.3 0.0 all-to-all-done.3
  397.3 2.1 copy.17
  399.4 0.7 slice_reduce_fusion
  400.2 1.1 slice.8
  (9 shorter events, 0.1 us)
Async XLA Ops:
  0.6 173.9 %copy-start = (bf16[512,512]{1,0:T(8,128)(2,1)S(1)}, bf16[512,512]{1,0:T(8,128)(2,1)}, u32[]{:S(2)}) copy-start(bf16[512,512]{1,0:T(8,128)(2,1)} %param.13) | copy-start | bytes 1572868
  1.4 104.5 %copy-start.5 = (s32[1,1,12]{2,1,0:T(1,128)S(1)}, s32[1,1,12]{2,1,0:T(1,128)}, u32[]{:S(2)}) copy-start(s32[1,1,12]{2,1,0:T(1,128)} %param.10) | copy-start | bytes 148
  1.4 104.5 %copy-start.6 = (s32[1,1,12]{2,1,0:T(1,128)S(1)}, s32[1,1,12]{2,1,0:T(1,128)}, u32[]{:S(2)}) copy-start(s32[1,1,12]{2,1,0:T(1,128)} %param.11) | copy-start | bytes 148
  1.4 104.5 %copy-start.3 = (bf16[1,1,12,128,128]{4,3,2,1,0:T(8,128)(2,1)S(1)}, bf16[1,1,12,128,128]{4,3,2,1,0:T(8,128)(2,1)}, u32[]{:S(2)}) copy-start(bf16[1,1,12,128,128]{4,3,2,1,0:T(8,128)(2,1)} %param.9) | copy-start | bytes 1179652
  113.2 1.4 copy-start.2
  172.4 2.1 copy-start.7
  172.4 2.1 copy-start.8
  177.3 66.1 %all-to-all-start = ((f32[32,16,640]{2,1,0:T(8,128)}), f32[32,16,640]{2,1,0:T(8,128)S(1)}, u32[]{:S(2)}, u32[]{:S(2)}) async-start(f32[32,16,640]{2,1,0:T(8,128)} %maximum_maximum_fusion), calls=%async_computation | async-start | bytes 2621440 | tf_op jit(solution)/shard_map/all_to_all | solution.py:227
  244.1 13.3 %all-to-all-start.1 = ((f32[16,1,640]{2,1,0:T(1,128)}), f32[16,1,640]{2,1,0:T(1,128)S(1)}, u32[]{:S(2)}, u32[]{:S(2)}) async-start(f32[16,1,640]{2,1,0:T(1,128)} %reshape.48), calls=%async_computation.1 | async-start | bytes 81920 | tf_op jit(solution)/shard_map/all_to_all | solution.py:227
  250.6 1.6 copy-start.1
  258.2 73.0 %all-to-all-start.2 = ((f32[32,1,640]{2,1,0:T(1,128)}), f32[32,1,640]{2,1,0:T(1,128)S(1)}, u32[]{:S(2)}, u32[]{:S(2)}) async-start(f32[32,1,640]{2,1,0:T(1,128)} %broadcast_in_dim.20), calls=%async_computation.2 | async-start | bytes 163840 | tf_op jit(solution)/shard_map/all_to_all | solution.py:220
  332.5 7.2 %copy-start.4 = (bf16[16,128,512]{2,1,0:T(8,128)(2,1)S(1)}, bf16[16,128,512]{2,1,0:T(8,128)(2,1)}, u32[]{:S(2)}) copy-start(bf16[16,128,512]{2,1,0:T(8,128)(2,1)} %shard_map.116) | copy-start | bytes 6291460
  332.5 64.8 %all-to-all-start.3 = ((f32[16,1,32,640]{3,2,1,0:T(8,128)}), f32[16,1,32,640]{3,2,1,0:T(8,128)}, u32[]{:S(2)}, u32[]{:S(2)}) async-start(f32[16,1,32,640]{3,2,1,0:T(8,128)} %broadcast_in_dim.21), calls=%async_computation.3 | async-start | bytes 2621440 | tf_op jit(solution)/shard_map/all_to_all | solution.py:220

commit v8 on v7

--- a/solution.py
+++ b/solution.py
@@ -128,6 +128,107 @@
             flops=0, transcendentals=0, bytes_accessed=2 * count * pieces[0].size * pieces.dtype.itemsize
         ),
     )(pieces)
+
+
+def _gather_steps_kernel(
+    axis, other, n, m, src_ref, pieces_ref, out_ref, pieces_out,
+    send_sem, recv_sem, own_sem, piece_send, piece_recv, piece_own,
+):
+    me = lax.axis_index(axis)
+    there = lax.axis_index(other)
+
+    def device(k):
+        return (k, there) if axis == "row" else (there, k)
+
+    def across(k):
+        return (me, k) if axis == "row" else (k, me)
+
+    def gather_copy(step, peer, slot):
+        return pltpu.make_async_remote_copy(
+            src_ref=src_ref, dst_ref=out_ref.at[slot], send_sem=send_sem.at[step],
+            recv_sem=recv_sem.at[step], device_id=device(peer), device_id_type=MESH_ID,
+        )
+
+    def piece_copy(step, peer, piece):
+        return pltpu.make_async_remote_copy(
+            src_ref=pieces_ref.at[piece], dst_ref=pieces_out.at[step], send_sem=piece_send.at[step],
+            recv_sem=piece_recv.at[step], device_id=across(peer), device_id_type=MESH_ID,
+        )
+
+    barrier = pltpu.get_barrier_semaphore()
+
+    def greet(step, carry):
+        pl.semaphore_signal(barrier, inc=1, device_id=device(lax.rem(me + step, n)), device_id_type=MESH_ID)
+        return carry
+
+    def greet_across(step, carry):
+        pl.semaphore_signal(barrier, inc=1, device_id=across(lax.rem(there + step, m)), device_id_type=MESH_ID)
+        return carry
+
+    lax.fori_loop(1, n, greet, 0)
+    lax.fori_loop(1, m, greet_across, 0)
+    pl.semaphore_wait(barrier, n - 1 + m - 1)
+    own = pltpu.make_async_copy(src_ref, out_ref.at[me], own_sem)
+    own.start()
+    own_piece = pltpu.make_async_copy(pieces_ref.at[there], pieces_out.at[0], piece_own)
+    own_piece.start()
+
+    def send(step, carry):
+        gather_copy(step, lax.rem(me + step, n), me).start()
+        return carry
+
+    def send_across(step, carry):
+        peer = lax.rem(there + step, m)
+        piece_copy(step, peer, peer).start()
+        return carry
+
+    lax.fori_loop(1, m, send_across, 0)
+    lax.fori_loop(1, n, send, 0)
+
+    def finish(step, carry):
+        gather_copy(step, lax.rem(me + step, n), me).wait_send()
+        source = lax.rem(me + n - step, n)
+        gather_copy(step, source, source).wait_recv()
+        return carry
+
+    def finish_across(step, carry):
+        peer = lax.rem(there + step, m)
+        piece_copy(step, peer, peer).wait_send()
+        source = lax.rem(there + m - step, m)
+        piece_copy(step, source, there).wait_recv()
+        return carry
+
+    lax.fori_loop(1, n, finish, 0)
+    lax.fori_loop(1, m, finish_across, 0)
+    own.wait()
+    own_piece.wait()
+
+
+def gather_and_exchange(x, pieces, axis, ident):
+    n = lax.axis_size(axis)
+    other = "col" if axis == "row" else "row"
+    m = lax.axis_size(other)
+    shapes = (
+        jax.ShapeDtypeStruct((n,) + x.shape, x.dtype),
+        jax.ShapeDtypeStruct(pieces.shape, pieces.dtype),
+    )
+    moved = 2 * n * x.size * x.dtype.itemsize + 2 * pieces.size * pieces.dtype.itemsize
+    return pl.pallas_call(
+        functools.partial(_gather_steps_kernel, axis, other, n, m),
+        out_shape=shapes,
+        in_specs=[pl.BlockSpec(memory_space=pl.ANY), pl.BlockSpec(memory_space=pl.ANY)],
+        out_specs=(pl.BlockSpec(memory_space=pl.ANY), pl.BlockSpec(memory_space=pl.ANY)),
+        scratch_shapes=[
+            pltpu.SemaphoreType.DMA((n,)),
+            pltpu.SemaphoreType.DMA((n,)),
+            pltpu.SemaphoreType.DMA(()),
+            pltpu.SemaphoreType.DMA((m,)),
+            pltpu.SemaphoreType.DMA((m,)),
+            pltpu.SemaphoreType.DMA(()),
+        ],
+        compiler_params=pltpu.CompilerParams(collective_id=ident, has_side_effects=True),
+        cost_estimate=pl.CostEstimate(flops=0, transcendentals=0, bytes_accessed=moved),
+    )(x, pieces)
 
 
 def exchange(x, axis, broadcast, ident):
@@ -278,9 +379,11 @@
     local_bias = jnp.sum(grad_pre, axis=0)
     grad_agg = transposed_product(grad_low, weight)
     packed = pack_grads(local_weight, local_bias)
-    by_row = scatter_sum(packed, "row")
-    grad_panel = exchange(grad_agg, "col", True, 0).reshape(-1, width)
-    grad_panel, by_row = lax.optimization_barrier((grad_panel, by_row))
+    rows_count = lax.axis_size("row")
+    row_pieces = packed.reshape((rows_count, packed.shape[0] // rows_count) + packed.shape[1:])
+    grad_stack, by_row_pieces = gather_and_exchange(grad_agg, row_pieces, "col", 0)
+    grad_panel = grad_stack.reshape(-1, width)
+    by_row = jnp.sum(by_row_pieces, axis=0)
     reduced = scatter_sum(by_row, "col")
     back = slot_product(tile_values, tile_rows, tile_cols, live_count, grad_panel, col_len, True)
     back_low = back.astype(jnp.bfloat16).reshape(col_len // own_nodes, own_nodes, width)

time: 404 us -> 399 us (0.988)
  starting transfers between devices: 41.2 us -> 33.3 us
    pallas_call x0 -> x1, Pallas kernels: none -> 57.7 us  [gather_and_exchange(): pl.pallas_call(functools.partial(_gather_steps_kernel, axis, other, n, m)...]
    pallas_call x2 -> x1, Pallas kernels: 159 us -> 104 us  [exchange(): pl.pallas_call(functools.partial(_exchange_kernel, axis, other, n, broadc...]
    all_to_all x2, starting transfers between devices: 24.4 us -> 17.4 us  [gather_rows(): lax.all_to_all(stacked, axis, split_axis=0, concat_axis=0, tiled=True)]
    all_to_all x2 -> x1, starting transfers between devices: 16.8 us -> 15.9 us  [scatter_sum(): lax.all_to_all(pieces, axis, split_axis=0, concat_axis=0, tiled=True)]
  transfers between devices with their start and end apart: 4 -> 3, of which waited for: 0 -> 1; matrix products, arithmetic and copies ran while one was open for 1% -> 1% of each run, Pallas kernels for 42% -> 29%
where the time goes in v8:
time: 399 us; the launch traced here: 397 us
  Pallas kernels  342 us (86%)
  starting transfers between devices  33.3 us (8%)
  local copies, waits for them, and re-layouts  9.9 us (2%)
  other arithmetic  7.48 us (2%)
    pallas_call x3, Pallas kernels, exchange_steps(): pl.pallas_call(functools.partial(_steps_kernel, axis, other, n, first, st...  169 us
    pallas_call x1, Pallas kernels, exchange(): pl.pallas_call(functools.partial(_exchange_kernel, axis, other, n, broadc...  104 us
    pallas_call x1, Pallas kernels, gather_and_exchange(): pl.pallas_call(functools.partial(_gather_steps_kernel, axis, other, n, m)...  57.7 us
    all_to_all x2, starting transfers between devices, gather_rows(): lax.all_to_all(stacked, axis, split_axis=0, concat_axis=0, tiled=True)  17.4 us
    all_to_all x1, starting transfers between devices, scatter_sum(): lax.all_to_all(pieces, axis, split_axis=0, concat_axis=0, tiled=True)  15.9 us
    pallas_call x2, Pallas kernels, slot_product(): pl.pallas_call(functools.partial(_slot_kernel, backward, slots), out_shap...  10.4 us
  transfers between devices with their start and end apart: 3, of which 1 were waited for; matrix products, arithmetic and copies ran while one was open for 1% of the time, Pallas kernels for 29%

profile of v8, /device:TPU:7, one launch (start us, length us, event | category | flops | bytes accessed | tf_op | source)
XLA Modules:
  0.0 397.2 jit_solution(18415085293379037271)
XLA Ops:
  0.6 0.0 copy-start
  1.4 0.0 copy-start.5
  1.4 0.0 copy-start.6
  1.4 0.0 copy-start.3
  1.4 104.4 %shard_map.111.src_ref = bf16[32,128,512]{2,1,0:T(8,128)(2,1)} custom-call(bf16[128,512]{1,0:T(8,128)(2,1)} %src_ref.1), custom_call_target="tpu_custom_call" | custom-call | bytes 8388608 | tf_op jit(solution)/shard_map/pallas_call | solution.py:238
  105.8 0.0 copy-done.5
  105.8 0.0 copy-done.6
  105.8 0.0 copy-done.3
  105.8 6.0 %shard_map.112.src_ref = bf16[16,128,512]{2,1,0:T(8,128)(2,1)S(1)} custom-call(s32[12]{0:T(128)S(1)} %get-tuple-element.22.src_ids.tgt_ids, s32[12]{0:T(128)S(1)} %get-tuple-element.21.tgt_ids.src_ids, s32[1]{0:T(128)} %bitcast.24.count_ref, bf16[12,128,128]{2,1,0:T(8,128)(2,1)S(1)} %bitcast.26, bf16[32,128,512]{2,1,0:T(8,128)(2,1)} %shard_map.111.src_ref), custom_call_target="tpu_custom_call" | custom-call | flops 201326592 | bytes 4063232 | tf_op jit(solution)/shard_map/pallas_call | solution.py:302
  111.9 0.0 copy-start.1
  111.9 1.3 copy-done.1
  113.2 58.9 %shard_map.113 = bf16[16,128,512]{2,1,0:T(8,128)(2,1)} custom-call(bf16[16,128,512]{2,1,0:T(8,128)(2,1)} %copy-done.1), custom_call_target="tpu_custom_call" | custom-call | bytes 4194304 | tf_op jit(solution)/shard_map/pallas_call | solution.py:116
  172.2 0.0 copy-start.7
  172.2 0.0 copy-start.8
  172.2 1.9 reduce_sum.61
  174.1 0.1 copy.15
  174.3 0.0 copy-done
  174.3 0.0 copy-done.7
  174.3 0.0 copy-done.8
  174.3 1.0 fusion.4
  175.3 1.0 convolution_convert_fusion.src_ref
  176.2 0.2 concatenate.9
  176.5 0.3 fusion
  176.7 0.1 pad.2.clone
  176.8 1.2 maximum_maximum_fusion.pieces_ref
  178.0 57.7 %shard_map.114 = (bf16[16,128,512]{2,1,0:T(8,128)(2,1)}, f32[32,16,640]{2,1,0:T(8,128)}) custom-call(bf16[128,512]{1,0:T(8,128)(2,1)} %convolution_convert_fusion.src_ref, f32[32,16,640]{2,1,0:T(8,128)} %maximum_maximum_fusion.pieces_ref), custom_call_target="tpu_custom_call" | custom-call | bytes 6815744 | tf_op jit(solution)/shard_map/pallas_call | solution.py:216
  235.7 1.4 reduce_sum.63
  237.1 0.6 reshape.40
  237.7 15.9 %all-to-all-start = ((f32[16,1,640]{2,1,0:T(1,128)}), f32[16,1,640]{2,1,0:T(1,128)S(1)}, u32[]{:S(2)}, u32[]{:S(2)}) async-start(f32[16,1,640]{2,1,0:T(1,128)} %reshape.40), calls=%async_computation | async-start | bytes 81920 | tf_op jit(solution)/shard_map/all_to_all | solution.py:328
  253.7 0.0 copy-start.2
  253.7 1.6 copy-done.2
  255.3 4.4 %shard_map.115.src_ref = bf16[32,128,512]{2,1,0:T(8,128)(2,1)} custom-call(s32[12]{0:T(128)S(1)} %get-tuple-element.21.tgt_ids.src_ids, s32[12]{0:T(128)S(1)} %get-tuple-element.22.src_ids.tgt_ids, s32[1]{0:T(128)} %bitcast.25.count_ref, bf16[12,128,128]{2,1,0:T(8,128)(2,1)S(1)} %bitcast.27, bf16[16,128,512]{2,1,0:T(8,128)(2,1)S(1)} %copy-done.2), custom_call_target="tpu_custom_call" | custom-call | flops 201326592 | bytes 6160384 | tf_op jit(solution)/shard_map/pallas_call | solution.py:302
  259.7 0.7 all-to-all-done
  260.4 0.7 broadcast_in_dim.20
  261.1 9.6 %all-to-all-start.1 = ((f32[32,1,640]{2,1,0:T(1,128)}), f32[32,1,640]{2,1,0:T(1,128)S(1)}, u32[]{:S(2)}, u32[]{:S(2)}) async-start(f32[32,1,640]{2,1,0:T(1,128)} %broadcast_in_dim.20), calls=%async_computation.1 | async-start | bytes 163840 | tf_op jit(solution)/shard_map/all_to_all | solution.py:321
  270.7 55.8 %shard_map.116 = bf16[16,128,512]{2,1,0:T(8,128)(2,1)} custom-call(bf16[32,128,512]{2,1,0:T(8,128)(2,1)} %shard_map.115.src_ref), custom_call_target="tpu_custom_call" | custom-call | bytes 4194304 | tf_op jit(solution)/shard_map/pallas_call | solution.py:116
  326.6 0.0 all-to-all-done.1
  326.6 1.3 broadcast_in_dim.21
  327.9 7.8 %all-to-all-start.2 = ((f32[16,1,32,640]{3,2,1,0:T(8,128)}), f32[16,1,32,640]{3,2,1,0:T(8,128)}, u32[]{:S(2)}, u32[]{:S(2)}) async-start(f32[16,1,32,640]{3,2,1,0:T(8,128)} %broadcast_in_dim.21), calls=%async_computation.2 | async-start | bytes 2621440 | tf_op jit(solution)/shard_map/all_to_all | solution.py:321
  335.6 0.0 copy-done.4
  335.6 0.3 reduce_sum.66
  335.9 54.7 %shard_map.117 = bf16[16,128,512]{2,1,0:T(8,128)(2,1)} custom-call(bf16[32,128,512]{2,1,0:T(8,128)(2,1)} %shard_map.115.src_ref), custom_call_target="tpu_custom_call" | custom-call | bytes 4194304 | tf_op jit(solution)/shard_map/pallas_call | solution.py:116
  390.7 1.9 reduce_sum.67
  392.6 0.7 reduce_sum.68
  393.3 0.0 all-to-all-done.2
  393.3 2.1 copy.17
  395.3 0.7 slice_reduce_fusion
  396.1 1.1 slice.8
  (7 shorter events, 0.1 us)
Async XLA Ops:
  0.6 173.6 %copy-start = (bf16[512,512]{1,0:T(8,128)(2,1)S(1)}, bf16[512,512]{1,0:T(8,128)(2,1)}, u32[]{:S(2)}) copy-start(bf16[512,512]{1,0:T(8,128)(2,1)} %param.13) | copy-start | bytes 1572868
  1.4 104.5 %copy-start.5 = (s32[1,1,12]{2,1,0:T(1,128)S(1)}, s32[1,1,12]{2,1,0:T(1,128)}, u32[]{:S(2)}) copy-start(s32[1,1,12]{2,1,0:T(1,128)} %param.10) | copy-start | bytes 148
  1.4 104.5 %copy-start.6 = (s32[1,1,12]{2,1,0:T(1,128)S(1)}, s32[1,1,12]{2,1,0:T(1,128)}, u32[]{:S(2)}) copy-start(s32[1,1,12]{2,1,0:T(1,128)} %param.11) | copy-start | bytes 148
  1.4 104.5 %copy-start.3 = (bf16[1,1,12,128,128]{4,3,2,1,0:T(8,128)(2,1)S(1)}, bf16[1,1,12,128,128]{4,3,2,1,0:T(8,128)(2,1)}, u32[]{:S(2)}) copy-start(bf16[1,1,12,128,128]{4,3,2,1,0:T(8,128)(2,1)} %param.9) | copy-start | bytes 1179652
  111.9 1.4 copy-start.1
  172.2 2.1 copy-start.7
  172.2 2.1 copy-start.8
  237.7 22.6 %all-to-all-start = ((f32[16,1,640]{2,1,0:T(1,128)}), f32[16,1,640]{2,1,0:T(1,128)S(1)}, u32[]{:S(2)}, u32[]{:S(2)}) async-start(f32[16,1,640]{2,1,0:T(1,128)} %reshape.40), calls=%async_computation | async-start | bytes 81920 | tf_op jit(solution)/shard_map/all_to_all | solution.py:328
  253.7 1.6 copy-start.2
  261.1 65.5 %all-to-all-start.1 = ((f32[32,1,640]{2,1,0:T(1,128)}), f32[32,1,640]{2,1,0:T(1,128)S(1)}, u32[]{:S(2)}, u32[]{:S(2)}) async-start(f32[32,1,640]{2,1,0:T(1,128)} %broadcast_in_dim.20), calls=%async_computation.1 | async-start | bytes 163840 | tf_op jit(solution)/shard_map/all_to_all | solution.py:321
  327.9 7.8 %copy-start.4 = (bf16[16,128,512]{2,1,0:T(8,128)(2,1)S(1)}, bf16[16,128,512]{2,1,0:T(8,128)(2,1)}, u32[]{:S(2)}) copy-start(bf16[16,128,512]{2,1,0:T(8,128)(2,1)} %shard_map.116) | copy-start | bytes 6291460
  327.9 65.4 %all-to-all-start.2 = ((f32[16,1,32,640]{3,2,1,0:T(8,128)}), f32[16,1,32,640]{3,2,1,0:T(8,128)}, u32[]{:S(2)}, u32[]{:S(2)}) async-start(f32[16,1,32,640]{3,2,1,0:T(8,128)} %broadcast_in_dim.21), calls=%async_computation.2 | async-start | bytes 2621440 | tf_op jit(solution)/shard_map/all_to_all | solution.py:321

commit v9 on v8

--- a/solution.py
+++ b/solution.py
@@ -229,6 +229,134 @@
         compiler_params=pltpu.CompilerParams(collective_id=ident, has_side_effects=True),
         cost_estimate=pl.CostEstimate(flops=0, transcendentals=0, bytes_accessed=moved),
     )(x, pieces)
+
+
+def _back_kernel(
+    n, m, src_ref, w_ref, out_ref, row_buf, col_buf,
+    send_sem, recv_sem, own_sem, a_send, a_recv, a_own, b_send, b_recv, b_own,
+):
+    me = lax.axis_index("row")
+    there = lax.axis_index("col")
+
+    def along(k):
+        return (k, there)
+
+    def across(k):
+        return (me, k)
+
+    def main_copy(step, peer, piece):
+        return pltpu.make_async_remote_copy(
+            src_ref=src_ref.at[piece], dst_ref=out_ref.at[step], send_sem=send_sem.at[step],
+            recv_sem=recv_sem.at[step], device_id=along(peer), device_id_type=MESH_ID,
+        )
+
+    def row_copy(step, peer, slot):
+        return pltpu.make_async_remote_copy(
+            src_ref=w_ref, dst_ref=row_buf.at[slot], send_sem=a_send.at[step],
+            recv_sem=a_recv.at[step], device_id=along(peer), device_id_type=MESH_ID,
+        )
+
+    def col_copy(step, peer, slot):
+        return pltpu.make_async_remote_copy(
+            src_ref=row_buf, dst_ref=col_buf.at[slot], send_sem=b_send.at[step],
+            recv_sem=b_recv.at[step], device_id=across(peer), device_id_type=MESH_ID,
+        )
+
+    barrier = pltpu.get_barrier_semaphore()
+
+    def greet(step, carry):
+        pl.semaphore_signal(barrier, inc=1, device_id=along(lax.rem(me + step, n)), device_id_type=MESH_ID)
+        return carry
+
+    def greet_across(step, carry):
+        pl.semaphore_signal(barrier, inc=1, device_id=across(lax.rem(there + step, m)), device_id_type=MESH_ID)
+        return carry
+
+    lax.fori_loop(1, n, greet, 0)
+    lax.fori_loop(1, m, greet_across, 0)
+    pl.semaphore_wait(barrier, n - 1 + m - 1)
+    own = pltpu.make_async_copy(src_ref.at[me], out_ref.at[0], own_sem)
+    own.start()
+    own_row = pltpu.make_async_copy(w_ref, row_buf.at[me], a_own)
+    own_row.start()
+
+    def send_row(step, carry):
+        row_copy(step, lax.rem(me + step, n), me).start()
+        return carry
+
+    def send_main(step, carry):
+        peer = lax.rem(me + step, n)
+        main_copy(step, peer, peer).start()
+        return carry
+
+    lax.fori_loop(1, n, send_row, 0)
+    lax.fori_loop(1, n, send_main, 0)
+
+    def finish_row(step, carry):
+        row_copy(step, lax.rem(me + step, n), me).wait_send()
+        source = lax.rem(me + n - step, n)
+        row_copy(step, source, source).wait_recv()
+        return carry
+
+    lax.fori_loop(1, n, finish_row, 0)
+    own_row.wait()
+    own_col = pltpu.make_async_copy(row_buf, col_buf.at[there], b_own)
+    own_col.start()
+
+    def send_col(step, carry):
+        col_copy(step, lax.rem(there + step, m), there).start()
+        return carry
+
+    lax.fori_loop(1, m, send_col, 0)
+
+    def finish_main(step, carry):
+        peer = lax.rem(me + step, n)
+        main_copy(step, peer, peer).wait_send()
+        source = lax.rem(me + n - step, n)
+        main_copy(step, source, me).wait_recv()
+        return carry
+
+    lax.fori_loop(1, n, finish_main, 0)
+
+    def finish_col(step, carry):
+        col_copy(step, lax.rem(there + step, m), there).wait_send()
+        source = lax.rem(there + m - step, m)
+        col_copy(step, source, source).wait_recv()
+        return carry
+
+    lax.fori_loop(1, m, finish_col, 0)
+    own_col.wait()
+    own.wait()
+
+
+def back_exchange(pieces, row, ident):
+    n = lax.axis_size("row")
+    m = lax.axis_size("col")
+    shapes = (
+        jax.ShapeDtypeStruct(pieces.shape, pieces.dtype),
+        jax.ShapeDtypeStruct((n,) + row.shape, row.dtype),
+        jax.ShapeDtypeStruct((m, n) + row.shape, row.dtype),
+    )
+    moved = 2 * pieces.size * pieces.dtype.itemsize + 2 * m * n * row.size * row.dtype.itemsize
+    return pl.pallas_call(
+        functools.partial(_back_kernel, n, m),
+        out_shape=shapes,
+        in_specs=[pl.BlockSpec(memory_space=pl.ANY), pl.BlockSpec(memory_space=pl.ANY)],
+        out_specs=tuple(pl.BlockSpec(memory_space=pl.ANY) for _ in range(3)),
+        scratch_shapes=[
+            pltpu.SemaphoreType.DMA((n,)),
+            pltpu.SemaphoreType.DMA((n,)),
+            pltpu.SemaphoreType.DMA(()),
+            pltpu.SemaphoreType.DMA((n,)),
+            pltpu.SemaphoreType.DMA((n,)),
+            pltpu.SemaphoreType.DMA(()),
+            pltpu.SemaphoreType.DMA((m,)),
+            pltpu.SemaphoreType.DMA((m,)),
+            pltpu.SemaphoreType.DMA(()),
+        ],
+        compiler_params=pltpu.CompilerParams(collective_id=ident, has_side_effects=True),
+        cost_estimate=pl.CostEstimate(flops=0, transcendentals=0, bytes_accessed=moved),
+    )(pieces, row)
 
 
 def exchange(x, axis, broadcast, ident):
@@ -387,14 +515,9 @@
     reduced = scatter_sum(by_row, "col")
     back = slot_product(tile_values, tile_rows, tile_cols, live_count, grad_panel, col_len, True)
     back_low = back.astype(jnp.bfloat16).reshape(col_len // own_nodes, own_nodes, width)
-    back_low, reduced = lax.optimization_barrier((back_low, reduced))
-    row_part = gather_rows(reduced, "row")
-    first_half = exchange_steps(back_low, "row", 1, 2, 1)
-    first_half, row_part, back_low = lax.optimization_barrier((first_half, row_part, back_low))
-    every = gather_rows(row_part[None], "col")
-    second_half = exchange_steps(back_low, "row", 0, 2, 3)
-    every_piece = jnp.concatenate([first_half, second_half], axis=0)
-    feature_grad = jnp.sum(every_piece.astype(jnp.float32), axis=0).astype(jnp.bfloat16)
+    received, _, gathered_rows = back_exchange(back_low, reduced, 1)
+    every = gathered_rows.reshape(gathered_rows.shape[0], gathered_rows.shape[1], -1)
+    feature_grad = jnp.sum(received.astype(jnp.float32), axis=0).astype(jnp.bfloat16)
     weight_grad, bias_grad = unpack_grads(every, width)
     return (hidden, weight_grad, bias_grad, feature_grad)
 

time: 399 us -> 387 us (0.970)
  starting transfers between devices: 33.3 us -> 14.4 us
  Pallas kernels: 342 us -> 347 us
    pallas_call x0 -> x1, Pallas kernels: none -> 115 us  [back_exchange(): pl.pallas_call(functools.partial(_back_kernel, n, m), out_shape=shapes, i...]
    pallas_call x3 -> x1, Pallas kernels: 169 us -> 58.2 us  [exchange_steps(): pl.pallas_call(functools.partial(_steps_kernel, axis, other, n, first, st...]
    all_to_all x2 -> x0, starting transfers between devices: 17.4 us -> none  [gather_rows(): lax.all_to_all(stacked, axis, split_axis=0, concat_axis=0, tiled=True)]
  transfers between devices with their start and end apart: 3 -> 1, of which waited for: 1 -> 1; matrix products, arithmetic and copies ran while one was open for 1% -> 0% of each run, Pallas kernels for 29% -> 1%
where the time goes in v9:
time: 387 us; the launch traced here: 381 us
  Pallas kernels  347 us (90%)
  starting transfers between devices  14.4 us (4%)
  local copies, waits for them, and re-layouts  8.51 us (2%)
  other arithmetic  8.05 us (2%)
    pallas_call x1, Pallas kernels, back_exchange(): pl.pallas_call(functools.partial(_back_kernel, n, m), out_shape=shapes, i...  115 us
    pallas_call x1, Pallas kernels, exchange(): pl.pallas_call(functools.partial(_exchange_kernel, axis, other, n, broadc...  104 us
    pallas_call x1, Pallas kernels, exchange_steps(): pl.pallas_call(functools.partial(_steps_kernel, axis, other, n, first, st...  58.2 us
    pallas_call x1, Pallas kernels, gather_and_exchange(): pl.pallas_call(functools.partial(_gather_steps_kernel, axis, other, n, m)...  56.4 us
    all_to_all x1, starting transfers between devices, scatter_sum(): lax.all_to_all(pieces, axis, split_axis=0, concat_axis=0, tiled=True)  14.4 us
    pallas_call x2, Pallas kernels, slot_product(): pl.pallas_call(functools.partial(_slot_kernel, backward, slots), out_shap...  12.3 us
  transfers between devices with their start and end apart: 1, of which 1 were waited for; matrix products, arithmetic and copies ran while one was open for 0% of the time, Pallas kernels for 1%

profile of v9, /device:TPU:7, one launch (start us, length us, event | category | flops | bytes accessed | tf_op | source)
XLA Modules:
  0.0 381.4 jit_solution(2259730620957450177)
XLA Ops:
  0.6 0.0 copy-start
  1.4 0.0 copy-start.4
  1.4 0.0 copy-start.5
  1.4 0.0 copy-start.3
  1.4 104.4 %shard_map.111.src_ref = bf16[32,128,512]{2,1,0:T(8,128)(2,1)} custom-call(bf16[128,512]{1,0:T(8,128)(2,1)} %src_ref.1), custom_call_target="tpu_custom_call" | custom-call | bytes 8388608 | tf_op jit(solution)/shard_map/pallas_call | solution.py:366
  105.8 0.0 copy-done.4
  105.8 0.0 copy-done.5
  105.8 0.0 copy-done.3
  105.8 7.3 %shard_map.112.src_ref = bf16[16,128,512]{2,1,0:T(8,128)(2,1)S(1)} custom-call(s32[12]{0:T(128)S(1)} %get-tuple-element.16.src_ids.tgt_ids, s32[12]{0:T(128)S(1)} %get-tuple-element.15.tgt_ids.src_ids, s32[1]{0:T(128)} %bitcast.22.count_ref, bf16[12,128,128]{2,1,0:T(8,128)(2,1)S(1)} %bitcast.24, bf16[32,128,512]{2,1,0:T(8,128)(2,1)} %shard_map.111.src_ref), custom_call_target="tpu_custom_call" | custom-call | flops 201326592 | bytes 4063232 | tf_op jit(solution)/shard_map/pallas_call | solution.py:430
  113.2 0.0 copy-start.1
  113.2 1.3 copy-done.1
  114.5 58.2 %shard_map.113 = bf16[16,128,512]{2,1,0:T(8,128)(2,1)} custom-call(bf16[16,128,512]{2,1,0:T(8,128)(2,1)} %copy-done.1), custom_call_target="tpu_custom_call" | custom-call | bytes 4194304 | tf_op jit(solution)/shard_map/pallas_call | solution.py:116
  172.7 0.0 copy-start.6
  172.7 0.0 copy-start.7
  172.7 1.9 reduce_sum.53
  174.7 0.1 copy.17
  174.8 0.0 copy-done
  174.8 0.0 copy-done.6
  174.8 0.0 copy-done.7
  174.8 1.0 fusion.4
  175.8 1.0 convolution_convert_fusion.src_ref
  176.8 0.2 concatenate.8
  177.0 0.3 fusion
  177.3 0.1 pad.2.clone
  177.4 1.2 maximum_maximum_fusion.pieces_ref
  178.6 56.4 %shard_map.114 = (bf16[16,128,512]{2,1,0:T(8,128)(2,1)}, f32[32,16,640]{2,1,0:T(8,128)}) custom-call(bf16[128,512]{1,0:T(8,128)(2,1)} %convolution_convert_fusion.src_ref, f32[32,16,640]{2,1,0:T(8,128)} %maximum_maximum_fusion.pieces_ref), custom_call_target="tpu_custom_call" | custom-call | bytes 6815744 | tf_op jit(solution)/shard_map/pallas_call | solution.py:216
  235.0 1.4 reduce_sum.55
  236.4 0.6 reshape.31
  237.0 14.4 %all-to-all-start = ((f32[16,1,640]{2,1,0:T(1,128)}), f32[16,1,640]{2,1,0:T(1,128)S(1)}, u32[]{:S(2)}, u32[]{:S(2)}) async-start(f32[16,1,640]{2,1,0:T(1,128)} %reshape.31), calls=%async_computation | async-start | bytes 81920 | tf_op jit(solution)/shard_map/all_to_all | solution.py:456
  251.4 0.0 copy-start.2
  251.4 1.6 copy-done.2
  253.0 5.0 %shard_map.115.src_ref = bf16[32,128,512]{2,1,0:T(8,128)(2,1)} custom-call(s32[12]{0:T(128)S(1)} %get-tuple-element.15.tgt_ids.src_ids, s32[12]{0:T(128)S(1)} %get-tuple-element.16.src_ids.tgt_ids, s32[1]{0:T(128)} %bitcast.23.count_ref, bf16[12,128,128]{2,1,0:T(8,128)(2,1)S(1)} %bitcast.25, bf16[16,128,512]{2,1,0:T(8,128)(2,1)S(1)} %copy-done.2), custom_call_target="tpu_custom_call" | custom-call | flops 201326592 | bytes 6160384 | tf_op jit(solution)/shard_map/pallas_call | solution.py:430
  258.0 0.1 all-to-all-done
  258.1 0.6 reduce_sum.57.w_ref
  258.7 115.3 %shard_map.116 = (bf16[32,128,512]{2,1,0:T(8,128)(2,1)}, f32[32,1,640]{2,1,0:T(1,128)}, f32[16,32,1,640]{3,2,1,0:T(1,128)}) custom-call(bf16[32,128,512]{2,1,0:T(8,128)(2,1)} %shard_map.115.src_ref, f32[1,640]{1,0:T(1,128)} %reduce_sum.57.w_ref), custom_call_target="tpu_custom_call" | custom-call | bytes 11010048 | tf_op jit(solution)/shard_map/pallas_call | solution.py:341
  374.0 2.1 copy.21
  376.1 0.7 slice_reduce_fusion
  376.8 1.1 slice.8
  377.9 3.5 reduce_sum.58
  (3 shorter events, 0.0 us)
Async XLA Ops:
  0.6 174.2 %copy-start = (bf16[512,512]{1,0:T(8,128)(2,1)S(1)}, bf16[512,512]{1,0:T(8,128)(2,1)}, u32[]{:S(2)}) copy-start(bf16[512,512]{1,0:T(8,128)(2,1)} %param.13) | copy-start | bytes 1572868
  1.4 104.5 %copy-start.4 = (s32[1,1,12]{2,1,0:T(1,128)S(1)}, s32[1,1,12]{2,1,0:T(1,128)}, u32[]{:S(2)}) copy-start(s32[1,1,12]{2,1,0:T(1,128)} %param.10) | copy-start | bytes 148
  1.4 104.5 %copy-start.5 = (s32[1,1,12]{2,1,0:T(1,128)S(1)}, s32[1,1,12]{2,1,0:T(1,128)}, u32[]{:S(2)}) copy-start(s32[1,1,12]{2,1,0:T(1,128)} %param.11) | copy-start | bytes 148
  1.4 104.5 %copy-start.3 = (bf16[1,1,12,128,128]{4,3,2,1,0:T(8,128)(2,1)S(1)}, bf16[1,1,12,128,128]{4,3,2,1,0:T(8,128)(2,1)}, u32[]{:S(2)}) copy-start(bf16[1,1,12,128,128]{4,3,2,1,0:T(8,128)(2,1)} %param.9) | copy-start | bytes 1179652
  113.2 1.4 copy-start.1
  172.7 2.1 copy-start.6
  172.7 2.1 copy-start.7
  237.0 21.0 %all-to-all-start = ((f32[16,1,640]{2,1,0:T(1,128)}), f32[16,1,640]{2,1,0:T(1,128)S(1)}, u32[]{:S(2)}, u32[]{:S(2)}) async-start(f32[16,1,640]{2,1,0:T(1,128)} %reshape.31), calls=%async_computation | async-start | bytes 81920 | tf_op jit(solution)/shard_map/all_to_all | solution.py:456
  251.4 1.6 copy-start.2

commit v10 on v9

--- a/solution.py
+++ b/solution.py
@@ -232,8 +232,9 @@
 
 
 def _back_kernel(
-    n, m, src_ref, w_ref, out_ref, row_buf, col_buf,
+    n, m, src_ref, part_ref, out_ref, row_buf, col_buf,
     send_sem, recv_sem, own_sem, a_send, a_recv, a_own, b_send, b_recv, b_own,
+    c_send, c_recv, c_own, part_buf, w_ref,
 ):
     me = lax.axis_index("row")
     there = lax.axis_index("col")
@@ -260,6 +261,12 @@
         return pltpu.make_async_remote_copy(
             src_ref=row_buf, dst_ref=col_buf.at[slot], send_sem=b_send.at[step],
             recv_sem=b_recv.at[step], device_id=across(peer), device_id_type=MESH_ID,
+        )
+
+    def part_copy(step, peer):
+        return pltpu.make_async_remote_copy(
+            src_ref=part_ref.at[peer], dst_ref=part_buf.at[step], send_sem=c_send.at[step],
+            recv_sem=c_recv.at[step], device_id=across(peer), device_id_type=MESH_ID,
         )
 
     barrier = pltpu.get_barrier_semaphore()
@@ -277,11 +284,11 @@
     pl.semaphore_wait(barrier, n - 1 + m - 1)
     own = pltpu.make_async_copy(src_ref.at[me], out_ref.at[0], own_sem)
     own.start()
-    own_row = pltpu.make_async_copy(w_ref, row_buf.at[me], a_own)
-    own_row.start()
-
-    def send_row(step, carry):
-        row_copy(step, lax.rem(me + step, n), me).start()
+    own_part = pltpu.make_async_copy(part_ref.at[there], part_buf.at[0], c_own)
+    own_part.start()
+
+    def send_part(step, carry):
+        part_copy(step, lax.rem(there + step, m)).start()
         return carry
 
     def send_main(step, carry):
@@ -289,8 +296,25 @@
         main_copy(step, peer, peer).start()
         return carry
 
+    lax.fori_loop(1, m, send_part, 0)
+    lax.fori_loop(1, n, send_main, 0)
+
+    def finish_part(step, carry):
+        part_copy(step, lax.rem(there + step, m)).wait_send()
+        part_copy(step, lax.rem(there + m - step, m)).wait_recv()
+        return carry
+
+    lax.fori_loop(1, m, finish_part, 0)
+    own_part.wait()
+    w_ref[...] = jnp.sum(part_buf[...], axis=0)
+    own_row = pltpu.make_async_copy(w_ref, row_buf.at[me], a_own)
+    own_row.start()
+
+    def send_row(step, carry):
+        row_copy(step, lax.rem(me + step, n), me).start()
+        return carry
+
     lax.fori_loop(1, n, send_row, 0)
-    lax.fori_loop(1, n, send_main, 0)
 
     def finish_row(step, carry):
         row_copy(step, lax.rem(me + step, n), me).wait_send()
@@ -329,9 +353,10 @@
     own.wait()
 
 
-def back_exchange(pieces, row, ident):
+def back_exchange(pieces, parts, ident):
     n = lax.axis_size("row")
     m = lax.axis_size("col")
+    row = parts[0]
     shapes = (
         jax.ShapeDtypeStruct(pieces.shape, pieces.dtype),
         jax.ShapeDtypeStruct((n,) + row.shape, row.dtype),
@@ -353,10 +378,15 @@
             pltpu.SemaphoreType.DMA((m,)),
             pltpu.SemaphoreType.DMA((m,)),
             pltpu.SemaphoreType.DMA(()),
+            pltpu.SemaphoreType.DMA((m,)),
+            pltpu.SemaphoreType.DMA((m,)),
+            pltpu.SemaphoreType.DMA(()),
+            pltpu.VMEM(parts.shape, parts.dtype),
+            pltpu.VMEM(row.shape, row.dtype),
         ],
         compiler_params=pltpu.CompilerParams(collective_id=ident, has_side_effects=True),
         cost_estimate=pl.CostEstimate(flops=0, transcendentals=0, bytes_accessed=moved),
-    )(pieces, row)
+    )(pieces, parts)
 
 
 def exchange(x, axis, broadcast, ident):
@@ -512,10 +542,10 @@
     grad_stack, by_row_pieces = gather_and_exchange(grad_agg, row_pieces, "col", 0)
     grad_panel = grad_stack.reshape(-1, width)
     by_row = jnp.sum(by_row_pieces, axis=0)
-    reduced = scatter_sum(by_row, "col")
     back = slot_product(tile_values, tile_rows, tile_cols, live_count, grad_panel, col_len, True)
     back_low = back.astype(jnp.bfloat16).reshape(col_len // own_nodes, own_nodes, width)
-    received, _, gathered_rows = back_exchange(back_low, reduced, 1)
+    parts = by_row.reshape((by_row.shape[0], 1) + by_row.shape[1:])
+    received, _, gathered_rows = back_exchange(back_low, parts, 1)
     every = gathered_rows.reshape(gathered_rows.shape[0], gathered_rows.shape[1], -1)
     feature_grad = jnp.sum(received.astype(jnp.float32), axis=0).astype(jnp.bfloat16)
     weight_grad, bias_grad = unpack_grads(every, width)

time: 387 us -> 403 us (1.041)
  Pallas kernels: 347 us -> 379 us
  starting transfers between devices: 14.4 us -> 0 us
    pallas_call x1, Pallas kernels: 115 us -> 146 us  [back_exchange(): pl.pallas_call(functools.partial(_back_kernel, n, m), out_shape=shapes, i...]
    all_to_all x1 -> x0, starting transfers between devices: 14.4 us -> none  [scatter_sum(): lax.all_to_all(pieces, axis, split_axis=0, concat_axis=0, tiled=True)]
  transfers between devices with their start and end apart: 1 -> 0, of which waited for: 1 -> 0; matrix products, arithmetic and copies ran while one was open for 0% -> 0% of each run, Pallas kernels for 1% -> 0%
where the time goes in v10:
time: 403 us; the launch traced here: 399 us
  Pallas kernels  379 us (94%)
  other arithmetic  8.68 us (2%)
  local copies, waits for them, and re-layouts  7.92 us (2%)
    pallas_call x1, Pallas kernels, back_exchange(): pl.pallas_call(functools.partial(_back_kernel, n, m), out_shape=shapes, i...  146 us
    pallas_call x1, Pallas kernels, exchange(): pl.pallas_call(functools.partial(_exchange_kernel, axis, other, n, broadc...  104 us
    pallas_call x1, Pallas kernels, exchange_steps(): pl.pallas_call(functools.partial(_steps_kernel, axis, other, n, first, st...  58.2 us
    pallas_call x1, Pallas kernels, gather_and_exchange(): pl.pallas_call(functools.partial(_gather_steps_kernel, axis, other, n, m)...  57.8 us
    pallas_call x2, Pallas kernels, slot_product(): pl.pallas_call(functools.partial(_slot_kernel, backward, slots), out_shap...  12.1 us

profile of v10, /device:TPU:7, one launch (start us, length us, event | category | flops | bytes accessed | tf_op | source)
XLA Modules:
  0.0 399.3 jit_solution(514001232371423073)
XLA Ops:
  0.6 0.0 copy-start
  1.4 0.7 clamp_bitcast_fusion
  2.0 0.1 pad.2.clone
  2.1 0.0 copy-start.3
  2.1 104.4 %shard_map.111.src_ref = bf16[32,128,512]{2,1,0:T(8,128)(2,1)} custom-call(bf16[128,512]{1,0:T(8,128)(2,1)} %src_ref.1), custom_call_target="tpu_custom_call" | custom-call | bytes 8388608 | tf_op jit(solution)/shard_map/pallas_call | solution.py:396
  106.5 0.0 copy-done.3
  106.5 7.1 %shard_map.112.src_ref = bf16[16,128,512]{2,1,0:T(8,128)(2,1)S(1)} custom-call(s32[12]{0:T(128)S(1)} %get-tuple-element.16.src_ids.tgt_ids, s32[12]{0:T(128)S(1)} %get-tuple-element.15.tgt_ids.src_ids, s32[1]{0:T(128)} %bitcast.22.count_ref, bf16[12,128,128]{2,1,0:T(8,128)(2,1)S(1)} %bitcast.24, bf16[32,128,512]{2,1,0:T(8,128)(2,1)} %shard_map.111.src_ref), custom_call_target="tpu_custom_call" | custom-call | flops 201326592 | bytes 4063232 | tf_op jit(solution)/shard_map/pallas_call | solution.py:460
  113.6 0.0 copy-start.1
  113.6 1.3 copy-done.1
  115.0 58.2 %shard_map.113 = bf16[16,128,512]{2,1,0:T(8,128)(2,1)} custom-call(bf16[16,128,512]{2,1,0:T(8,128)(2,1)} %copy-done.1), custom_call_target="tpu_custom_call" | custom-call | bytes 4194304 | tf_op jit(solution)/shard_map/pallas_call | solution.py:116
  173.2 0.0 copy-start.4
  173.2 0.0 copy-start.5
  173.2 1.9 reduce_sum.42
  175.2 0.1 copy.17
  175.3 0.0 copy-done
  175.3 0.0 copy-done.4
  175.3 0.0 copy-done.5
  175.3 1.0 fusion.4
  176.3 1.0 convolution_convert_fusion.src_ref
  177.3 0.2 concatenate.8
  177.5 0.3 fusion
  177.8 1.2 maximum_maximum_fusion.pieces_ref
  179.0 57.8 %shard_map.114 = (bf16[16,128,512]{2,1,0:T(8,128)(2,1)}, f32[32,16,640]{2,1,0:T(8,128)}) custom-call(bf16[128,512]{1,0:T(8,128)(2,1)} %convolution_convert_fusion.src_ref, f32[32,16,640]{2,1,0:T(8,128)} %maximum_maximum_fusion.pieces_ref), custom_call_target="tpu_custom_call" | custom-call | bytes 6815744 | tf_op jit(solution)/shard_map/pallas_call | solution.py:216
  236.8 1.4 reduce_sum.44
  238.2 0.6 reshape.30.part_ref
  238.8 0.0 copy-start.2
  238.8 1.6 copy-done.2
  240.4 5.0 %shard_map.115.src_ref = bf16[32,128,512]{2,1,0:T(8,128)(2,1)} custom-call(s32[12]{0:T(128)S(1)} %get-tuple-element.15.tgt_ids.src_ids, s32[12]{0:T(128)S(1)} %get-tuple-element.16.src_ids.tgt_ids, s32[1]{0:T(128)} %bitcast.23.count_ref, bf16[12,128,128]{2,1,0:T(8,128)(2,1)S(1)} %bitcast.25, bf16[16,128,512]{2,1,0:T(8,128)(2,1)S(1)} %copy-done.2), custom_call_target="tpu_custom_call" | custom-call | flops 201326592 | bytes 6160384 | tf_op jit(solution)/shard_map/pallas_call | solution.py:460
  245.4 146.5 %shard_map.116 = (bf16[32,128,512]{2,1,0:T(8,128)(2,1)}, f32[32,1,640]{2,1,0:T(1,128)}, f32[16,32,1,640]{3,2,1,0:T(1,128)}) custom-call(bf16[32,128,512]{2,1,0:T(8,128)(2,1)} %shard_map.115.src_ref, f32[16,1,640]{2,1,0:T(1,128)} %reshape.30.part_ref), custom_call_target="tpu_custom_call" | custom-call | bytes 11010048 | tf_op jit(solution)/shard_map/pallas_call | solution.py:366
  391.9 2.1 copy.21
  394.0 0.7 slice_reduce_fusion
  394.7 1.1 slice.8
  395.8 3.5 reduce_sum.45
  (1 shorter events, 0.0 us)
Async XLA Ops:
  0.6 174.6 %copy-start = (bf16[512,512]{1,0:T(8,128)(2,1)S(1)}, bf16[512,512]{1,0:T(8,128)(2,1)}, u32[]{:S(2)}) copy-start(bf16[512,512]{1,0:T(8,128)(2,1)} %param.13) | copy-start | bytes 1572868
  2.1 104.4 %copy-start.3 = (bf16[1,1,12,128,128]{4,3,2,1,0:T(8,128)(2,1)S(1)}, bf16[1,1,12,128,128]{4,3,2,1,0:T(8,128)(2,1)}, u32[]{:S(2)}) copy-start(bf16[1,1,12,128,128]{4,3,2,1,0:T(8,128)(2,1)} %param.9) | copy-start | bytes 1179652
  113.6 1.4 copy-start.1
  173.2 2.1 copy-start.4
  173.2 2.1 copy-start.5
  238.8 1.6 copy-start.2

commit v11 on v10

--- a/solution.py
+++ b/solution.py
@@ -297,7 +297,6 @@
         return carry
 
     lax.fori_loop(1, m, send_part, 0)
-    lax.fori_loop(1, n, send_main, 0)
 
     def finish_part(step, carry):
         part_copy(step, lax.rem(there + step, m)).wait_send()
@@ -315,6 +314,7 @@
         return carry
 
     lax.fori_loop(1, n, send_row, 0)
+    lax.fori_loop(1, n, send_main, 0)
 
     def finish_row(step, carry):
         row_copy(step, lax.rem(me + step, n), me).wait_send()

time: 403 us -> 379 us (0.940)
  Pallas kernels: 379 us -> 354 us
    pallas_call x1, Pallas kernels: 146 us -> 121 us  [back_exchange(): pl.pallas_call(functools.partial(_back_kernel, n, m), out_shape=shapes, i...]
where the time goes in v11:
time: 379 us; the launch traced here: 375 us
  Pallas kernels  354 us (93%)
  other arithmetic  8.68 us (2%)
  local copies, waits for them, and re-layouts  7.92 us (2%)
    pallas_call x1, Pallas kernels, back_exchange(): pl.pallas_call(functools.partial(_back_kernel, n, m), out_shape=shapes, i...  121 us
    pallas_call x1, Pallas kernels, exchange(): pl.pallas_call(functools.partial(_exchange_kernel, axis, other, n, broadc...  104 us
    pallas_call x1, Pallas kernels, gather_and_exchange(): pl.pallas_call(functools.partial(_gather_steps_kernel, axis, other, n, m)...  58.5 us
    pallas_call x1, Pallas kernels, exchange_steps(): pl.pallas_call(functools.partial(_steps_kernel, axis, other, n, first, st...  58.3 us
    pallas_call x2, Pallas kernels, slot_product(): pl.pallas_call(functools.partial(_slot_kernel, backward, slots), out_shap...  11.9 us

profile of v11, /device:TPU:7, one launch (start us, length us, event | category | flops | bytes accessed | tf_op | source)
XLA Modules:
  0.0 374.5 jit_solution(10046456034210670236)
XLA Ops:
  0.6 0.0 copy-start
  1.4 0.7 clamp_bitcast_fusion
  2.0 0.1 pad.2.clone
  2.1 0.0 copy-start.3
  2.1 104.4 %shard_map.111.src_ref = bf16[32,128,512]{2,1,0:T(8,128)(2,1)} custom-call(bf16[128,512]{1,0:T(8,128)(2,1)} %src_ref.1), custom_call_target="tpu_custom_call" | custom-call | bytes 8388608 | tf_op jit(solution)/shard_map/pallas_call | solution.py:396
  106.5 0.0 copy-done.3
  106.5 7.1 %shard_map.112.src_ref = bf16[16,128,512]{2,1,0:T(8,128)(2,1)S(1)} custom-call(s32[12]{0:T(128)S(1)} %get-tuple-element.16.src_ids.tgt_ids, s32[12]{0:T(128)S(1)} %get-tuple-element.15.tgt_ids.src_ids, s32[1]{0:T(128)} %bitcast.22.count_ref, bf16[12,128,128]{2,1,0:T(8,128)(2,1)S(1)} %bitcast.24, bf16[32,128,512]{2,1,0:T(8,128)(2,1)} %shard_map.111.src_ref), custom_call_target="tpu_custom_call" | custom-call | flops 201326592 | bytes 4063232 | tf_op jit(solution)/shard_map/pallas_call | solution.py:460
  113.7 0.0 copy-start.1
  113.7 1.3 copy-done.1
  115.0 58.3 %shard_map.113 = bf16[16,128,512]{2,1,0:T(8,128)(2,1)} custom-call(bf16[16,128,512]{2,1,0:T(8,128)(2,1)} %copy-done.1), custom_call_target="tpu_custom_call" | custom-call | bytes 4194304 | tf_op jit(solution)/shard_map/pallas_call | solution.py:116
  173.4 0.0 copy-start.4
  173.4 0.0 copy-start.5
  173.4 1.9 reduce_sum.42
  175.3 0.1 copy.17
  175.4 0.0 copy-done
  175.4 0.0 copy-done.4
  175.5 0.0 copy-done.5
  175.5 1.0 fusion.4
  176.5 1.0 convolution_convert_fusion.src_ref
  177.4 0.2 concatenate.8
  177.6 0.3 fusion
  177.9 1.2 maximum_maximum_fusion.pieces_ref
  179.1 58.5 %shard_map.114 = (bf16[16,128,512]{2,1,0:T(8,128)(2,1)}, f32[32,16,640]{2,1,0:T(8,128)}) custom-call(bf16[128,512]{1,0:T(8,128)(2,1)} %convolution_convert_fusion.src_ref, f32[32,16,640]{2,1,0:T(8,128)} %maximum_maximum_fusion.pieces_ref), custom_call_target="tpu_custom_call" | custom-call | bytes 6815744 | tf_op jit(solution)/shard_map/pallas_call | solution.py:216
  237.7 1.4 reduce_sum.44
  239.1 0.6 reshape.30.part_ref
  239.7 0.0 copy-start.2
  239.7 1.6 copy-done.2
  241.3 4.8 %shard_map.115.src_ref = bf16[32,128,512]{2,1,0:T(8,128)(2,1)} custom-call(s32[12]{0:T(128)S(1)} %get-tuple-element.15.tgt_ids.src_ids, s32[12]{0:T(128)S(1)} %get-tuple-element.16.src_ids.tgt_ids, s32[1]{0:T(128)} %bitcast.23.count_ref, bf16[12,128,128]{2,1,0:T(8,128)(2,1)S(1)} %bitcast.25, bf16[16,128,512]{2,1,0:T(8,128)(2,1)S(1)} %copy-done.2), custom_call_target="tpu_custom_call" | custom-call | flops 201326592 | bytes 6160384 | tf_op jit(solution)/shard_map/pallas_call | solution.py:460
  246.1 121.0 %shard_map.116 = (bf16[32,128,512]{2,1,0:T(8,128)(2,1)}, f32[32,1,640]{2,1,0:T(1,128)}, f32[16,32,1,640]{3,2,1,0:T(1,128)}) custom-call(bf16[32,128,512]{2,1,0:T(8,128)(2,1)} %shard_map.115.src_ref, f32[16,1,640]{2,1,0:T(1,128)} %reshape.30.part_ref), custom_call_target="tpu_custom_call" | custom-call | bytes 11010048 | tf_op jit(solution)/shard_map/pallas_call | solution.py:366
  367.1 2.1 copy.21
  369.2 0.7 slice_reduce_fusion
  369.9 1.1 slice.8
  371.0 3.5 reduce_sum.45
  (1 shorter events, 0.0 us)
Async XLA Ops:
  0.6 174.8 %copy-start = (bf16[512,512]{1,0:T(8,128)(2,1)S(1)}, bf16[512,512]{1,0:T(8,128)(2,1)}, u32[]{:S(2)}) copy-start(bf16[512,512]{1,0:T(8,128)(2,1)} %param.13) | copy-start | bytes 1572868
  2.1 104.4 %copy-start.3 = (bf16[1,1,12,128,128]{4,3,2,1,0:T(8,128)(2,1)S(1)}, bf16[1,1,12,128,128]{4,3,2,1,0:T(8,128)(2,1)}, u32[]{:S(2)}) copy-start(bf16[1,1,12,128,128]{4,3,2,1,0:T(8,128)(2,1)} %param.9) | copy-start | bytes 1179652
  113.7 1.4 copy-start.1
  173.4 2.1 copy-start.4
  173.4 2.1 copy-start.5
  239.7 1.6 copy-start.2

commit v12 on v11

--- a/solution.py
+++ b/solution.py
@@ -297,6 +297,7 @@
         return carry
 
     lax.fori_loop(1, m, send_part, 0)
+    lax.fori_loop(0, n // 2, lambda i, c: send_main(1 + 2 * i, c), 0)
 
     def finish_part(step, carry):
         part_copy(step, lax.rem(there + step, m)).wait_send()
@@ -314,7 +315,7 @@
         return carry
 
     lax.fori_loop(1, n, send_row, 0)
-    lax.fori_loop(1, n, send_main, 0)
+    lax.fori_loop(1, n // 2, lambda i, c: send_main(2 * i, c), 0)
 
     def finish_row(step, carry):
         row_copy(step, lax.rem(me + step, n), me).wait_send()

time: 379 us -> 369 us (0.974)
  Pallas kernels: 354 us -> 344 us
    pallas_call x1, Pallas kernels: 121 us -> 113 us  [back_exchange(): pl.pallas_call(functools.partial(_back_kernel, n, m), out_shape=shapes, i...]
where the time goes in v12:
time: 369 us; the launch traced here: 365 us
  Pallas kernels  344 us (93%)
  other arithmetic  8.68 us (2%)
  local copies, waits for them, and re-layouts  7.92 us (2%)
    pallas_call x1, Pallas kernels, back_exchange(): pl.pallas_call(functools.partial(_back_kernel, n, m), out_shape=shapes, i...  113 us
    pallas_call x1, Pallas kernels, exchange(): pl.pallas_call(functools.partial(_exchange_kernel, axis, other, n, broadc...  104 us
    pallas_call x1, Pallas kernels, exchange_steps(): pl.pallas_call(functools.partial(_steps_kernel, axis, other, n, first, st...  58.4 us
    pallas_call x1, Pallas kernels, gather_and_exchange(): pl.pallas_call(functools.partial(_gather_steps_kernel, axis, other, n, m)...  56.6 us
    pallas_call x2, Pallas kernels, slot_product(): pl.pallas_call(functools.partial(_slot_kernel, backward, slots), out_shap...  11.9 us

profile of v12, /device:TPU:7, one launch (start us, length us, event | category | flops | bytes accessed | tf_op | source)
XLA Modules:
  0.0 364.7 jit_solution(13844593001269077503)
XLA Ops:
  0.6 0.0 copy-start
  1.4 0.7 clamp_bitcast_fusion
  2.0 0.1 pad.2.clone
  2.1 0.0 copy-start.3
  2.1 104.4 %shard_map.111.src_ref = bf16[32,128,512]{2,1,0:T(8,128)(2,1)} custom-call(bf16[128,512]{1,0:T(8,128)(2,1)} %src_ref.1), custom_call_target="tpu_custom_call" | custom-call | bytes 8388608 | tf_op jit(solution)/shard_map/pallas_call | solution.py:397
  106.5 0.0 copy-done.3
  106.5 7.1 %shard_map.112.src_ref = bf16[16,128,512]{2,1,0:T(8,128)(2,1)S(1)} custom-call(s32[12]{0:T(128)S(1)} %get-tuple-element.16.src_ids.tgt_ids, s32[12]{0:T(128)S(1)} %get-tuple-element.15.tgt_ids.src_ids, s32[1]{0:T(128)} %bitcast.22.count_ref, bf16[12,128,128]{2,1,0:T(8,128)(2,1)S(1)} %bitcast.24, bf16[32,128,512]{2,1,0:T(8,128)(2,1)} %shard_map.111.src_ref), custom_call_target="tpu_custom_call" | custom-call | flops 201326592 | bytes 4063232 | tf_op jit(solution)/shard_map/pallas_call | solution.py:461
  113.7 0.0 copy-start.1
  113.7 1.3 copy-done.1
  115.0 58.4 %shard_map.113 = bf16[16,128,512]{2,1,0:T(8,128)(2,1)} custom-call(bf16[16,128,512]{2,1,0:T(8,128)(2,1)} %copy-done.1), custom_call_target="tpu_custom_call" | custom-call | bytes 4194304 | tf_op jit(solution)/shard_map/pallas_call | solution.py:116
  173.4 0.0 copy-start.4
  173.4 0.0 copy-start.5
  173.4 1.9 reduce_sum.42
  175.4 0.1 copy.17
  175.5 0.0 copy-done
  175.5 0.0 copy-done.4
  175.5 0.0 copy-done.5
  175.5 1.0 fusion.4
  176.5 1.0 convolution_convert_fusion.src_ref
  177.5 0.2 concatenate.8
  177.7 0.3 fusion
  178.0 1.2 maximum_maximum_fusion.pieces_ref
  179.2 56.6 %shard_map.114 = (bf16[16,128,512]{2,1,0:T(8,128)(2,1)}, f32[32,16,640]{2,1,0:T(8,128)}) custom-call(bf16[128,512]{1,0:T(8,128)(2,1)} %convolution_convert_fusion.src_ref, f32[32,16,640]{2,1,0:T(8,128)} %maximum_maximum_fusion.pieces_ref), custom_call_target="tpu_custom_call" | custom-call | bytes 6815744 | tf_op jit(solution)/shard_map/pallas_call | solution.py:216
  235.8 1.4 reduce_sum.44
  237.2 0.6 reshape.30.part_ref
  237.8 0.0 copy-start.2
  237.8 1.6 copy-done.2
  239.4 4.8 %shard_map.115.src_ref = bf16[32,128,512]{2,1,0:T(8,128)(2,1)} custom-call(s32[12]{0:T(128)S(1)} %get-tuple-element.15.tgt_ids.src_ids, s32[12]{0:T(128)S(1)} %get-tuple-element.16.src_ids.tgt_ids, s32[1]{0:T(128)} %bitcast.23.count_ref, bf16[12,128,128]{2,1,0:T(8,128)(2,1)S(1)} %bitcast.25, bf16[16,128,512]{2,1,0:T(8,128)(2,1)S(1)} %copy-done.2), custom_call_target="tpu_custom_call" | custom-call | flops 201326592 | bytes 6160384 | tf_op jit(solution)/shard_map/pallas_call | solution.py:461
  244.2 113.1 %shard_map.116 = (bf16[32,128,512]{2,1,0:T(8,128)(2,1)}, f32[32,1,640]{2,1,0:T(1,128)}, f32[16,32,1,640]{3,2,1,0:T(1,128)}) custom-call(bf16[32,128,512]{2,1,0:T(8,128)(2,1)} %shard_map.115.src_ref, f32[16,1,640]{2,1,0:T(1,128)} %reshape.30.part_ref), custom_call_target="tpu_custom_call" | custom-call | bytes 11010048 | tf_op jit(solution)/shard_map/pallas_call | solution.py:367
  357.4 2.1 copy.21
  359.4 0.7 slice_reduce_fusion
  360.2 1.1 slice.8
  361.3 3.5 reduce_sum.45
  (1 shorter events, 0.0 us)
Async XLA Ops:
  0.6 174.9 %copy-start = (bf16[512,512]{1,0:T(8,128)(2,1)S(1)}, bf16[512,512]{1,0:T(8,128)(2,1)}, u32[]{:S(2)}) copy-start(bf16[512,512]{1,0:T(8,128)(2,1)} %param.13) | copy-start | bytes 1572868
  2.1 104.4 %copy-start.3 = (bf16[1,1,12,128,128]{4,3,2,1,0:T(8,128)(2,1)S(1)}, bf16[1,1,12,128,128]{4,3,2,1,0:T(8,128)(2,1)}, u32[]{:S(2)}) copy-start(bf16[1,1,12,128,128]{4,3,2,1,0:T(8,128)(2,1)} %param.9) | copy-start | bytes 1179652
  113.7 1.4 copy-start.1
  173.4 2.1 copy-start.4
  173.4 2.1 copy-start.5
  237.8 1.6 copy-start.2

commit v13 on v11

--- a/solution.py
+++ b/solution.py
@@ -297,6 +297,7 @@
         return carry
 
     lax.fori_loop(1, m, send_part, 0)
+    lax.fori_loop(0, n // 4, lambda i, c: send_main(2 + 4 * i, c), 0)
 
     def finish_part(step, carry):
         part_copy(step, lax.rem(there + step, m)).wait_send()
@@ -314,7 +315,8 @@
         return carry
 
     lax.fori_loop(1, n, send_row, 0)
-    lax.fori_loop(1, n, send_main, 0)
+    lax.fori_loop(0, n // 2, lambda i, c: send_main(1 + 2 * i, c), 0)
+    lax.fori_loop(1, n // 4, lambda i, c: send_main(4 * i, c), 0)
 
     def finish_row(step, carry):
         row_copy(step, lax.rem(me + step, n), me).wait_send()

time: 379 us -> 374 us (0.987)
  Pallas kernels: 354 us -> 348 us
where the time goes in v13:
time: 374 us; the launch traced here: 369 us
  Pallas kernels  348 us (93%)
  other arithmetic  8.68 us (2%)
  local copies, waits for them, and re-layouts  7.92 us (2%)
    pallas_call x1, Pallas kernels, back_exchange(): pl.pallas_call(functools.partial(_back_kernel, n, m), out_shape=shapes, i...  118 us
    pallas_call x1, Pallas kernels, exchange(): pl.pallas_call(functools.partial(_exchange_kernel, axis, other, n, broadc...  104 us
    pallas_call x1, Pallas kernels, exchange_steps(): pl.pallas_call(functools.partial(_steps_kernel, axis, other, n, first, st...  58.6 us
    pallas_call x1, Pallas kernels, gather_and_exchange(): pl.pallas_call(functools.partial(_gather_steps_kernel, axis, other, n, m)...  55.3 us
    pallas_call x2, Pallas kernels, slot_product(): pl.pallas_call(functools.partial(_slot_kernel, backward, slots), out_shap...  11.9 us

profile of v13, /device:TPU:7, one launch (start us, length us, event | category | flops | bytes accessed | tf_op | source)
XLA Modules:
  0.0 368.5 jit_solution(8331089245198022760)
XLA Ops:
  0.6 0.0 copy-start
  1.4 0.7 clamp_bitcast_fusion
  2.0 0.1 pad.2.clone
  2.1 0.0 copy-start.3
  2.1 104.4 %shard_map.111.src_ref = bf16[32,128,512]{2,1,0:T(8,128)(2,1)} custom-call(bf16[128,512]{1,0:T(8,128)(2,1)} %src_ref.1), custom_call_target="tpu_custom_call" | custom-call | bytes 8388608 | tf_op jit(solution)/shard_map/pallas_call | solution.py:398
  106.5 0.0 copy-done.3
  106.5 7.1 %shard_map.112.src_ref = bf16[16,128,512]{2,1,0:T(8,128)(2,1)S(1)} custom-call(s32[12]{0:T(128)S(1)} %get-tuple-element.16.src_ids.tgt_ids, s32[12]{0:T(128)S(1)} %get-tuple-element.15.tgt_ids.src_ids, s32[1]{0:T(128)} %bitcast.22.count_ref, bf16[12,128,128]{2,1,0:T(8,128)(2,1)S(1)} %bitcast.24, bf16[32,128,512]{2,1,0:T(8,128)(2,1)} %shard_map.111.src_ref), custom_call_target="tpu_custom_call" | custom-call | flops 201326592 | bytes 4063232 | tf_op jit(solution)/shard_map/pallas_call | solution.py:462
  113.6 0.0 copy-start.1
  113.7 1.3 copy-done.1
  115.0 58.6 %shard_map.113 = bf16[16,128,512]{2,1,0:T(8,128)(2,1)} custom-call(bf16[16,128,512]{2,1,0:T(8,128)(2,1)} %copy-done.1), custom_call_target="tpu_custom_call" | custom-call | bytes 4194304 | tf_op jit(solution)/shard_map/pallas_call | solution.py:116
  173.6 0.0 copy-start.4
  173.7 0.0 copy-start.5
  173.7 1.9 reduce_sum.42
  175.6 0.1 copy.17
  175.7 0.0 copy-done
  175.7 0.0 copy-done.4
  175.7 0.0 copy-done.5
  175.7 1.0 fusion.4
  176.7 1.0 convolution_convert_fusion.src_ref
  177.7 0.2 concatenate.8
  177.9 0.3 fusion
  178.2 1.2 maximum_maximum_fusion.pieces_ref
  179.4 55.3 %shard_map.114 = (bf16[16,128,512]{2,1,0:T(8,128)(2,1)}, f32[32,16,640]{2,1,0:T(8,128)}) custom-call(bf16[128,512]{1,0:T(8,128)(2,1)} %convolution_convert_fusion.src_ref, f32[32,16,640]{2,1,0:T(8,128)} %maximum_maximum_fusion.pieces_ref), custom_call_target="tpu_custom_call" | custom-call | bytes 6815744 | tf_op jit(solution)/shard_map/pallas_call | solution.py:216
  234.7 1.4 reduce_sum.44
  236.1 0.6 reshape.30.part_ref
  236.8 0.0 copy-start.2
  236.8 1.6 copy-done.2
  238.4 4.8 %shard_map.115.src_ref = bf16[32,128,512]{2,1,0:T(8,128)(2,1)} custom-call(s32[12]{0:T(128)S(1)} %get-tuple-element.15.tgt_ids.src_ids, s32[12]{0:T(128)S(1)} %get-tuple-element.16.src_ids.tgt_ids, s32[1]{0:T(128)} %bitcast.23.count_ref, bf16[12,128,128]{2,1,0:T(8,128)(2,1)S(1)} %bitcast.25, bf16[16,128,512]{2,1,0:T(8,128)(2,1)S(1)} %copy-done.2), custom_call_target="tpu_custom_call" | custom-call | flops 201326592 | bytes 6160384 | tf_op jit(solution)/shard_map/pallas_call | solution.py:462
  243.2 118.0 %shard_map.116 = (bf16[32,128,512]{2,1,0:T(8,128)(2,1)}, f32[32,1,640]{2,1,0:T(1,128)}, f32[16,32,1,640]{3,2,1,0:T(1,128)}) custom-call(bf16[32,128,512]{2,1,0:T(8,128)(2,1)} %shard_map.115.src_ref, f32[16,1,640]{2,1,0:T(1,128)} %reshape.30.part_ref), custom_call_target="tpu_custom_call" | custom-call | bytes 11010048 | tf_op jit(solution)/shard_map/pallas_call | solution.py:368
  361.1 2.1 copy.21
  363.2 0.7 slice_reduce_fusion
  364.0 1.1 slice.8
  365.1 3.5 reduce_sum.45
  (1 shorter events, 0.0 us)
Async XLA Ops:
  0.6 175.1 %copy-start = (bf16[512,512]{1,0:T(8,128)(2,1)S(1)}, bf16[512,512]{1,0:T(8,128)(2,1)}, u32[]{:S(2)}) copy-start(bf16[512,512]{1,0:T(8,128)(2,1)} %param.13) | copy-start | bytes 1572868
  2.1 104.4 %copy-start.3 = (bf16[1,1,12,128,128]{4,3,2,1,0:T(8,128)(2,1)S(1)}, bf16[1,1,12,128,128]{4,3,2,1,0:T(8,128)(2,1)}, u32[]{:S(2)}) copy-start(bf16[1,1,12,128,128]{4,3,2,1,0:T(8,128)(2,1)} %param.9) | copy-start | bytes 1179652
  113.6 1.4 copy-start.1
  173.6 2.1 copy-start.4
  173.7 2.1 copy-start.5
  236.8 1.6 copy-start.2

commit v14 on v13

--- a/solution.py
+++ b/solution.py
@@ -297,6 +297,7 @@
         return carry
 
     lax.fori_loop(1, m, send_part, 0)
+    lax.fori_loop(0, n // 2, lambda i, c: send_main(1 + 2 * i, c), 0)
     lax.fori_loop(0, n // 4, lambda i, c: send_main(2 + 4 * i, c), 0)
 
     def finish_part(step, carry):
@@ -315,7 +316,6 @@
         return carry
 
     lax.fori_loop(1, n, send_row, 0)
-    lax.fori_loop(0, n // 2, lambda i, c: send_main(1 + 2 * i, c), 0)
     lax.fori_loop(1, n // 4, lambda i, c: send_main(4 * i, c), 0)
 
     def finish_row(step, carry):

time: 374 us -> 388 us (1.037); the launches traced: 369 us -> 388 us
  Pallas kernels: 348 us -> 367 us
    pallas_call x1, Pallas kernels: 118 us -> 137 us  [back_exchange(): pl.pallas_call(functools.partial(_back_kernel, n, m), out_shape=shapes, i...]
where the time goes in v14:
time: 388 us
  Pallas kernels  367 us (95%)
  other arithmetic  8.68 us (2%)
  local copies, waits for them, and re-layouts  7.92 us (2%)
    pallas_call x1, Pallas kernels, back_exchange(): pl.pallas_call(functools.partial(_back_kernel, n, m), out_shape=shapes, i...  137 us
    pallas_call x1, Pallas kernels, exchange(): pl.pallas_call(functools.partial(_exchange_kernel, axis, other, n, broadc...  104 us
    pallas_call x1, Pallas kernels, exchange_steps(): pl.pallas_call(functools.partial(_steps_kernel, axis, other, n, first, st...  58.9 us
    pallas_call x1, Pallas kernels, gather_and_exchange(): pl.pallas_call(functools.partial(_gather_steps_kernel, axis, other, n, m)...  55.8 us
    pallas_call x2, Pallas kernels, slot_product(): pl.pallas_call(functools.partial(_slot_kernel, backward, slots), out_shap...  11.4 us

profile of v14, /device:TPU:7, one launch (start us, length us, event | category | flops | bytes accessed | tf_op | source)
XLA Modules:
  0.0 387.6 jit_solution(13857868770904886375)
XLA Ops:
  0.6 0.0 copy-start
  1.4 0.7 clamp_bitcast_fusion
  2.0 0.1 pad.2.clone
  2.1 0.0 copy-start.3
  2.1 104.4 %shard_map.111.src_ref = bf16[32,128,512]{2,1,0:T(8,128)(2,1)} custom-call(bf16[128,512]{1,0:T(8,128)(2,1)} %src_ref.1), custom_call_target="tpu_custom_call" | custom-call | bytes 8388608 | tf_op jit(solution)/shard_map/pallas_call | solution.py:398
  106.5 0.0 copy-done.3
  106.5 7.0 %shard_map.112.src_ref = bf16[16,128,512]{2,1,0:T(8,128)(2,1)S(1)} custom-call(s32[12]{0:T(128)S(1)} %get-tuple-element.16.src_ids.tgt_ids, s32[12]{0:T(128)S(1)} %get-tuple-element.15.tgt_ids.src_ids, s32[1]{0:T(128)} %bitcast.22.count_ref, bf16[12,128,128]{2,1,0:T(8,128)(2,1)S(1)} %bitcast.24, bf16[32,128,512]{2,1,0:T(8,128)(2,1)} %shard_map.111.src_ref), custom_call_target="tpu_custom_call" | custom-call | flops 201326592 | bytes 4063232 | tf_op jit(solution)/shard_map/pallas_call | solution.py:462
  113.5 0.0 copy-start.1
  113.5 1.3 copy-done.1
  114.9 58.9 %shard_map.113 = bf16[16,128,512]{2,1,0:T(8,128)(2,1)} custom-call(bf16[16,128,512]{2,1,0:T(8,128)(2,1)} %copy-done.1), custom_call_target="tpu_custom_call" | custom-call | bytes 4194304 | tf_op jit(solution)/shard_map/pallas_call | solution.py:116
  173.7 0.0 copy-start.4
  173.7 0.0 copy-start.5
  173.8 1.9 reduce_sum.42
  175.7 0.1 copy.17
  175.8 0.0 copy-done
  175.8 0.0 copy-done.4
  175.8 0.0 copy-done.5
  175.8 1.0 fusion.4
  176.8 1.0 convolution_convert_fusion.src_ref
  177.8 0.2 concatenate.8
  178.0 0.3 fusion
  178.3 1.2 maximum_maximum_fusion.pieces_ref
  179.5 55.8 %shard_map.114 = (bf16[16,128,512]{2,1,0:T(8,128)(2,1)}, f32[32,16,640]{2,1,0:T(8,128)}) custom-call(bf16[128,512]{1,0:T(8,128)(2,1)} %convolution_convert_fusion.src_ref, f32[32,16,640]{2,1,0:T(8,128)} %maximum_maximum_fusion.pieces_ref), custom_call_target="tpu_custom_call" | custom-call | bytes 6815744 | tf_op jit(solution)/shard_map/pallas_call | solution.py:216
  235.4 1.4 reduce_sum.44
  236.8 0.6 reshape.30.part_ref
  237.4 0.0 copy-start.2
  237.4 1.6 copy-done.2
  239.0 4.4 %shard_map.115.src_ref = bf16[32,128,512]{2,1,0:T(8,128)(2,1)} custom-call(s32[12]{0:T(128)S(1)} %get-tuple-element.15.tgt_ids.src_ids, s32[12]{0:T(128)S(1)} %get-tuple-element.16.src_ids.tgt_ids, s32[1]{0:T(128)} %bitcast.23.count_ref, bf16[12,128,128]{2,1,0:T(8,128)(2,1)S(1)} %bitcast.25, bf16[16,128,512]{2,1,0:T(8,128)(2,1)S(1)} %copy-done.2), custom_call_target="tpu_custom_call" | custom-call | flops 201326592 | bytes 6160384 | tf_op jit(solution)/shard_map/pallas_call | solution.py:462
  243.4 136.8 %shard_map.116 = (bf16[32,128,512]{2,1,0:T(8,128)(2,1)}, f32[32,1,640]{2,1,0:T(1,128)}, f32[16,32,1,640]{3,2,1,0:T(1,128)}) custom-call(bf16[32,128,512]{2,1,0:T(8,128)(2,1)} %shard_map.115.src_ref, f32[16,1,640]{2,1,0:T(1,128)} %reshape.30.part_ref), custom_call_target="tpu_custom_call" | custom-call | bytes 11010048 | tf_op jit(solution)/shard_map/pallas_call | solution.py:368
  380.2 2.1 copy.21
  382.3 0.7 slice_reduce_fusion
  383.1 1.1 slice.8
  384.2 3.5 reduce_sum.45
  (1 shorter events, 0.0 us)
Async XLA Ops:
  0.6 175.2 %copy-start = (bf16[512,512]{1,0:T(8,128)(2,1)S(1)}, bf16[512,512]{1,0:T(8,128)(2,1)}, u32[]{:S(2)}) copy-start(bf16[512,512]{1,0:T(8,128)(2,1)} %param.13) | copy-start | bytes 1572868
  2.1 104.4 %copy-start.3 = (bf16[1,1,12,128,128]{4,3,2,1,0:T(8,128)(2,1)S(1)}, bf16[1,1,12,128,128]{4,3,2,1,0:T(8,128)(2,1)}, u32[]{:S(2)}) copy-start(bf16[1,1,12,128,128]{4,3,2,1,0:T(8,128)(2,1)} %param.9) | copy-start | bytes 1179652
  113.5 1.4 copy-start.1
  173.7 2.1 copy-start.4
  173.7 2.1 copy-start.5
  237.4 1.6 copy-start.2
